TPU v7x, 32 devices: a whole 2x2x4 slice. The times are simulated.
32 devices in a mesh: expert: 4 (over y, x), dp: 8 (over z, core).
Axes of the slice: x: 2, y: 2, z: 4, core: 2. Of those that a mesh axis runs over, the one named last changes fastest.
Arguments:
- tokens: bfloat16 [1024, 5120], P('dp', 'expert'), may hold values from -6 to 6
- routes: int32 [1024, 2], P('dp'), may hold values from 0 to 7, all different within a row; in each aligned block of 128 rows (0 to 127, 128 to 255, ...) at most 48 rows name the same one
- combine: bfloat16 [1024, 2], P('dp'), may hold values from 0.099609375 to 1
- cotangent: bfloat16 [1024, 5120], P('dp', 'expert'), may hold values from -1.5 to 1.5
- w_gate: bfloat16 [8, 5120, 768], P('dp', 'expert'), may hold values from -0.078125 to 0.078125
- w_up: bfloat16 [8, 5120, 768], P('dp', 'expert'), may hold values from -0.078125 to 0.078125
- w_down: bfloat16 [8, 768, 5120], P('dp', None, 'expert'), may hold values from -0.21875 to 0.21875
Outputs:
- token_grad: bfloat16 [1024, 5120], P('dp', 'expert')
- combine_grad: float32 [1024, 2], P('dp')
- grad_gate: bfloat16 [8, 5120, 768], P('dp', 'expert')
- grad_up: bfloat16 [8, 5120, 768], P('dp', 'expert')
- grad_down: bfloat16 [8, 768, 5120], P('dp', None, 'expert')
Inputs may be any that keep to these rules, and one draw needn't show every extreme that they name: `routes`: each token names 2 different experts. The tokens of one group name any one expert at most 48 times, a bound that some block reaches.
All inputs are finite; a program needn't handle non-finite values.
Results may differ from a plain program's by a relative error of at most 0.018.
Values may be sent and summed in bfloat16 or wider, within the bound.
No kernel may reach another device: no remote copies, remote signals or barrier semaphores. Data moves between devices by JAX's collectives and lax.ppermute only.
A program may use at most 64 MiB of HBM per device.

v0:
```python
import jax
import jax.numpy as jnp
from jax import lax
from jax.sharding import PartitionSpec as P


def contract_last(matrix_a, matrix_b):
    return lax.dot_general(
        matrix_a, matrix_b, (((1,), (1,)), ((), ())), preferred_element_type=jnp.float32
    )


def contract_first(matrix_a, matrix_b):
    return lax.dot_general(
        matrix_a, matrix_b, (((0,), (0,)), ((), ())), preferred_element_type=jnp.float32
    )


def swiglu_grads(pre_gate, pre_up, back_hidden, weights):
    sigmas = jax.nn.sigmoid(pre_gate)
    active = pre_gate * sigmas
    hidden = (active * pre_up).astype(jnp.bfloat16)
    scaled = weights[:, None] * back_hidden
    grad_gate_pre = (scaled * pre_up * sigmas * (1.0 + pre_gate * (1.0 - sigmas))).astype(
        jnp.bfloat16
    )
    grad_up_pre = (scaled * active).astype(jnp.bfloat16)
    return (hidden, grad_gate_pre, grad_up_pre)


def body(tokens, routes, combine, cotangent, w_gate, w_up, w_down):
    tok_rows, slice_width = tokens.shape
    top_routes = routes.shape[1]
    experts = lax.axis_size("dp")
    capacity = 3 * tok_rows * top_routes // (2 * experts)
    route_count = tok_rows * top_routes
    slot_total = experts * capacity
    route_flat = routes.reshape(route_count)
    onehot = (route_flat[:, None] == jnp.arange(experts, dtype=jnp.int32)[None, :]).astype(
        jnp.int32
    )
    slot_rank = jnp.sum((jnp.cumsum(onehot, axis=0) - onehot) * onehot, axis=1)
    places = route_flat * capacity + slot_rank
    source = jnp.full((slot_total,), route_count, jnp.int32)
    source = source.at[places].set(jnp.arange(route_count, dtype=jnp.int32))
    blank_row = jnp.zeros((1, slice_width), jnp.bfloat16)
    token_send = jnp.concatenate([tokens, blank_row], axis=0)[source // top_routes]
    cot_send = jnp.concatenate([cotangent, blank_row], axis=0)[source // top_routes]
    comb_send = jnp.concatenate(
        [combine.reshape(route_count), jnp.zeros((1,), jnp.bfloat16)], axis=0
    )[source]
    arrived_tok, arrived_cot, arrived_comb = (
        lax.all_to_all(
            token_send.reshape(experts, capacity, slice_width),
            "dp",
            split_axis=0,
            concat_axis=0,
            tiled=True,
        ),
        lax.all_to_all(
            cot_send.reshape(experts, capacity, slice_width),
            "dp",
            split_axis=0,
            concat_axis=0,
            tiled=True,
        ),
        lax.all_to_all(
            comb_send.reshape(experts, capacity), "dp", split_axis=0, concat_axis=0, tiled=True
        ),
    )
    token_slots = arrived_tok.reshape(slot_total, slice_width)
    cot_slots = arrived_cot.reshape(slot_total, slice_width)
    comb_slots = arrived_comb.reshape(slot_total).astype(jnp.float32)
    gate_mat = w_gate[0]
    up_mat = w_up[0]
    down_mat = w_down[0]
    partials = jnp.stack(
        [
            jnp.dot(token_slots, gate_mat, preferred_element_type=jnp.float32),
            jnp.dot(token_slots, up_mat, preferred_element_type=jnp.float32),
            contract_last(cot_slots, down_mat),
        ],
        axis=1,
    )
    summed = lax.psum_scatter(
        partials.astype(jnp.bfloat16), "expert", scatter_dimension=2, tiled=True
    ).astype(jnp.float32)
    hidden_part, gate_part, up_part = swiglu_grads(
        summed[:, 0], summed[:, 1], summed[:, 2], comb_slots
    )
    slot_comb = jnp.sum(hidden_part.astype(jnp.float32) * summed[:, 2], axis=1)
    joined = lax.all_gather(
        jnp.stack([hidden_part, gate_part, up_part], axis=1), "expert", axis=2, tiled=True
    )
    hidden = joined[:, 0]
    grad_gate_pre = joined[:, 1]
    grad_up_pre = joined[:, 2]
    slot_dx = contract_last(grad_gate_pre, gate_mat) + contract_last(grad_up_pre, up_mat)
    scaled_dy = (comb_slots[:, None] * cot_slots.astype(jnp.float32)).astype(jnp.bfloat16)
    grad_gate = contract_first(token_slots, grad_gate_pre).astype(jnp.bfloat16)[None]
    grad_up = contract_first(token_slots, grad_up_pre).astype(jnp.bfloat16)[None]
    grad_down = contract_first(hidden, scaled_dy).astype(jnp.bfloat16)[None]
    back_dx, back_comb = (
        lax.all_to_all(
            slot_dx.reshape(experts, capacity, slice_width).astype(jnp.bfloat16),
            "dp",
            split_axis=0,
            concat_axis=0,
            tiled=True,
        ).astype(jnp.float32),
        lax.all_to_all(
            slot_comb.reshape(experts, capacity).astype(jnp.bfloat16),
            "dp",
            split_axis=0,
            concat_axis=0,
            tiled=True,
        ).astype(jnp.float32),
    )
    route_dx = back_dx.reshape(slot_total, slice_width)[places].reshape(
        tok_rows, top_routes, slice_width
    )
    token_grad = jnp.sum(route_dx, axis=1).astype(jnp.bfloat16)
    comb_part = back_comb.reshape(slot_total)[places].reshape(tok_rows, top_routes)
    combine_grad = lax.psum(comb_part, "expert")
    return (token_grad, combine_grad, grad_gate, grad_up, grad_down)


def solution(mesh):
    in_specs = (
        P("dp", "expert"),
        P("dp", None),
        P("dp", None),
        P("dp", "expert"),
        P("dp", "expert", None),
        P("dp", "expert", None),
        P("dp", None, "expert"),
    )
    out_specs = (
        P("dp", "expert"),
        P("dp", None),
        P("dp", "expert", None),
        P("dp", "expert", None),
        P("dp", None, "expert"),
    )
    return jax.shard_map(body, mesh=mesh, in_specs=in_specs, out_specs=out_specs, check_vma=False)
```

profile of v0, /device:TPU:0, one launch (start us, length us, event | category | flops | bytes accessed | tf_op | source)
XLA Modules:
  0.0 218.3 jit_solution(15409593457587932573)
XLA Ops:
  12.7 2.8 %gather_fusion = bf16[384,1280]{1,0:T(8,128)(2,1)} fusion(bf16[129,1280]{1,0:T(8,128)(2,1)S(1)} %concatenate.9, s32[1024]{0:T(1024)S(1)} %get-tuple-element.26), kind=kCustom, calls=%fused_computation | custom fusion | bytes 1967616 | tf_op jit(solution)/shard_map/gather | solution.py:47
  15.5 6.3 %all-to-all-start = ((bf16[8,48,1280]{2,1,0:T(8,128)(2,1)}), bf16[8,48,1280]{2,1,0:T(8,128)(2,1)S(1)}, u32[]{:S(2)}, u32[]{:S(2)}) async-start(bf16[8,48,1280]{2,1,0:T(8,128)(2,1)} %bitcast.4), calls=%async_computation | async-start | bytes 1966080 | tf_op jit(solution)/shard_map/all_to_all | solution.py:53
  22.8 2.8 %gather_fusion.1 = bf16[384,1280]{1,0:T(8,128)(2,1)} fusion(bf16[129,1280]{1,0:T(8,128)(2,1)S(1)} %concatenate.10, s32[1024]{0:T(1024)S(1)} %get-tuple-element.26), kind=kCustom, calls=%fused_computation.1 | custom fusion | bytes 1967616 | tf_op jit(solution)/shard_map/gather | solution.py:48
  25.6 21.4 %all-to-all-done = bf16[8,48,1280]{2,1,0:T(8,128)(2,1)S(1)} async-done(((bf16[8,48,1280]{2,1,0:T(8,128)(2,1)}), bf16[8,48,1280]{2,1,0:T(8,128)(2,1)S(1)}, u32[]{:S(2)}, u32[]{:S(2)}) %all-to-all-start) | async-done | bytes 983072 | tf_op jit(solution)/shard_map/all_to_all | solution.py:53
  48.0 3.6 %all-to-all-start.1 = ((bf16[8,48,1280]{2,1,0:T(8,128)(2,1)}), bf16[8,48,1280]{2,1,0:T(8,128)(2,1)S(1)}, u32[]{:S(2)}, u32[]{:S(2)}) async-start(bf16[8,48,1280]{2,1,0:T(8,128)(2,1)} %bitcast.107), calls=%async_computation.1 | async-start | bytes 1966080 | tf_op jit(solution)/shard_map/all_to_all | solution.py:60
  51.6 2.9 %fusion.25 = bf16[384,1,768]{2,0,1:T(8,128)(2,1)S(1)} fusion(bf16[384,1280]{1,0:T(8,128)(2,1)} %bitcast.109, bf16[1,1280,768]{2,1,0:T(8,128)(2,1)} %param.12), kind=kOutput, calls=%fused_computation.29 | convolution fusion | flops 755269632 | bytes 3538944 | tf_op jit(solution)/shard_map/dot_general | solution.py:80
  56.2 20.4 %all-to-all-done.1 = bf16[8,48,1280]{2,1,0:T(8,128)(2,1)S(1)} async-done(((bf16[8,48,1280]{2,1,0:T(8,128)(2,1)}), bf16[8,48,1280]{2,1,0:T(8,128)(2,1)S(1)}, u32[]{:S(2)}, u32[]{:S(2)}) %all-to-all-start.1) | async-done | bytes 983072 | tf_op jit(solution)/shard_map/all_to_all | solution.py:60
  76.6 2.9 %fusion.22 = bf16[384,1,768]{2,0,1:T(8,128)(2,1)S(1)} fusion(bf16[384,1280]{1,0:T(8,128)(2,1)S(1)} %bitcast.106, bf16[1,768,1280]{2,1,0:T(8,128)(2,1)} %param.13), kind=kOutput, calls=%fused_computation.28 | convolution fusion | flops 755269632 | bytes 3538944 | tf_op jit(solution)/shard_map/dot_general | solution.py:8
  81.0 5.2 %copy.32 = bf16[384,3,768]{0,1,2:T(4,128)(2,1)} copy(bf16[384,3,768]{2,0,1:T(8,128)(2,1)} %pad_maximum_fusion) | data formatting | bytes 3538944
  86.2 3.2 %copy.34 = bf16[96,8,3,384]{3,1,2,0:T(8,128)(2,1)} copy(bf16[96,8,3,384]{3,2,1,0:T(4,128)(2,1)} %bitcast.104) | data formatting | bytes 3538944
  89.7 2.8 %gather_fusion.2 = bf16[384]{0:T(512)(128)(2,1)S(1)} fusion(bf16[257]{0:T(512)(128)(2,1)S(1)} %pad_maximum_fusion.2, s32[1024]{0:T(1024)S(1)} %get-tuple-element.25), kind=kCustom, calls=%fused_computation.2 | custom fusion | bytes 3072 | tf_op jit(solution)/shard_map/gather | solution.py:49
  92.6 7.9 %all_to_all.31 = bf16[8,1,48]{2,1,0:T(2,128)(2,1)S(1)} all-to-all(bf16[8,1,48]{2,1,0:T(2,128)(2,1)S(1)} %all_to_all.25), channel_id=1, replica_groups=mesh['expert'=4,'dp'=8] {'dp'}, dimensions={0} | all-to-all | bytes 1536 | tf_op jit(solution)/shard_map/all_to_all | solution.py:67
  100.6 20.2 %reduce-scatter.4.cloned.1.call-done = bf16[192,1152]{1,0:T(8,128)(2,1)} async-done(((bf16[768,1152]{1,0:T(8,128)(2,1)}), bf16[192,1152]{1,0:T(8,128)(2,1)}) %reduce-scatter.4.cloned.1.call-update) | async-done | bytes 442384
  129.0 4.6 %all-to-all-start.4 = ((bf16[8,1,48]{2,1,0:T(2,128)(2,1)}), bf16[8,1,48]{2,1,0:T(2,128)(2,1)S(1)}, u32[]{:S(2)}, u32[]{:S(2)}) async-start(bf16[8,1,48]{2,1,0:T(2,128)(2,1)} %convert_element_type.121), calls=%async_computation.4 | async-start | bytes 8192 | tf_op jit(solution)/shard_map/all_to_all | solution.py:111
  133.6 27.2 %all-gather.2.cloned.1.call-done = bf16[384,3,768]{0,2,1:T(8,128)(2,1)} async-done(((bf16[384,3,192]{0,2,1:T(8,128)(2,1)}), bf16[384,3,768]{0,2,1:T(8,128)(2,1)}) %all-gather.2.cloned.1.call-update) | async-done | bytes 1769488 | tf_op jit(solution)/shard_map/all_gather | solution.py:92
  163.0 3.1 %fusion.3 = bf16[384,1280]{1,0:T(8,128)(2,1)} fusion(f32[384,1280]{1,0:T(8,128)S(1)} %fusion.9, bf16[1,1280,768]{2,1,0:T(8,128)(2,1)S(1)} %copy-done.9, bf16[384,3,768]{0,2,1:T(8,128)(2,1)} %all-gather.2.cloned.1.call-done), kind=kOutput, calls=%fused_computation.13 | convolution fusion | flops 755957760 | bytes 5505024 | tf_op jit(solution)/shard_map/dot_general | solution.py:8
  166.1 4.7 %all-to-all-start.3 = ((bf16[8,48,1280]{2,1,0:T(8,128)(2,1)}), bf16[8,48,1280]{2,1,0:T(8,128)(2,1)}, u32[]{:S(2)}, u32[]{:S(2)}) async-start(bf16[8,48,1280]{2,1,0:T(8,128)(2,1)} %bitcast.113), calls=%async_computation.3 | async-start | bytes 1966080 | tf_op jit(solution)/shard_map/all_to_all | solution.py:104
  174.2 16.2 %psum.7 = f32[128,2]{1,0:T(8,128)S(1)} all-reduce(f32[128,2]{1,0:T(8,128)S(1)} %reshape.146), channel_id=1, replica_groups=mesh['expert'=4,'dp'=8] {'expert'}, use_global_device_ids=true, to_apply=%region_7.8 | all-reduce | flops 256 | bytes 2048 | tf_op jit(solution)/shard_map/psum | solution.py:124
  191.0 4.0 %fusion = bf16[1,1280,768]{2,1,0:T(8,128)(2,1)} fusion(bf16[384,1280]{1,0:T(8,128)(2,1)} %bitcast.110, bf16[384,3,768]{0,2,1:T(8,128)(2,1)} %all-gather.2.cloned.1.call-done), kind=kOutput, calls=%fused_computation.10 | convolution fusion | flops 755957760 | bytes 3538944 | tf_op jit(solution)/shard_map/dot_general | solution.py:14
  195.0 2.5 %fusion.1 = bf16[1,1280,768]{2,1,0:T(8,128)(2,1)} fusion(bf16[384,1280]{1,0:T(8,128)(2,1)S(1)} %bitcast.112, bf16[384,3,768]{0,2,1:T(8,128)(2,1)S(1)} %copy-done.10), kind=kOutput, calls=%fused_computation.11 | convolution fusion | flops 755957760 | bytes 3538944 | tf_op jit(solution)/shard_map/dot_general | solution.py:14
  197.6 2.4 %fusion.2 = bf16[1,768,1280]{2,1,0:T(8,128)(2,1)} fusion(bf16[384,1280]{1,0:T(8,128)(2,1)S(1)} %bitcast.114, bf16[384,3,768]{0,2,1:T(8,128)(2,1)S(1)} %copy-done.10), kind=kOutput, calls=%fused_computation.12 | convolution fusion | flops 755957760 | bytes 3538944 | tf_op jit(solution)/shard_map/dot_general | solution.py:14
  200.0 2.6 %bitcast_convert_fusion = f32[384,1280]{1,0:T(8,128)} fusion(bf16[8,48,1280]{2,1,0:T(8,128)(2,1)} %all-to-all-done.3), kind=kLoop, calls=%fused_computation.31 | loop fusion | flops 491520 | bytes 2949120 | tf_op jit(solution)/shard_map/reshape | solution.py:119
  202.6 3.3 %gather_fusion.3 = f32[256,1280]{1,0:T(8,128)S(1)} fusion(f32[384,1280]{1,0:T(8,128)} %bitcast_convert_fusion, s32[1024]{0:T(1024)S(1)} %pad_clamp_fusion), kind=kCustom, calls=%fused_computation.3 | custom fusion | bytes 2622464 | tf_op jit(solution)/shard_map/gather | solution.py:119
  207.8 3.6 %reduce_sum.31 = bf16[128,1280]{1,0:T(8,128)(2,1)} reduce(f32[128,2,1280]{2,1,0:T(2,128)} %reshape.145, f32[]{:T(128)} %constant.40.clone.1), dimensions={1}, to_apply=%region_5.6 | reduce | flops 163840 | bytes 1638404 | tf_op jit(solution)/shard_map/reduce_sum | solution.py:122
  (73 shorter events, 27.3 us)
Async XLA Ops:
  7.2 47.3 %copy-start = (bf16[1,1280,768]{2,1,0:T(8,128)(2,1)S(1)}, bf16[1,1280,768]{2,1,0:T(8,128)(2,1)}, u32[]{:S(2)}) copy-start(bf16[1,1280,768]{2,1,0:T(8,128)(2,1)} %param.11) | copy-start | bytes 5898244
  15.5 31.5 %all-to-all-start = ((bf16[8,48,1280]{2,1,0:T(8,128)(2,1)}), bf16[8,48,1280]{2,1,0:T(8,128)(2,1)S(1)}, u32[]{:S(2)}, u32[]{:S(2)}) async-start(bf16[8,48,1280]{2,1,0:T(8,128)(2,1)} %bitcast.4), calls=%async_computation | async-start | bytes 1966080 | tf_op jit(solution)/shard_map/all_to_all | solution.py:53
  47.0 0.9 copy-start.3
  48.0 28.7 %all-to-all-start.1 = ((bf16[8,48,1280]{2,1,0:T(8,128)(2,1)}), bf16[8,48,1280]{2,1,0:T(8,128)(2,1)S(1)}, u32[]{:S(2)}, u32[]{:S(2)}) async-start(bf16[8,48,1280]{2,1,0:T(8,128)(2,1)} %bitcast.107), calls=%async_computation.1 | async-start | bytes 1966080 | tf_op jit(solution)/shard_map/all_to_all | solution.py:60
  51.5 69.4 %reduce-scatter.4.cloned.1.call-start = ((), (), s32[]{:S(2)}) async-start(), calls=%async_computation.7 | async-start | bytes 2211840
  51.6 2.9 %copy-start.4 = (bf16[8,48,1280]{2,1,0:T(8,128)(2,1)S(1)}, bf16[8,48,1280]{2,1,0:T(8,128)(2,1)}, u32[]{:S(2)}) copy-start(bf16[8,48,1280]{2,1,0:T(8,128)(2,1)} %copy-done.3) | copy-start | bytes 2949124
  76.6 2.9 %copy-start.1 = (bf16[8,48,1280]{2,1,0:T(8,128)(2,1)}, bf16[8,48,1280]{2,1,0:T(8,128)(2,1)S(1)}, u32[]{:S(2)}) copy-start(bf16[8,48,1280]{2,1,0:T(8,128)(2,1)S(1)} %all-to-all-done.1) | copy-start | bytes 2949124
  76.6 2.9 %copy-start.7 = (bf16[384,1,768]{2,0,1:T(8,128)(2,1)S(1)}, bf16[384,1,768]{2,0,1:T(8,128)(2,1)}, u32[]{:S(2)}) copy-start(bf16[384,1,768]{2,0,1:T(8,128)(2,1)} %fusion.28) | copy-start | bytes 1769476
  86.1 3.3 %copy-start.8 = (bf16[128,2]{0,1:T(2,128)(2,1)S(1)}, bf16[128,2]{0,1:T(2,128)(2,1)}, u32[]{:S(2)}) copy-start(bf16[128,2]{0,1:T(2,128)(2,1)} %param.9) | copy-start | bytes 1540
  89.4 71.4 %all-gather.2.cloned.1.call-start = ((), (), s32[]{:S(2)}) async-start(), calls=%async_computation.6 | async-start | bytes 2211840 | tf_op jit(solution)/shard_map/all_gather | solution.py:92
  129.0 37.1 %all-to-all-start.4 = ((bf16[8,1,48]{2,1,0:T(2,128)(2,1)}), bf16[8,1,48]{2,1,0:T(2,128)(2,1)S(1)}, u32[]{:S(2)}, u32[]{:S(2)}) async-start(bf16[8,1,48]{2,1,0:T(2,128)(2,1)} %convert_element_type.121), calls=%async_computation.4 | async-start | bytes 8192 | tf_op jit(solution)/shard_map/all_to_all | solution.py:111
  160.8 2.2 %copy-start.9 = (bf16[1,1280,768]{2,1,0:T(8,128)(2,1)S(1)}, bf16[1,1280,768]{2,1,0:T(8,128)(2,1)}, u32[]{:S(2)}) copy-start(bf16[1,1280,768]{2,1,0:T(8,128)(2,1)} %param.12) | copy-start | bytes 5898244
  166.1 4.8 %copy-start.2 = (bf16[8,48,1280]{2,1,0:T(8,128)(2,1)S(1)}, bf16[8,48,1280]{2,1,0:T(8,128)(2,1)}, u32[]{:S(2)}) copy-start(bf16[8,48,1280]{2,1,0:T(8,128)(2,1)} %copy-done.1) | copy-start | bytes 2949124
  166.1 33.9 %all-to-all-start.3 = ((bf16[8,48,1280]{2,1,0:T(8,128)(2,1)}), bf16[8,48,1280]{2,1,0:T(8,128)(2,1)}, u32[]{:S(2)}, u32[]{:S(2)}) async-start(bf16[8,48,1280]{2,1,0:T(8,128)(2,1)} %bitcast.113), calls=%async_computation.3 | async-start | bytes 1966080 | tf_op jit(solution)/shard_map/all_to_all | solution.py:104
  174.2 20.8 %copy-start.5 = (bf16[8,48,1280]{2,1,0:T(8,128)(2,1)S(1)}, bf16[8,48,1280]{2,1,0:T(8,128)(2,1)}, u32[]{:S(2)}) copy-start(bf16[8,48,1280]{2,1,0:T(8,128)(2,1)} %copy-done.3) | copy-start | bytes 2949124
  191.0 4.0 %copy-start.10 = (bf16[384,3,768]{0,2,1:T(8,128)(2,1)S(1)}, bf16[384,3,768]{0,2,1:T(8,128)(2,1)}, u32[]{:S(2)}) copy-start(bf16[384,3,768]{0,2,1:T(8,128)(2,1)} %all-gather.2.cloned.1.call-done) | copy-start | bytes 5308420
  195.0 2.5 %copy-start.6 = (bf16[8,48,1280]{2,1,0:T(8,128)(2,1)S(1)}, bf16[8,48,1280]{2,1,0:T(8,128)(2,1)}, u32[]{:S(2)}) copy-start(bf16[8,48,1280]{2,1,0:T(8,128)(2,1)} %multiply_convert_fusion) | copy-start | bytes 2949124
Sparse Core Ops, SparseCore 0:
  89.5 31.3 reduce-scatter.3
  128.2 32.5 all-gather.1
where the time goes:
time: 219 us; the launch traced here: 218 us
  waiting for transfers between devices  89.4 us (41%)
  local copies, waits for them, and re-layouts  36.5 us (17%)
  blocking collectives  24.1 us (11%)
  matrix products  21.7 us (10%)
  starting transfers between devices  19.3 us (9%)
  between operations  14.3 us (7%)
  other arithmetic  13 us (6%)
    all_gather x1, waiting for transfers between devices, body(): lax.all_gather(jnp.stack([hidden_part, gate_part, up_part], axis=1), 'exp...  27.2 us
    all_to_all x1, waiting for transfers between devices, body(): lax.all_to_all(token_send.reshape(experts, capacity, slice_width), 'dp',...  21.4 us
    all_to_all x1, waiting for transfers between devices, body(): lax.all_to_all(cot_send.reshape(experts, capacity, slice_width), 'dp', sp...  20.4 us
    unnamed x3, waiting for transfers between devices  20.3 us
    psum x1, blocking collectives, body(): combine_grad = lax.psum(comb_part, 'expert')  16.2 us
    unnamed x29, local copies, waits for them, and re-layouts  13.6 us
    dot_general x3, matrix products, contract_first(): lax.dot_general(matrix_a, matrix_b, (((0,), (0,)), ((), ())), preferred_e...  8.94 us
    dot_general x3, matrix products, contract_last(): lax.dot_general(matrix_a, matrix_b, (((1,), (1,)), ((), ())), preferred_e...  8.15 us
  transfers between devices with their start and end apart: 6, of which 4 were waited for; matrix products, arithmetic and copies ran while one was open for 14% of the time, Pallas kernels for 0%

commit v1 on v0

v1 whole, which is shorter than its diff:
```python
import functools
import jax
import jax.numpy as jnp
from jax import lax
from jax.experimental import pallas as pl
from jax.experimental.pallas import tpu as pltpu
from jax.sharding import PartitionSpec as P

F32 = jnp.float32
BF16 = jnp.bfloat16
LANES = 128


def contract_last(matrix_a, matrix_b):
    return lax.dot_general(
        matrix_a, matrix_b, (((1,), (1,)), ((), ())), preferred_element_type=F32
    )


def contract_first(matrix_a, matrix_b):
    return lax.dot_general(
        matrix_a, matrix_b, (((0,), (0,)), ((), ())), preferred_element_type=F32
    )


def swiglu_grads(pre_gate, pre_up, back_hidden, weights):
    sigmas = jax.nn.sigmoid(pre_gate)
    active = pre_gate * sigmas
    hidden = (active * pre_up).astype(BF16)
    scaled = weights[:, None] * back_hidden
    grad_gate_pre = (scaled * pre_up * sigmas * (1.0 + pre_gate * (1.0 - sigmas))).astype(BF16)
    grad_up_pre = (scaled * active).astype(BF16)
    return (hidden, grad_gate_pre, grad_up_pre)


def slot_masks(routes_ref, experts, capacity):
    me = lax.axis_index("dp")
    tok_rows = routes_ref.shape[1]
    expert_of_row = jnp.bitwise_xor(me, lax.broadcasted_iota(jnp.int32, (experts, tok_rows), 0))
    first = routes_ref[0:1, :] == expert_of_row
    second = routes_ref[1:2, :] == expert_of_row
    named = jnp.where(first, 1.0, 0.0) + jnp.where(second, 1.0, 0.0)
    before = jnp.where(
        lax.broadcasted_iota(jnp.int32, (tok_rows, tok_rows), 0)
        < lax.broadcasted_iota(jnp.int32, (tok_rows, tok_rows), 1),
        1.0,
        0.0,
    ).astype(BF16)
    rank = jnp.dot(named.astype(BF16), before, preferred_element_type=F32).astype(jnp.int32)
    rank = jnp.where(named > 0.5, rank, -1)
    place = lax.broadcasted_iota(jnp.int32, (capacity, tok_rows), 0)
    hits = [place == rank[k : k + 1, :] for k in range(experts)]
    return first, second, hits


def send_kernel(experts, capacity, routes_ref, combine_ref, tokens_ref, cot_ref, *out_refs):
    first, second, hits = slot_masks(routes_ref, experts, capacity)
    comb = combine_ref[...].astype(F32)
    scale = jnp.where(first, comb[0:1, :], 0.0) + jnp.where(second, comb[1:2, :], 0.0)
    tokens = tokens_ref[...]
    cot = cot_ref[...]
    for k in range(experts):
        pick = jnp.where(hits[k], 1.0, 0.0).astype(BF16)
        weigh = jnp.where(hits[k], scale[k : k + 1, :], 0.0).astype(BF16)
        out_refs[k][0:capacity, :] = jnp.dot(pick, tokens, preferred_element_type=F32).astype(BF16)
        out_refs[k][capacity:, :] = jnp.dot(weigh, cot, preferred_element_type=F32).astype(BF16)


def forward_kernel(blocks, capacity, *refs):
    block_refs = refs[:blocks]
    gate_ref, up_ref, down_ref, left_ref, right_ref = refs[blocks:]
    tok = jnp.concatenate([ref[0:capacity, :] for ref in block_refs], axis=0)
    cot = jnp.concatenate([ref[capacity:, :] for ref in block_refs], axis=0)
    half = blocks // 2 * capacity
    parts = (
        jnp.dot(tok, gate_ref[0], preferred_element_type=F32),
        jnp.dot(tok, up_ref[0], preferred_element_type=F32),
        contract_last(cot, down_ref[0]),
    )
    for i, part in enumerate(parts):
        rounded = part.astype(BF16)
        left_ref[i] = rounded[:half]
        right_ref[i] = rounded[half:]


def backward_kernel(blocks, capacity, u_ref, ur_ref, v_ref, vr_ref, gate_ref, up_ref, *refs):
    hid_ref, gg_ref, gu_ref = refs[:3]
    back_refs = refs[3 : 3 + blocks]
    step = pl.program_id(0)
    columns = gate_ref.shape[1]
    width = pl.num_programs(0) * columns
    half = blocks // 2 * capacity

    @pl.when(step == 0)
    def _():
        eye = lax.broadcasted_iota(jnp.int32, (capacity, LANES), 0) == lax.broadcasted_iota(
            jnp.int32, (capacity, LANES), 1
        )
        for side, (own_ref, got_ref) in enumerate(((u_ref, ur_ref), (v_ref, vr_ref))):
            for b in range(blocks // 2):
                lo, hi = b * capacity, (b + 1) * capacity
                pre_gate, pre_up, back_hidden = (
                    own_ref[i, lo:hi, :].astype(F32) + got_ref[i, lo:hi, :].astype(F32)
                    for i in range(3)
                )
                sigmas = jax.nn.sigmoid(pre_gate)
                active = pre_gate * sigmas
                hidden = (active * pre_up).astype(BF16)
                gg = back_hidden * pre_up * sigmas * (1.0 + pre_gate * (1.0 - sigmas))
                rows = slice(side * half + lo, side * half + hi)
                hid_ref[rows, :] = hidden
                gg_ref[rows, :] = gg.astype(BF16)
                gu_ref[rows, :] = (back_hidden * active).astype(BF16)
                comb = jnp.sum(hidden.astype(F32) * back_hidden, axis=1, keepdims=True)
                row = jnp.sum(jnp.where(eye, comb, 0.0), axis=0, keepdims=True)
                high = row.astype(BF16)
                low = (row - high.astype(F32)).astype(BF16)
                tail = jnp.concatenate(
                    [high.astype(F32), low.astype(F32), jnp.zeros((14, LANES), F32)], axis=0
                )
                k = side * (blocks // 2) + b
                base = width // LANES * capacity
                back_refs[k][base : base + 16, :] = tail.astype(BF16)

    dx = contract_last(gg_ref[...], gate_ref[0]) + contract_last(gu_ref[...], up_ref[0])
    dx = dx.astype(BF16)
    per = columns // LANES
    for k in range(blocks):
        part = dx[k * capacity : (k + 1) * capacity, :]
        stacked = jnp.concatenate(
            [part[:, c * LANES : (c + 1) * LANES] for c in range(per)], axis=0
        )
        start = pl.multiple_of(step * (per * capacity), per * capacity)
        back_refs[k][pl.ds(start, per * capacity), :] = stacked


def weight_kernel(blocks, capacity, chunks, *refs):
    block_refs = refs[:blocks]
    hid_refs = refs[blocks : blocks + chunks]
    gg_refs = refs[blocks + chunks : blocks + 2 * chunks]
    gu_refs = refs[blocks + 2 * chunks : blocks + 3 * chunks]
    gate_ref, up_ref, down_ref = refs[blocks + 3 * chunks :]
    tok = jnp.concatenate([ref[0:capacity, :] for ref in block_refs], axis=0)
    cot = jnp.concatenate([ref[capacity:, :] for ref in block_refs], axis=0)
    join = lambda part: jnp.concatenate([ref[...] for ref in part], axis=0)
    gate_ref[0] = contract_first(tok, join(gg_refs)).astype(BF16)
    up_ref[0] = contract_first(tok, join(gu_refs)).astype(BF16)
    down_ref[0] = contract_first(join(hid_refs), cot).astype(BF16)


def merge_kernel(experts, capacity, routes_ref, combine_ref, *refs):
    back_refs = refs[:experts]
    grad_ref, comb_ref = refs[experts:]
    first, second, hits = slot_masks(routes_ref, experts, capacity)
    picks = [jnp.where(hit, 1.0, 0.0).astype(BF16) for hit in hits]
    pick = jnp.concatenate(picks, axis=0)
    groups = grad_ref.shape[1] // LANES
    for c in range(groups):
        piece = jnp.concatenate(
            [ref[c * capacity : (c + 1) * capacity, :] for ref in back_refs], axis=0
        )
        grad_ref[:, c * LANES : (c + 1) * LANES] = contract_first(pick, piece).astype(BF16)
    total0 = jnp.zeros(first[0:1].shape, F32)
    total1 = total0
    for k in range(experts):
        tail = back_refs[k][groups * capacity : groups * capacity + 16, :][:, :capacity]
        seen = jnp.dot(tail, picks[k], preferred_element_type=F32)
        value = seen[0:1, :] + seen[1:2, :]
        total0 = total0 + jnp.where(first[k : k + 1, :], value, 0.0)
        total1 = total1 + jnp.where(second[k : k + 1, :], value, 0.0)
    comb = combine_ref[...].astype(F32)
    comb_ref[0:1, :] = total0 / comb[0:1, :]
    comb_ref[1:2, :] = total1 / comb[1:2, :]


def permuted(value, axis, flip):
    size = lax.axis_size(axis)
    return lax.ppermute(value, axis, [(i, i ^ flip) for i in range(size)])


def vmem(mib):
    return pltpu.CompilerParams(vmem_limit_bytes=mib * 1024 * 1024)


def shape_of(*dims, dtype=BF16):
    return jax.ShapeDtypeStruct(dims, dtype)


def run_forward(blocks, capacity, w_gate, w_up, w_down):
    count = len(blocks)
    rows, width = blocks[0].shape
    hidden = w_gate.shape[2]
    tile = 256
    half = count // 2 * capacity
    whole = pl.BlockSpec((rows, width), lambda j: (0, 0))
    column = pl.BlockSpec((1, width, tile), lambda j: (0, 0, j))
    out = pl.BlockSpec((3, half, tile), lambda j: (0, 0, j))
    return pl.pallas_call(
        functools.partial(forward_kernel, count, capacity),
        grid=(hidden // tile,),
        in_specs=[whole] * count
        + [column, column, pl.BlockSpec((1, tile, width), lambda j: (0, j, 0))],
        out_specs=[out, out],
        out_shape=[shape_of(3, half, hidden)] * 2,
        compiler_params=vmem(40),
        cost_estimate=pl.CostEstimate(
            flops=6 * count * capacity * width * hidden,
            bytes_accessed=6 * width * hidden,
            transcendentals=0,
        ),
    )(*blocks, w_gate, w_up, w_down)


def run_backward(sums, count, capacity, w_gate, w_up):
    _, width, hidden = w_gate.shape
    tile = 256
    half = count // 2 * capacity
    rows = count * capacity
    part = pl.BlockSpec((3, half, hidden), lambda j: (0, 0, 0))
    row = pl.BlockSpec((1, tile, hidden), lambda j: (0, j, 0))
    kept = pl.BlockSpec((rows, hidden), lambda j: (0, 0))
    length = width // LANES * capacity + 16
    return pl.pallas_call(
        functools.partial(backward_kernel, count, capacity),
        grid=(width // tile,),
        in_specs=[part] * 4 + [row, row],
        out_specs=[kept] * 3 + [pl.BlockSpec((length, LANES), lambda j: (0, 0))] * count,
        out_shape=[shape_of(rows, hidden)] * 3 + [shape_of(length, LANES)] * count,
        compiler_params=vmem(40),
        cost_estimate=pl.CostEstimate(
            flops=4 * rows * width * hidden,
            bytes_accessed=4 * width * hidden,
            transcendentals=rows * hidden,
        ),
    )(*sums, w_gate, w_up)


def run_weights(blocks, capacity, kept, hidden):
    count, chunks = len(blocks), len(kept)
    rows, width = blocks[0].shape
    tile = 256
    column = pl.BlockSpec((rows, tile), lambda j: (0, j))
    flat = [kept[c][i] for i in range(3) for c in range(chunks)]
    held = [pl.BlockSpec(value.shape, lambda j: (0, 0)) for value in flat]
    row = pl.BlockSpec((1, tile, hidden), lambda j: (0, j, 0))
    return pl.pallas_call(
        functools.partial(weight_kernel, count, capacity, chunks),
        grid=(width // tile,),
        in_specs=[column] * count + held,
        out_specs=[row, row, pl.BlockSpec((1, hidden, tile), lambda j: (0, 0, j))],
        out_shape=[shape_of(1, width, hidden)] * 2 + [shape_of(1, hidden, width)],
        compiler_params=vmem(40),
        cost_estimate=pl.CostEstimate(
            flops=6 * count * capacity * width * hidden,
            bytes_accessed=6 * width * hidden,
            transcendentals=0,
        ),
    )(*blocks, *flat)


def expert_total(left, right):
    add = lambda a, b: (a.astype(F32) + b.astype(F32)).astype(BF16)
    left_got = permuted(left, "expert", 1)
    right_got = permuted(right, "expert", 2)
    left_pair = add(left, left_got)
    right_pair = add(right, right_got)
    left_rest = permuted(left_pair, "expert", 2)
    right_rest = permuted(right_pair, "expert", 1)
    return left_pair, left_rest, right_pair, right_rest


def exchange_body(tokens, routes, combine, cotangent, w_gate, w_up, w_down):
    tok_rows, width = tokens.shape
    top_routes = routes.shape[1]
    experts = lax.axis_size("dp")
    capacity = 3 * tok_rows * top_routes // (2 * experts)
    hidden = w_gate.shape[2]
    routes_t, combine_t = routes.T, combine.T
    sends = pl.pallas_call(
        functools.partial(send_kernel, experts, capacity),
        out_shape=[shape_of(2 * capacity, width)] * experts,
        compiler_params=vmem(40),
    )(routes_t, combine_t, tokens, cotangent)
    order = [4, 5, 6, 7, 2, 3, 1]
    blocks = {0: sends[0]}
    for k in order:
        blocks[k] = permuted(sends[k], "dp", k)
    kept, backs = [], {}
    for chunk in ((0, 1, 2, 3), (4, 5), (6, 7)):
        left, right = run_forward([blocks[k] for k in chunk], capacity, w_gate, w_up, w_down)
        sums = expert_total(left, right)
        out = run_backward(sums, len(chunk), capacity, w_gate, w_up)
        kept.append(out[:3])
        for k, value in zip(chunk, out[3:]):
            backs[k] = value if k == 0 else permuted(value, "dp", k)
    grad_gate, grad_up, grad_down = run_weights(
        [blocks[k] for k in range(experts)], capacity, kept, hidden
    )
    token_grad, comb_grad = pl.pallas_call(
        functools.partial(merge_kernel, experts, capacity),
        out_shape=[shape_of(tok_rows, width), shape_of(top_routes, tok_rows, dtype=F32)],
        compiler_params=vmem(40),
    )(routes_t, combine_t, *[backs[k] for k in range(experts)])
    return (token_grad, comb_grad.T, grad_gate, grad_up, grad_down)


def gather_body(tokens, routes, combine, cotangent, w_gate, w_up, w_down):
    tok_rows, slice_width = tokens.shape
    top_routes = routes.shape[1]
    experts = lax.axis_size("dp")
    capacity = 3 * tok_rows * top_routes // (2 * experts)
    route_count = tok_rows * top_routes
    slot_total = experts * capacity
    route_flat = routes.reshape(route_count)
    onehot = (route_flat[:, None] == jnp.arange(experts, dtype=jnp.int32)[None, :]).astype(
        jnp.int32
    )
    slot_rank = jnp.sum((jnp.cumsum(onehot, axis=0) - onehot) * onehot, axis=1)
    places = route_flat * capacity + slot_rank
    source = jnp.full((slot_total,), route_count, jnp.int32)
    source = source.at[places].set(jnp.arange(route_count, dtype=jnp.int32))
    blank_row = jnp.zeros((1, slice_width), BF16)
    token_send = jnp.concatenate([tokens, blank_row], axis=0)[source // top_routes]
    cot_send = jnp.concatenate([cotangent, blank_row], axis=0)[source // top_routes]
    comb_send = jnp.concatenate(
        [combine.reshape(route_count), jnp.zeros((1,), BF16)], axis=0
    )[source]
    spread = functools.partial(
        lax.all_to_all, axis_name="dp", split_axis=0, concat_axis=0, tiled=True
    )
    token_slots = spread(token_send.reshape(experts, capacity, slice_width)).reshape(
        slot_total, slice_width
    )
    cot_slots = spread(cot_send.reshape(experts, capacity, slice_width)).reshape(
        slot_total, slice_width
    )
    comb_slots = spread(comb_send.reshape(experts, capacity)).reshape(slot_total).astype(F32)
    gate_mat, up_mat, down_mat = w_gate[0], w_up[0], w_down[0]
    partials = jnp.stack(
        [
            jnp.dot(token_slots, gate_mat, preferred_element_type=F32),
            jnp.dot(token_slots, up_mat, preferred_element_type=F32),
            contract_last(cot_slots, down_mat),
        ],
        axis=1,
    )
    summed = lax.psum_scatter(
        partials.astype(BF16), "expert", scatter_dimension=2, tiled=True
    ).astype(F32)
    hidden_part, gate_part, up_part = swiglu_grads(
        summed[:, 0], summed[:, 1], summed[:, 2], comb_slots
    )
    slot_comb = jnp.sum(hidden_part.astype(F32) * summed[:, 2], axis=1)
    joined = lax.all_gather(
        jnp.stack([hidden_part, gate_part, up_part], axis=1), "expert", axis=2, tiled=True
    )
    hidden, grad_gate_pre, grad_up_pre = joined[:, 0], joined[:, 1], joined[:, 2]
    slot_dx = contract_last(grad_gate_pre, gate_mat) + contract_last(grad_up_pre, up_mat)
    scaled_dy = (comb_slots[:, None] * cot_slots.astype(F32)).astype(BF16)
    grad_gate = contract_first(token_slots, grad_gate_pre).astype(BF16)[None]
    grad_up = contract_first(token_slots, grad_up_pre).astype(BF16)[None]
    grad_down = contract_first(hidden, scaled_dy).astype(BF16)[None]
    back_dx = spread(slot_dx.reshape(experts, capacity, slice_width).astype(BF16)).astype(F32)
    back_comb = spread(slot_comb.reshape(experts, capacity).astype(BF16)).astype(F32)
    route_dx = back_dx.reshape(slot_total, slice_width)[places].reshape(
        tok_rows, top_routes, slice_width
    )
    token_grad = jnp.sum(route_dx, axis=1).astype(BF16)
    comb_part = back_comb.reshape(slot_total)[places].reshape(tok_rows, top_routes)
    combine_grad = lax.psum(comb_part, "expert")
    return (token_grad, combine_grad, grad_gate, grad_up, grad_down)


def body(tokens, routes, combine, cotangent, w_gate, w_up, w_down):
    tok_rows, width = tokens.shape
    experts = lax.axis_size("dp")
    capacity = 3 * tok_rows * routes.shape[1] // (2 * experts)
    fits = (
        experts == 8
        and lax.axis_size("expert") == 4
        and routes.shape[1] == 2
        and tok_rows == LANES
        and capacity % 16 == 0
        and width % 256 == 0
        and w_gate.shape[2] % 256 == 0
    )
    run = exchange_body if fits else gather_body
    return run(tokens, routes, combine, cotangent, w_gate, w_up, w_down)


def solution(mesh):
    in_specs = (
        P("dp", "expert"),
        P("dp", None),
        P("dp", None),
        P("dp", "expert"),
        P("dp", "expert", None),
        P("dp", "expert", None),
        P("dp", None, "expert"),
    )
    out_specs = (
        P("dp", "expert"),
        P("dp", None),
        P("dp", "expert", None),
        P("dp", "expert", None),
        P("dp", None, "expert"),
    )
    return jax.shard_map(body, mesh=mesh, in_specs=in_specs, out_specs=out_specs, check_vma=False)
```

time: 219 us -> 113 us (0.52)
  waiting for transfers between devices: 89.4 us -> 27.1 us
  starting transfers between devices: 19.3 us -> 55.2 us
  local copies, waits for them, and re-layouts: 36.5 us -> 7.92 us
  blocking collectives: 24.1 us -> 0 us
  matrix products: 21.7 us -> 0 us
  Pallas kernels: 0 us -> 21.1 us
  between operations: 14.3 us -> 0.8 us
  other arithmetic: 13 us -> 0.47 us
    ppermute x0 -> x26, starting transfers between devices: none -> 55.2 us  [permuted(): return lax.ppermute(value, axis, [(i, i ^ flip) for i in range(size)])]
    all_to_all x4 -> x0, waiting for transfers between devices: 41.9 us -> none  [the longest x1 21.4 us: body(): lax.all_to_all(token_send.reshape(experts, capacity, slice_width), 'dp',...]
    all_gather x1 -> x0, waiting for transfers between devices: 27.2 us -> none  [body(): lax.all_gather(jnp.stack([hidden_part, gate_part, up_part], axis=1), 'exp...]
    ppermute x0 -> x26, waiting for transfers between devices: none -> 27.1 us  [permuted(): return lax.ppermute(value, axis, [(i, i ^ flip) for i in range(size)])]
    dot_general x8 -> x0, matrix products: 21.7 us -> none  [the longest x3 8.94 us: contract_first(): lax.dot_general(matrix_a, matrix_b, (((0,), (0,)), ((), ())), preferred_e...]
    pallas_call x0 -> x9, Pallas kernels: none -> 21.1 us  [the longest x3 7.21 us: run_backward(): pl.pallas_call(functools.partial(backward_kernel, count, capacity), grid=...]
    unnamed x3 -> x0, waiting for transfers between devices: 20.3 us -> none
    all_to_all x4 -> x0, starting transfers between devices: 19.2 us -> none  [the longest x1 6.33 us: body(): lax.all_to_all(token_send.reshape(experts, capacity, slice_width), 'dp',...]
  transfers between devices with their start and end apart: 6 -> 26, of which waited for: 4 -> 8; matrix products, arithmetic and copies ran while one was open for 14% -> 0% of each run, Pallas kernels for 0% -> 17%
where the time goes in v1:
time: 113 us
  starting transfers between devices  55.2 us (49%)
  waiting for transfers between devices  27.1 us (24%)
  Pallas kernels  21.1 us (19%)
  local copies, waits for them, and re-layouts  7.92 us (7%)
    ppermute x26, starting transfers between devices, permuted(): return lax.ppermute(value, axis, [(i, i ^ flip) for i in range(size)])  55.2 us
    ppermute x26, waiting for transfers between devices, permuted(): return lax.ppermute(value, axis, [(i, i ^ flip) for i in range(size)])  27.1 us
    unnamed x20, local copies, waits for them, and re-layouts  7.92 us
    pallas_call x3, Pallas kernels, run_backward(): pl.pallas_call(functools.partial(backward_kernel, count, capacity), grid=...  7.21 us
    pallas_call x3, Pallas kernels, run_forward(): pl.pallas_call(functools.partial(forward_kernel, count, capacity), grid=(...  6.28 us
    pallas_call x1, Pallas kernels, run_weights(): pl.pallas_call(functools.partial(weight_kernel, count, capacity, chunks),...  5.28 us
  transfers between devices with their start and end apart: 26, of which 8 were waited for; matrix products, arithmetic and copies ran while one was open for 0% of the time, Pallas kernels for 17%

profile of v1, /device:TPU:0, one launch (start us, length us, event | category | flops | bytes accessed | tf_op | source)
XLA Modules:
  0.0 112.6 jit_solution(13503970794323038237)
XLA Ops:
  4.9 5.1 %collective-permute-start.18 = (bf16[96,1280]{1,0:T(8,128)(2,1)S(1)}, bf16[96,1280]{1,0:T(8,128)(2,1)S(1)}, u32[]{:S(2)}, u32[]{:S(2)}) collective-permute-start(bf16[96,1280]{1,0:T(8,128)(2,1)S(1)} %get-tuple-element.57), channel_id=1, source_target_pairs={{0,6},{1,7},{2,4},{3,5},{4,2},{5,3},{6,0},{7,1},{8,14},{9,15},{10,... | collective-permute-start | bytes 737288 | tf_op jit(solution)/shard_map/ppermute | solution.py:178
  10.2 2.3 %collective-permute-start.11 = (bf16[96,1280]{1,0:T(8,128)(2,1)S(1)}, bf16[96,1280]{1,0:T(8,128)(2,1)S(1)}, u32[]{:S(2)}, u32[]{:S(2)}) collective-permute-start(bf16[96,1280]{1,0:T(8,128)(2,1)S(1)} %get-tuple-element.52), channel_id=1, source_target_pairs={{0,5},{1,4},{2,7},{3,6},{4,1},{5,0},{6,3},{7,2},{8,13},{9,12},{10,... | collective-permute-start | bytes 737288 | tf_op jit(solution)/shard_map/ppermute | solution.py:178
  13.0 3.8 %collective-permute-done.18.refs_0_.refs_6_ = bf16[96,1280]{1,0:T(8,128)(2,1)S(1)} collective-permute-done((bf16[96,1280]{1,0:T(8,128)(2,1)S(1)}, bf16[96,1280]{1,0:T(8,128)(2,1)S(1)}, u32[]{:S(2)}, u32[]{:S(2)}) %collective-permute-start.18) | collective-permute-done | bytes 245792 | tf_op jit(solution)/shard_map/ppermute | solution.py:178
  16.9 20.8 %collective-permute-start.1 = (bf16[96,1280]{1,0:T(8,128)(2,1)S(1)}, bf16[96,1280]{1,0:T(8,128)(2,1)S(1)}, u32[]{:S(2)}, u32[]{:S(2)}) collective-permute-start(bf16[96,1280]{1,0:T(8,128)(2,1)S(1)} %get-tuple-element.43), channel_id=1, source_target_pairs={{0,2},{1,3},{2,0},{3,1},{4,6},{5,7},{6,4},{7,5},{8,10},{9,11},{10,... | collective-permute-start | bytes 737288 | tf_op jit(solution)/shard_map/ppermute | solution.py:178
  37.7 5.0 %collective-permute-start.2 = (bf16[96,1280]{1,0:T(8,128)(2,1)S(1)}, bf16[96,1280]{1,0:T(8,128)(2,1)S(1)}, u32[]{:S(2)}, u32[]{:S(2)}) collective-permute-start(bf16[96,1280]{1,0:T(8,128)(2,1)S(1)} %get-tuple-element.44), channel_id=1, source_target_pairs={{0,3},{1,2},{2,1},{3,0},{4,7},{5,6},{6,5},{7,4},{8,11},{9,10},{10,... | collective-permute-start | bytes 737288 | tf_op jit(solution)/shard_map/ppermute | solution.py:178
  42.7 1.5 %copy-done = bf16[1,1280,768]{2,1,0:T(8,128)(2,1)S(1)} copy-done((bf16[1,1280,768]{2,1,0:T(8,128)(2,1)S(1)}, bf16[1,1280,768]{2,1,0:T(8,128)(2,1)}, u32[]{:S(2)}) %copy-start) | copy-done | bytes 1966104
  44.2 1.5 %copy-done.2 = bf16[1,1280,768]{2,1,0:T(8,128)(2,1)S(1)} copy-done((bf16[1,1280,768]{2,1,0:T(8,128)(2,1)S(1)}, bf16[1,1280,768]{2,1,0:T(8,128)(2,1)}, u32[]{:S(2)}) %copy-start.2) | copy-done | bytes 1966104
  47.3 2.0 %shard_map.115 = (bf16[3,48,768]{2,1,0:T(8,128)(2,1)S(1)}, bf16[3,48,768]{2,1,0:T(8,128)(2,1)S(1)}) custom-call(bf16[96,1280]{1,0:T(8,128)(2,1)S(1)} %collective-permute-done.18.refs_0_.refs_6_, bf16[96,1280]{1,0:T(8,128)(2,1)S(1)} %collective-permute-done.19.refs_1_.refs_7_, bf16[1,1280,768]{2,1,0:T(8,128)(2,1)S(1)} %copy-done, ...), custom_call_target="tpu_custom_call" | custom-call | flops 566231040 | bytes 5898240 | tf_op jit(solution)/shard_map/pallas_call | solution.py:198
  49.3 1.6 %collective-permute-start.20 = (bf16[3,48,768]{2,1,0:T(8,128)(2,1)S(1)}, bf16[3,48,768]{2,1,0:T(8,128)(2,1)S(1)}, u32[]{:S(2)}, u32[]{:S(2)}) collective-permute-start(bf16[3,48,768]{2,1,0:T(8,128)(2,1)S(1)} %get-tuple-element.59), channel_id=1, source_target_pairs={{0,8},{8,0},{16,24},{24,16},{1,9},{9,1},{17,25},{25,17},{2,10},{10... | collective-permute-start | bytes 663560 | tf_op jit(solution)/shard_map/ppermute | solution.py:178
  52.6 2.0 %shard_map.113 = (bf16[3,48,768]{2,1,0:T(8,128)(2,1)S(1)}, bf16[3,48,768]{2,1,0:T(8,128)(2,1)S(1)}) custom-call(bf16[96,1280]{1,0:T(8,128)(2,1)S(1)} %collective-permute-done.10.refs_0_.refs_4_, bf16[96,1280]{1,0:T(8,128)(2,1)S(1)} %collective-permute-done.11.refs_1_.refs_5_, bf16[1,1280,768]{2,1,0:T(8,128)(2,1)S(1)} %copy-done, ...), custom_call_target="tpu_custom_call" | custom-call | flops 566231040 | bytes 5898240 | tf_op jit(solution)/shard_map/pallas_call | solution.py:198
  54.6 1.6 %collective-permute-start.12 = (bf16[3,48,768]{2,1,0:T(8,128)(2,1)S(1)}, bf16[3,48,768]{2,1,0:T(8,128)(2,1)S(1)}, u32[]{:S(2)}, u32[]{:S(2)}) collective-permute-start(bf16[3,48,768]{2,1,0:T(8,128)(2,1)S(1)} %get-tuple-element.53), channel_id=1, source_target_pairs={{0,8},{8,0},{16,24},{24,16},{1,9},{9,1},{17,25},{25,17},{2,10},{10... | collective-permute-start | bytes 663560 | tf_op jit(solution)/shard_map/ppermute | solution.py:178
  57.4 2.3 %shard_map.111 = (bf16[3,96,768]{2,1,0:T(8,128)(2,1)S(1)}, bf16[3,96,768]{2,1,0:T(8,128)(2,1)S(1)}) custom-call(bf16[96,1280]{1,0:T(8,128)(2,1)S(1)} %get-tuple-element.41.refs_0_, bf16[96,1280]{1,0:T(8,128)(2,1)S(1)} %collective-permute-done.refs_1_, bf16[96,1280]{1,0:T(8,128)(2,1)S(1)} %collective-permute-done.1.refs_2_, ...), custom_call_target="tpu_custom_call" | custom-call | flops 1132462080 | bytes 5898240 | tf_op jit(solution)/shard_map/pallas_call | solution.py:198
  59.7 1.6 %collective-permute-start.3 = (bf16[3,96,768]{2,1,0:T(8,128)(2,1)S(1)}, bf16[3,96,768]{2,1,0:T(8,128)(2,1)S(1)}, u32[]{:S(2)}, u32[]{:S(2)}) collective-permute-start(bf16[3,96,768]{2,1,0:T(8,128)(2,1)S(1)} %get-tuple-element.45), channel_id=1, source_target_pairs={{0,8},{8,0},{16,24},{24,16},{1,9},{9,1},{17,25},{25,17},{2,10},{10... | collective-permute-start | bytes 1327112 | tf_op jit(solution)/shard_map/ppermute | solution.py:178
  64.2 8.6 %collective-permute-done.3 = bf16[3,96,768]{2,1,0:T(8,128)(2,1)S(1)} collective-permute-done((bf16[3,96,768]{2,1,0:T(8,128)(2,1)S(1)}, bf16[3,96,768]{2,1,0:T(8,128)(2,1)S(1)}, u32[]{:S(2)}, u32[]{:S(2)}) %collective-permute-start.3) | collective-permute-done | bytes 442400 | tf_op jit(solution)/shard_map/ppermute | solution.py:178
  76.9 2.1 %collective-permute-done.21.ur_ref = bf16[3,48,768]{2,1,0:T(8,128)(2,1)S(1)} collective-permute-done((bf16[3,48,768]{2,1,0:T(8,128)(2,1)S(1)}, bf16[3,48,768]{2,1,0:T(8,128)(2,1)S(1)}, u32[]{:S(2)}, u32[]{:S(2)}) %collective-permute-start.21) | collective-permute-done | bytes 221216 | tf_op jit(solution)/shard_map/ppermute | solution.py:178
  79.9 2.2 %shard_map.116 = (bf16[96,768]{1,0:T(8,128)(2,1)S(1)}, bf16[96,768]{1,0:T(8,128)(2,1)S(1)}, bf16[96,768]{1,0:T(8,128)(2,1)S(1)}, bf16[496,128]{1,0:T(8,128)(2,1)S(1)}, bf16[496,128]{1,0:T(8,128)(2,1)S(1)}) custom-call(bf16[3,48,768]{2,1,0:T(8,128)(2,1)S(1)} %add_convert_fusion.3.u_ref, bf16[3,48,768]{2,1,0:T(8,128)(2,1)S(1)} %collective-permute-done.21.ur_ref, ...), custom_call_target="tpu_custom_call" | custom-call | flops 377487360 | bytes 3932160 | tf_op jit(solution)/shard_map/pallas_call | solution.py:223
  82.1 2.3 %collective-permute-start.24 = (bf16[496,128]{1,0:T(8,128)(2,1)S(1)}, bf16[496,128]{1,0:T(8,128)(2,1)S(1)}, u32[]{:S(2)}, u32[]{:S(2)}) collective-permute-start(bf16[496,128]{1,0:T(8,128)(2,1)S(1)} %get-tuple-element.61), channel_id=1, source_target_pairs={{0,6},{1,7},{2,4},{3,5},{4,2},{5,3},{6,0},{7,1},{8,14},{9,15},{10,... | collective-permute-start | bytes 380936 | tf_op jit(solution)/shard_map/ppermute | solution.py:178
  84.8 6.6 %collective-permute-done.15.vr_ref = bf16[3,48,768]{2,1,0:T(8,128)(2,1)S(1)} collective-permute-done((bf16[3,48,768]{2,1,0:T(8,128)(2,1)S(1)}, bf16[3,48,768]{2,1,0:T(8,128)(2,1)S(1)}, u32[]{:S(2)}, u32[]{:S(2)}) %collective-permute-start.15) | collective-permute-done | bytes 221216 | tf_op jit(solution)/shard_map/ppermute | solution.py:178
  91.4 2.2 %shard_map.114 = (bf16[96,768]{1,0:T(8,128)(2,1)S(1)}, bf16[96,768]{1,0:T(8,128)(2,1)S(1)}, bf16[96,768]{1,0:T(8,128)(2,1)S(1)}, bf16[496,128]{1,0:T(8,128)(2,1)S(1)}, bf16[496,128]{1,0:T(8,128)(2,1)S(1)}) custom-call(bf16[3,48,768]{2,1,0:T(8,128)(2,1)S(1)} %add_convert_fusion.5.u_ref, bf16[3,48,768]{2,1,0:T(8,128)(2,1)S(1)} %collective-permute-done.13.ur_ref, ...), custom_call_target="tpu_custom_call" | custom-call | flops 377487360 | bytes 3932160 | tf_op jit(solution)/shard_map/pallas_call | solution.py:223
  93.8 2.8 %shard_map.112 = (bf16[192,768]{1,0:T(8,128)(2,1)S(1)}, bf16[192,768]{1,0:T(8,128)(2,1)S(1)}, bf16[192,768]{1,0:T(8,128)(2,1)S(1)}, bf16[496,128]{1,0:T(8,128)(2...) custom-call(bf16[3,96,768]{2,1,0:T(8,128)(2,1)S(1)} %add_convert_fusion.1.u_ref, ...), custom_call_target="tpu_custom_call" | custom-call | flops 754974720 | bytes 3932160 | tf_op jit(solution)/shard_map/pallas_call | solution.py:223
  96.6 3.0 %collective-permute-start.7 = (bf16[496,128]{1,0:T(8,128)(2,1)S(1)}, bf16[496,128]{1,0:T(8,128)(2,1)S(1)}, u32[]{:S(2)}, u32[]{:S(2)}) collective-permute-start(bf16[496,128]{1,0:T(8,128)(2,1)S(1)} %get-tuple-element.48), channel_id=1, source_target_pairs={{0,1},{1,0},{2,3},{3,2},{4,5},{5,4},{6,7},{7,6},{8,9},{9,8},{10,11... | collective-permute-start | bytes 380936 | tf_op jit(solution)/shard_map/ppermute | solution.py:178
  101.0 5.3 %shard_map.118 = (bf16[1,1280,768]{2,1,0:T(8,128)(2,1)}, bf16[1,1280,768]{2,1,0:T(8,128)(2,1)}, bf16[1,768,1280]{2,1,0:T(8,128)(2,1)}) custom-call(bf16[96,1280]{1,0:T(8,128)(2,1)S(1)} %get-tuple-element.41.refs_0_, bf16[96,1280]{1,0:T(8,128)(2,1)S(1)} %collective-permute-done.refs_1_, bf16[96,1280]{1,0:T(8,128)(2,1)S(1)} %collective-permute-done.1.refs_2_, ...), custom_call_target="tpu_custom_call" | custom-call | flops 2264924160 | bytes 5898240 | tf_op jit(solution)/shard_map/pallas_call | solution.py:246
  106.3 2.4 %collective-permute-done.8.refs_2_ = bf16[496,128]{1,0:T(8,128)(2,1)S(1)} collective-permute-done((bf16[496,128]{1,0:T(8,128)(2,1)S(1)}, bf16[496,128]{1,0:T(8,128)(2,1)S(1)}, u32[]{:S(2)}, u32[]{:S(2)}) %collective-permute-start.8) | collective-permute-done | bytes 127008 | tf_op jit(solution)/shard_map/ppermute | solution.py:178
  108.7 2.6 %collective-permute-done.9.refs_3_ = bf16[496,128]{1,0:T(8,128)(2,1)S(1)} collective-permute-done((bf16[496,128]{1,0:T(8,128)(2,1)S(1)}, bf16[496,128]{1,0:T(8,128)(2,1)S(1)}, u32[]{:S(2)}, u32[]{:S(2)}) %collective-permute-start.9) | collective-permute-done | bytes 127008 | tf_op jit(solution)/shard_map/ppermute | solution.py:178
  (63 shorter events, 20.7 us)
Async XLA Ops:
  4.9 12.0 %collective-permute-start.18 = (bf16[96,1280]{1,0:T(8,128)(2,1)S(1)}, bf16[96,1280]{1,0:T(8,128)(2,1)S(1)}, u32[]{:S(2)}, u32[]{:S(2)}) collective-permute-start(bf16[96,1280]{1,0:T(8,128)(2,1)S(1)} %get-tuple-element.57), channel_id=1, source_target_pairs={{0,6},{1,7},{2,4},{3,5},{4,2},{5,3},{6,0},{7,1},{8,14},{9,15},{10,... | collective-permute-start | bytes 737288 | tf_op jit(solution)/shard_map/ppermute | solution.py:178
  10.0 27.7 %collective-permute-start.19 = (bf16[96,1280]{1,0:T(8,128)(2,1)S(1)}, bf16[96,1280]{1,0:T(8,128)(2,1)S(1)}, u32[]{:S(2)}, u32[]{:S(2)}) collective-permute-start(bf16[96,1280]{1,0:T(8,128)(2,1)S(1)} %get-tuple-element.58), channel_id=1, source_target_pairs={{0,7},{1,6},{2,5},{3,4},{4,3},{5,2},{6,1},{7,0},{8,15},{9,14},{10,... | collective-permute-start | bytes 737288 | tf_op jit(solution)/shard_map/ppermute | solution.py:178
  10.0 39.3 %collective-permute-start.10 = (bf16[96,1280]{1,0:T(8,128)(2,1)S(1)}, bf16[96,1280]{1,0:T(8,128)(2,1)S(1)}, u32[]{:S(2)}, u32[]{:S(2)}) collective-permute-start(bf16[96,1280]{1,0:T(8,128)(2,1)S(1)} %get-tuple-element.51), channel_id=1, source_target_pairs={{0,4},{1,5},{2,6},{3,7},{4,0},{5,1},{6,2},{7,3},{8,12},{9,13},{10,... | collective-permute-start | bytes 737288 | tf_op jit(solution)/shard_map/ppermute | solution.py:178
  10.2 40.9 %collective-permute-start.11 = (bf16[96,1280]{1,0:T(8,128)(2,1)S(1)}, bf16[96,1280]{1,0:T(8,128)(2,1)S(1)}, u32[]{:S(2)}, u32[]{:S(2)}) collective-permute-start(bf16[96,1280]{1,0:T(8,128)(2,1)S(1)} %get-tuple-element.52), channel_id=1, source_target_pairs={{0,5},{1,4},{2,7},{3,6},{4,1},{5,0},{6,3},{7,2},{8,13},{9,12},{10,... | collective-permute-start | bytes 737288 | tf_op jit(solution)/shard_map/ppermute | solution.py:178
  12.4 42.2 %collective-permute-start = (bf16[96,1280]{1,0:T(8,128)(2,1)S(1)}, bf16[96,1280]{1,0:T(8,128)(2,1)S(1)}, u32[]{:S(2)}, u32[]{:S(2)}) collective-permute-start(bf16[96,1280]{1,0:T(8,128)(2,1)S(1)} %get-tuple-element.42), channel_id=1, source_target_pairs={{0,1},{1,0},{2,3},{3,2},{4,5},{5,4},{6,7},{7,6},{8,9},{9,8},{10,11... | collective-permute-start | bytes 737288 | tf_op jit(solution)/shard_map/ppermute | solution.py:178
  16.9 39.3 %collective-permute-start.1 = (bf16[96,1280]{1,0:T(8,128)(2,1)S(1)}, bf16[96,1280]{1,0:T(8,128)(2,1)S(1)}, u32[]{:S(2)}, u32[]{:S(2)}) collective-permute-start(bf16[96,1280]{1,0:T(8,128)(2,1)S(1)} %get-tuple-element.43), channel_id=1, source_target_pairs={{0,2},{1,3},{2,0},{3,1},{4,6},{5,7},{6,4},{7,5},{8,10},{9,11},{10,... | collective-permute-start | bytes 737288 | tf_op jit(solution)/shard_map/ppermute | solution.py:178
  37.7 19.7 %collective-permute-start.2 = (bf16[96,1280]{1,0:T(8,128)(2,1)S(1)}, bf16[96,1280]{1,0:T(8,128)(2,1)S(1)}, u32[]{:S(2)}, u32[]{:S(2)}) collective-permute-start(bf16[96,1280]{1,0:T(8,128)(2,1)S(1)} %get-tuple-element.44), channel_id=1, source_target_pairs={{0,3},{1,2},{2,1},{3,0},{4,7},{5,6},{6,5},{7,4},{8,11},{9,10},{10,... | collective-permute-start | bytes 737288 | tf_op jit(solution)/shard_map/ppermute | solution.py:178
  49.3 12.0 %collective-permute-start.20 = (bf16[3,48,768]{2,1,0:T(8,128)(2,1)S(1)}, bf16[3,48,768]{2,1,0:T(8,128)(2,1)S(1)}, u32[]{:S(2)}, u32[]{:S(2)}) collective-permute-start(bf16[3,48,768]{2,1,0:T(8,128)(2,1)S(1)} %get-tuple-element.59), channel_id=1, source_target_pairs={{0,8},{8,0},{16,24},{24,16},{1,9},{9,1},{17,25},{25,17},{2,10},{10... | collective-permute-start | bytes 663560 | tf_op jit(solution)/shard_map/ppermute | solution.py:178
  51.1 11.8 %collective-permute-start.22 = (bf16[3,48,768]{2,1,0:T(8,128)(2,1)S(1)}, bf16[3,48,768]{2,1,0:T(8,128)(2,1)S(1)}, u32[]{:S(2)}, u32[]{:S(2)}) collective-permute-start(bf16[3,48,768]{2,1,0:T(8,128)(2,1)S(1)} %get-tuple-element.60), channel_id=1, source_target_pairs={{0,16},{8,24},{16,0},{24,8},{1,17},{9,25},{17,1},{25,9},{2,18},{10... | collective-permute-start | bytes 663560 | tf_op jit(solution)/shard_map/ppermute | solution.py:178
  56.2 19.8 %collective-permute-start.14 = (bf16[3,48,768]{2,1,0:T(8,128)(2,1)S(1)}, bf16[3,48,768]{2,1,0:T(8,128)(2,1)S(1)}, u32[]{:S(2)}, u32[]{:S(2)}) collective-permute-start(bf16[3,48,768]{2,1,0:T(8,128)(2,1)S(1)} %get-tuple-element.54), channel_id=1, source_target_pairs={{0,16},{8,24},{16,0},{24,8},{1,17},{9,25},{17,1},{25,9},{2,18},{10... | collective-permute-start | bytes 663560 | tf_op jit(solution)/shard_map/ppermute | solution.py:178
  59.7 13.0 %collective-permute-start.3 = (bf16[3,96,768]{2,1,0:T(8,128)(2,1)S(1)}, bf16[3,96,768]{2,1,0:T(8,128)(2,1)S(1)}, u32[]{:S(2)}, u32[]{:S(2)}) collective-permute-start(bf16[3,96,768]{2,1,0:T(8,128)(2,1)S(1)} %get-tuple-element.45), channel_id=1, source_target_pairs={{0,8},{8,0},{16,24},{24,16},{1,9},{9,1},{17,25},{25,17},{2,10},{10... | collective-permute-start | bytes 1327112 | tf_op jit(solution)/shard_map/ppermute | solution.py:178
  61.3 13.1 %collective-permute-start.5 = (bf16[3,96,768]{2,1,0:T(8,128)(2,1)S(1)}, bf16[3,96,768]{2,1,0:T(8,128)(2,1)S(1)}, u32[]{:S(2)}, u32[]{:S(2)}) collective-permute-start(bf16[3,96,768]{2,1,0:T(8,128)(2,1)S(1)} %get-tuple-element.46), channel_id=1, source_target_pairs={{0,16},{8,24},{16,0},{24,8},{1,17},{9,25},{17,1},{25,9},{2,18},{10... | collective-permute-start | bytes 1327112 | tf_op jit(solution)/shard_map/ppermute | solution.py:178
  62.9 16.1 %collective-permute-start.21 = (bf16[3,48,768]{2,1,0:T(8,128)(2,1)S(1)}, bf16[3,48,768]{2,1,0:T(8,128)(2,1)S(1)}, u32[]{:S(2)}, u32[]{:S(2)}) collective-permute-start(bf16[3,48,768]{2,1,0:T(8,128)(2,1)S(1)} %add_convert_fusion.3.u_ref), channel_id=1, source_target_pairs={{0,16},{8,24},{16,0},{24,8},{1,17},{9,25},{17,1},{25,9},{2,18},{10... | collective-permute-start | bytes 663560 | tf_op jit(solution)/shard_map/ppermute | solution.py:178
  63.5 16.3 %collective-permute-start.23 = (bf16[3,48,768]{2,1,0:T(8,128)(2,1)S(1)}, bf16[3,48,768]{2,1,0:T(8,128)(2,1)S(1)}, u32[]{:S(2)}, u32[]{:S(2)}) collective-permute-start(bf16[3,48,768]{2,1,0:T(8,128)(2,1)S(1)} %add_convert_fusion.2.v_ref), channel_id=1, source_target_pairs={{0,8},{8,0},{16,24},{24,16},{1,9},{9,1},{17,25},{25,17},{2,10},{10... | collective-permute-start | bytes 663560 | tf_op jit(solution)/shard_map/ppermute | solution.py:178
  72.8 11.7 %collective-permute-start.13 = (bf16[3,48,768]{2,1,0:T(8,128)(2,1)S(1)}, bf16[3,48,768]{2,1,0:T(8,128)(2,1)S(1)}, u32[]{:S(2)}, u32[]{:S(2)}) collective-permute-start(bf16[3,48,768]{2,1,0:T(8,128)(2,1)S(1)} %add_convert_fusion.5.u_ref), channel_id=1, source_target_pairs={{0,16},{8,24},{16,0},{24,8},{1,17},{9,25},{17,1},{25,9},{2,18},{10... | collective-permute-start | bytes 663560 | tf_op jit(solution)/shard_map/ppermute | solution.py:178
  74.4 19.4 %collective-permute-start.4 = (bf16[3,96,768]{2,1,0:T(8,128)(2,1)S(1)}, bf16[3,96,768]{2,1,0:T(8,128)(2,1)S(1)}, u32[]{:S(2)}, u32[]{:S(2)}) collective-permute-start(bf16[3,96,768]{2,1,0:T(8,128)(2,1)S(1)} %add_convert_fusion.1.u_ref), channel_id=1, source_target_pairs={{0,16},{8,24},{16,0},{24,8},{1,17},{9,25},{17,1},{25,9},{2,18},{10... | collective-permute-start | bytes 1327112 | tf_op jit(solution)/shard_map/ppermute | solution.py:178
  76.0 17.9 %collective-permute-start.6 = (bf16[3,96,768]{2,1,0:T(8,128)(2,1)S(1)}, bf16[3,96,768]{2,1,0:T(8,128)(2,1)S(1)}, u32[]{:S(2)}, u32[]{:S(2)}) collective-permute-start(bf16[3,96,768]{2,1,0:T(8,128)(2,1)S(1)} %add_convert_fusion.v_ref), channel_id=1, source_target_pairs={{0,8},{8,0},{16,24},{24,16},{1,9},{9,1},{17,25},{25,17},{2,10},{10... | collective-permute-start | bytes 1327112 | tf_op jit(solution)/shard_map/ppermute | solution.py:178
  79.0 12.3 %collective-permute-start.15 = (bf16[3,48,768]{2,1,0:T(8,128)(2,1)S(1)}, bf16[3,48,768]{2,1,0:T(8,128)(2,1)S(1)}, u32[]{:S(2)}, u32[]{:S(2)}) collective-permute-start(bf16[3,48,768]{2,1,0:T(8,128)(2,1)S(1)} %add_convert_fusion.4.v_ref), channel_id=1, source_target_pairs={{0,8},{8,0},{16,24},{24,16},{1,9},{9,1},{17,25},{25,17},{2,10},{10... | collective-permute-start | bytes 663560 | tf_op jit(solution)/shard_map/ppermute | solution.py:178
  82.1 17.4 %collective-permute-start.24 = (bf16[496,128]{1,0:T(8,128)(2,1)S(1)}, bf16[496,128]{1,0:T(8,128)(2,1)S(1)}, u32[]{:S(2)}, u32[]{:S(2)}) collective-permute-start(bf16[496,128]{1,0:T(8,128)(2,1)S(1)} %get-tuple-element.61), channel_id=1, source_target_pairs={{0,6},{1,7},{2,4},{3,5},{4,2},{5,3},{6,0},{7,1},{8,14},{9,15},{10,... | collective-permute-start | bytes 380936 | tf_op jit(solution)/shard_map/ppermute | solution.py:178
  84.4 15.5 %collective-permute-start.25 = (bf16[496,128]{1,0:T(8,128)(2,1)S(1)}, bf16[496,128]{1,0:T(8,128)(2,1)S(1)}, u32[]{:S(2)}, u32[]{:S(2)}) collective-permute-start(bf16[496,128]{1,0:T(8,128)(2,1)S(1)} %get-tuple-element.62), channel_id=1, source_target_pairs={{0,7},{1,6},{2,5},{3,4},{4,3},{5,2},{6,1},{7,0},{8,15},{9,14},{10,... | collective-permute-start | bytes 380936 | tf_op jit(solution)/shard_map/ppermute | solution.py:178
  93.6 12.7 %collective-permute-start.16 = (bf16[496,128]{1,0:T(8,128)(2,1)S(1)}, bf16[496,128]{1,0:T(8,128)(2,1)S(1)}, u32[]{:S(2)}, u32[]{:S(2)}) collective-permute-start(bf16[496,128]{1,0:T(8,128)(2,1)S(1)} %get-tuple-element.55), channel_id=1, source_target_pairs={{0,4},{1,5},{2,6},{3,7},{4,0},{5,1},{6,2},{7,3},{8,12},{9,13},{10,... | collective-permute-start | bytes 380936 | tf_op jit(solution)/shard_map/ppermute | solution.py:178
  93.8 12.5 %collective-permute-start.17 = (bf16[496,128]{1,0:T(8,128)(2,1)S(1)}, bf16[496,128]{1,0:T(8,128)(2,1)S(1)}, u32[]{:S(2)}, u32[]{:S(2)}) collective-permute-start(bf16[496,128]{1,0:T(8,128)(2,1)S(1)} %get-tuple-element.56), channel_id=1, source_target_pairs={{0,5},{1,4},{2,7},{3,6},{4,1},{5,0},{6,3},{7,2},{8,13},{9,12},{10,... | collective-permute-start | bytes 380936 | tf_op jit(solution)/shard_map/ppermute | solution.py:178
  96.6 9.7 %collective-permute-start.7 = (bf16[496,128]{1,0:T(8,128)(2,1)S(1)}, bf16[496,128]{1,0:T(8,128)(2,1)S(1)}, u32[]{:S(2)}, u32[]{:S(2)}) collective-permute-start(bf16[496,128]{1,0:T(8,128)(2,1)S(1)} %get-tuple-element.48), channel_id=1, source_target_pairs={{0,1},{1,0},{2,3},{3,2},{4,5},{5,4},{6,7},{7,6},{8,9},{9,8},{10,11... | collective-permute-start | bytes 380936 | tf_op jit(solution)/shard_map/ppermute | solution.py:178
  99.9 11.3 %collective-permute-start.9 = (bf16[496,128]{1,0:T(8,128)(2,1)S(1)}, bf16[496,128]{1,0:T(8,128)(2,1)S(1)}, u32[]{:S(2)}, u32[]{:S(2)}) collective-permute-start(bf16[496,128]{1,0:T(8,128)(2,1)S(1)} %get-tuple-element.50), channel_id=1, source_target_pairs={{0,3},{1,2},{2,1},{3,0},{4,7},{5,6},{6,5},{7,4},{8,11},{9,10},{10,... | collective-permute-start | bytes 380936 | tf_op jit(solution)/shard_map/ppermute | solution.py:178
  (12 other events, 52.7 us)

commit v2 on v1

v2 whole, which is shorter than its diff:
```python
import functools
import jax
import jax.numpy as jnp
from jax import lax
from jax.experimental import pallas as pl
from jax.experimental.pallas import tpu as pltpu
from jax.sharding import PartitionSpec as P

F32 = jnp.float32
BF16 = jnp.bfloat16
LANES = 128
NO_COST = pl.CostEstimate(flops=1, bytes_accessed=1, transcendentals=0)


def contract_last(matrix_a, matrix_b):
    return lax.dot_general(
        matrix_a, matrix_b, (((1,), (1,)), ((), ())), preferred_element_type=F32
    )


def contract_first(matrix_a, matrix_b):
    return lax.dot_general(
        matrix_a, matrix_b, (((0,), (0,)), ((), ())), preferred_element_type=F32
    )


def swiglu_grads(pre_gate, pre_up, back_hidden, weights):
    sigmas = jax.nn.sigmoid(pre_gate)
    active = pre_gate * sigmas
    hidden = (active * pre_up).astype(BF16)
    scaled = weights[:, None] * back_hidden
    grad_gate_pre = (scaled * pre_up * sigmas * (1.0 + pre_gate * (1.0 - sigmas))).astype(BF16)
    grad_up_pre = (scaled * active).astype(BF16)
    return (hidden, grad_gate_pre, grad_up_pre)


HBM = pltpu.MemorySpace.HBM


def slot_masks(routes, messages, capacity, experts):
    me = lax.axis_index("dp")
    tok_rows = routes.shape[1]
    row = lax.broadcasted_iota(jnp.int32, (len(messages), tok_rows), 0)
    expert = jnp.zeros((len(messages), tok_rows), jnp.int32)
    for k, (shift, flip) in enumerate(messages):
        target = lax.rem((me // 2) + shift, experts // 2) * 2 + jnp.bitwise_xor(me % 2, flip)
        expert = jnp.where(row == k, target, expert)
    first = routes[0:1, :] == expert
    second = routes[1:2, :] == expert
    named = jnp.where(first, 1.0, 0.0) + jnp.where(second, 1.0, 0.0)
    before = jnp.where(
        lax.broadcasted_iota(jnp.int32, (tok_rows, tok_rows), 0)
        < lax.broadcasted_iota(jnp.int32, (tok_rows, tok_rows), 1),
        1.0,
        0.0,
    ).astype(BF16)
    rank = jnp.dot(named.astype(BF16), before, preferred_element_type=F32).astype(jnp.int32)
    rank = jnp.where(named > 0.5, rank, -1)
    place = lax.broadcasted_iota(jnp.int32, (capacity, tok_rows), 0)
    hits = [place == rank[k : k + 1, :] for k in range(len(messages))]
    return first, second, hits


def send_kernel(messages, capacity, experts, routes_hbm, combine_hbm, tokens_hbm, cot_hbm, *refs):
    out_refs = refs[:-5]
    routes_ref, combine_ref, tokens_ref, cot_ref, sems = refs[-5:]
    pairs = (
        (routes_hbm, routes_ref),
        (combine_hbm, combine_ref),
        (tokens_hbm, tokens_ref),
        (cot_hbm, cot_ref),
    )
    copies = [pltpu.make_async_copy(a, b, sems.at[i]) for i, (a, b) in enumerate(pairs)]
    for copy in copies:
        copy.start()
    copies[0].wait()
    copies[1].wait()
    first, second, hits = slot_masks(routes_ref[...], messages, capacity, experts)
    comb = combine_ref[...].astype(F32)
    scale = jnp.where(first, comb[0:1, :], 0.0) + jnp.where(second, comb[1:2, :], 0.0)
    copies[2].wait()
    copies[3].wait()
    tokens = tokens_ref[...]
    cot = cot_ref[...]
    places = [(out, at) for out in out_refs for at in range(0, out.shape[0], 2 * capacity)]
    for k, (out, at) in enumerate(places):
        pick = jnp.where(hits[k], 1.0, 0.0).astype(BF16)
        weigh = jnp.where(hits[k], scale[k : k + 1, :], 0.0).astype(BF16)
        mid, end = at + capacity, at + 2 * capacity
        out[at:mid, :] = jnp.dot(pick, tokens, preferred_element_type=F32).astype(BF16)
        out[mid:end, :] = jnp.dot(weigh, cot, preferred_element_type=F32).astype(BF16)


def hold_kernel(*refs):
    sems = refs[-1]
    count = len(refs) // 2
    copies = [
        pltpu.make_async_copy(refs[i], refs[count + i], sems.at[i]) for i in range(count)
    ]
    for copy in copies:
        copy.start()
    for copy in copies:
        copy.wait()


def forward_kernel(blocks, capacity, tile, *refs):
    block_refs = refs[:blocks]
    weights = refs[blocks : blocks + 3]
    out_ref = refs[-1]
    tok = jnp.concatenate([ref[0:capacity, :] for ref in block_refs], axis=0)
    cot = jnp.concatenate([ref[capacity : 2 * capacity, :] for ref in block_refs], axis=0)

    def step(j, _):
        at = pl.ds(pl.multiple_of(j * tile, tile), tile)
        for i in range(3):
            if i < 2:
                part = jnp.dot(tok, weights[i][0, :, at], preferred_element_type=F32)
            else:
                part = contract_last(cot, weights[i][0, at, :])
            out_ref[i, :, at] = part.astype(BF16)
        return 0

    lax.fori_loop(0, out_ref.shape[2] // tile, step, 0)


def backward_kernel(blocks, capacity, tile, own_ref, got_ref, gate_ref, up_ref, *refs):
    out_refs = refs[-3 - blocks :]
    hid_ref, gg_ref, gu_ref = out_refs[:3]
    back_refs = out_refs[3:]
    width = gate_ref.shape[1]
    eye = lax.broadcasted_iota(jnp.int32, (capacity, LANES), 0) == lax.broadcasted_iota(
        jnp.int32, (capacity, LANES), 1
    )
    base = width // LANES * capacity
    for k in range(blocks):
        rows = slice(k * capacity, (k + 1) * capacity)
        pre_gate, pre_up, back_hidden = (
            own_ref[i, rows, :].astype(F32) + got_ref[i, rows, :].astype(F32) for i in range(3)
        )
        sigmas = jax.nn.sigmoid(pre_gate)
        active = pre_gate * sigmas
        hidden = (active * pre_up).astype(BF16)
        gg = back_hidden * pre_up * sigmas * (1.0 + pre_gate * (1.0 - sigmas))
        hid_ref[rows, :] = hidden
        gg_ref[rows, :] = gg.astype(BF16)
        gu_ref[rows, :] = (back_hidden * active).astype(BF16)
        comb = jnp.sum(hidden.astype(F32) * back_hidden, axis=1, keepdims=True)
        row = jnp.sum(jnp.where(eye, comb, 0.0), axis=0, keepdims=True)
        high = row.astype(BF16)
        low = (row - high.astype(F32)).astype(BF16)
        tail = jnp.concatenate(
            [high.astype(F32), low.astype(F32), jnp.zeros((14, LANES), F32)], axis=0
        )
        back_refs[k][base : base + 16, :] = tail.astype(BF16)
    gg, gu = gg_ref[...], gu_ref[...]
    per = tile // LANES

    def step(j, _):
        at = pl.ds(pl.multiple_of(j * tile, tile), tile)
        dx = contract_last(gg, gate_ref[0, at, :]) + contract_last(gu, up_ref[0, at, :])
        dx = dx.astype(BF16)
        start = pl.multiple_of(j * (per * capacity), per * capacity)
        for k in range(blocks):
            part = dx[k * capacity : (k + 1) * capacity, :]
            stacked = jnp.concatenate(
                [part[:, c * LANES : (c + 1) * LANES] for c in range(per)], axis=0
            )
            back_refs[k][pl.ds(start, per * capacity), :] = stacked
        return 0

    lax.fori_loop(0, width // tile, step, 0)


def weight_kernel(blocks, capacity, chunks, *refs):
    block_refs = refs[:blocks]
    hid_refs = refs[blocks : blocks + chunks]
    gg_refs = refs[blocks + chunks : blocks + 2 * chunks]
    gu_refs = refs[blocks + 2 * chunks : blocks + 3 * chunks]
    gate_ref, up_ref, down_ref = refs[blocks + 3 * chunks :]
    tok = jnp.concatenate([ref[0:capacity, :] for ref in block_refs], axis=0)
    cot = jnp.concatenate([ref[capacity : 2 * capacity, :] for ref in block_refs], axis=0)
    join = lambda part: jnp.concatenate([ref[...] for ref in part], axis=0)
    gate_ref[0] = contract_first(tok, join(gg_refs)).astype(BF16)
    up_ref[0] = contract_first(tok, join(gu_refs)).astype(BF16)
    down_ref[0] = contract_first(join(hid_refs), cot).astype(BF16)


def merge_kernel(messages, capacity, experts, early, *refs):
    routes_ref, combine_ref = refs[early : early + 2]
    back_refs = refs[early + 2 : -2]
    grad_ref, comb_ref = refs[-2:]
    first, second, hits = slot_masks(routes_ref[...], messages, capacity, experts)
    picks = [jnp.where(hit, 1.0, 0.0).astype(BF16) for hit in hits]
    pick = jnp.concatenate(picks, axis=0)
    groups = grad_ref.shape[1] // LANES
    for c in range(groups):
        piece = jnp.concatenate(
            [ref[c * capacity : (c + 1) * capacity, :] for ref in back_refs], axis=0
        )
        grad_ref[:, c * LANES : (c + 1) * LANES] = contract_first(pick, piece).astype(BF16)
    total0 = jnp.zeros((1, LANES), F32)
    total1 = total0
    for k in range(len(messages)):
        tail = back_refs[k][groups * capacity : groups * capacity + 16, :][:, :capacity]
        seen = jnp.dot(tail, picks[k], preferred_element_type=F32)
        value = seen[0:1, :] + seen[1:2, :]
        total0 = total0 + jnp.where(first[k : k + 1, :], value, 0.0)
        total1 = total1 + jnp.where(second[k : k + 1, :], value, 0.0)
    comb = combine_ref[...].astype(F32)
    comb_ref[0:1, :] = total0 / comb[0:1, :]
    comb_ref[1:2, :] = total1 / comb[1:2, :]


def crossed(value, flips):
    experts, slots = lax.axis_size("expert"), lax.axis_size("dp")
    pairs = [
        (e * slots + d, (e ^ flips[d % 2]) * slots + d)
        for e in range(experts)
        for d in range(slots)
    ]
    return lax.ppermute(value, ("expert", "dp"), pairs)


def moved(value, message, back=False):
    shift, flip = message
    size = lax.axis_size("dp")
    chips = size // 2
    pairs = [(i, (i // 2 + shift) % chips * 2 + (i % 2 ^ flip)) for i in range(size)]
    if back:
        pairs = sorted((b, a) for a, b in pairs)
    return lax.ppermute(value, "dp", pairs)


def vmem(mib):
    return pltpu.CompilerParams(vmem_limit_bytes=mib * 1024 * 1024)


def shape_of(*dims, dtype=BF16):
    return jax.ShapeDtypeStruct(dims, dtype)


def in_hbm(count):
    return [pl.BlockSpec(memory_space=HBM)] * count


def in_vmem(count):
    return [pl.BlockSpec(memory_space=pltpu.MemorySpace.VMEM)] * count


def anywhere(count):
    return [pl.BlockSpec(memory_space=pl.ANY)] * count


def run_hold(*weights):
    return pl.pallas_call(
        hold_kernel,
        in_specs=in_hbm(len(weights)),
        out_specs=in_vmem(len(weights)),
        out_shape=[shape_of(*value.shape) for value in weights],
        scratch_shapes=[pltpu.SemaphoreType.DMA((len(weights),))],
        compiler_params=vmem(16),
        cost_estimate=NO_COST,
    )(*weights)


def run_forward(blocks, capacity, weights, *earlier):
    count = len(blocks)
    _, width, hidden = weights[0].shape
    return pl.pallas_call(
        functools.partial(forward_kernel, count, capacity, 256),
        in_specs=in_vmem(count + 3) + anywhere(len(earlier)),
        out_specs=in_vmem(1)[0],
        out_shape=shape_of(3, count * capacity, hidden),
        compiler_params=vmem(24),
        cost_estimate=NO_COST,
    )(*blocks, *weights, *earlier)


def run_backward(sums, count, capacity, w_gate, w_up, *earlier):
    _, width, hidden = w_gate.shape
    rows = count * capacity
    length = width // LANES * capacity + 16
    return pl.pallas_call(
        functools.partial(backward_kernel, count, capacity, 256),
        in_specs=in_vmem(4) + anywhere(len(earlier)),
        out_specs=in_vmem(3 + count),
        out_shape=[shape_of(rows, hidden)] * 3 + [shape_of(length, LANES)] * count,
        compiler_params=vmem(24),
        cost_estimate=NO_COST,
    )(*sums, w_gate, w_up, *earlier)


def run_weights(blocks, capacity, kept, hidden):
    count, chunks = len(blocks), len(kept)
    width = blocks[0].shape[1]
    tile = 256
    column = pl.BlockSpec((2 * capacity, tile), lambda j: (0, j))
    flat = [kept[c][i] for i in range(3) for c in range(chunks)]
    held = [pl.BlockSpec(value.shape, lambda j: (0, 0)) for value in flat]
    row = pl.BlockSpec((1, tile, hidden), lambda j: (0, j, 0))
    return pl.pallas_call(
        functools.partial(weight_kernel, count, capacity, chunks),
        grid=(width // tile,),
        in_specs=[column] * count + held,
        out_specs=[row, row, pl.BlockSpec((1, hidden, tile), lambda j: (0, 0, j))],
        out_shape=[shape_of(1, width, hidden)] * 2 + [shape_of(1, hidden, width)],
        compiler_params=vmem(40),
        cost_estimate=NO_COST,
    )(*blocks, *flat)


def expert_total(part):
    got = crossed(part, (1, 2))
    pair = (part.astype(F32) + got.astype(F32)).astype(BF16)
    return pair, crossed(pair, (2, 1))


SHIFTS = (0, 1, 3, 2)
MESSAGES = tuple((shift, flip) for shift in SHIFTS for flip in (0, 1))


def exchange_body(tokens, routes, combine, cotangent, w_gate, w_up, w_down):
    tok_rows, width = tokens.shape
    top_routes = routes.shape[1]
    experts = lax.axis_size("dp")
    capacity = 3 * tok_rows * top_routes // (2 * experts)
    hidden = w_gate.shape[2]
    routes_t, combine_t = routes.T, combine.T
    chunks = len(SHIFTS)
    sends = pl.pallas_call(
        functools.partial(send_kernel, MESSAGES, capacity, experts),
        in_specs=in_hbm(4),
        out_specs=in_vmem(chunks + 1),
        out_shape=[shape_of(2 * capacity, width)] * 2
        + [shape_of(4 * capacity, width)] * (chunks - 1),
        scratch_shapes=[
            pltpu.VMEM(routes_t.shape, jnp.int32),
            pltpu.VMEM(combine_t.shape, BF16),
            pltpu.VMEM(tokens.shape, BF16),
            pltpu.VMEM(tokens.shape, BF16),
            pltpu.SemaphoreType.DMA((4,)),
        ],
        compiler_params=vmem(32),
        cost_estimate=NO_COST,
    )(routes_t, combine_t, tokens, cotangent)
    blocks = [(sends[0], moved(sends[1], (0, 1)))]
    for shift, value in zip(SHIFTS[1:], sends[2:]):
        whole = moved(value, (shift, 0))
        blocks.append((whole, moved(whole[2 * capacity :], (0, 1))))
    weights = run_hold(w_gate, w_up, w_down)
    sums, kept, backs = [], [], []

    def backward(i, *earlier):
        out = run_backward(sums[i], 2, capacity, *weights[:2], *earlier)
        kept.append(out[:3])
        for message, value in zip(MESSAGES[2 * i : 2 * i + 2], out[3:]):
            backs.append(value if message == (0, 0) else moved(value, message, back=True))

    for i, pair in enumerate(blocks):
        earlier = [done[0] for done in sums[-1:]] + [done[0] for done in kept[-1:]]
        part = run_forward(pair, capacity, weights, *earlier)
        sums.append(expert_total(part))
        if i:
            backward(i - 1, part)
    backward(chunks - 1, kept[-1][0])
    flat = [block for pair in blocks for block in pair]
    grad_gate, grad_up, grad_down = run_weights(flat, capacity, kept, hidden)
    token_grad, comb_grad = pl.pallas_call(
        functools.partial(merge_kernel, MESSAGES, capacity, experts, 0),
        in_specs=in_vmem(2 + experts),
        out_specs=in_vmem(2),
        out_shape=[shape_of(tok_rows, width), shape_of(top_routes, tok_rows, dtype=F32)],
        compiler_params=vmem(32),
        cost_estimate=NO_COST,
    )(routes_t, combine_t, *backs)
    return (token_grad, comb_grad.T, grad_gate, grad_up, grad_down)


def gather_body(tokens, routes, combine, cotangent, w_gate, w_up, w_down):
    tok_rows, slice_width = tokens.shape
    top_routes = routes.shape[1]
    experts = lax.axis_size("dp")
    capacity = 3 * tok_rows * top_routes // (2 * experts)
    route_count = tok_rows * top_routes
    slot_total = experts * capacity
    route_flat = routes.reshape(route_count)
    onehot = (route_flat[:, None] == jnp.arange(experts, dtype=jnp.int32)[None, :]).astype(
        jnp.int32
    )
    slot_rank = jnp.sum((jnp.cumsum(onehot, axis=0) - onehot) * onehot, axis=1)
    places = route_flat * capacity + slot_rank
    source = jnp.full((slot_total,), route_count, jnp.int32)
    source = source.at[places].set(jnp.arange(route_count, dtype=jnp.int32))
    blank_row = jnp.zeros((1, slice_width), BF16)
    token_send = jnp.concatenate([tokens, blank_row], axis=0)[source // top_routes]
    cot_send = jnp.concatenate([cotangent, blank_row], axis=0)[source // top_routes]
    comb_send = jnp.concatenate(
        [combine.reshape(route_count), jnp.zeros((1,), BF16)], axis=0
    )[source]
    spread = functools.partial(
        lax.all_to_all, axis_name="dp", split_axis=0, concat_axis=0, tiled=True
    )
    token_slots = spread(token_send.reshape(experts, capacity, slice_width)).reshape(
        slot_total, slice_width
    )
    cot_slots = spread(cot_send.reshape(experts, capacity, slice_width)).reshape(
        slot_total, slice_width
    )
    comb_slots = spread(comb_send.reshape(experts, capacity)).reshape(slot_total).astype(F32)
    gate_mat, up_mat, down_mat = w_gate[0], w_up[0], w_down[0]
    partials = jnp.stack(
        [
            jnp.dot(token_slots, gate_mat, preferred_element_type=F32),
            jnp.dot(token_slots, up_mat, preferred_element_type=F32),
            contract_last(cot_slots, down_mat),
        ],
        axis=1,
    )
    summed = lax.psum_scatter(
        partials.astype(BF16), "expert", scatter_dimension=2, tiled=True
    ).astype(F32)
    hidden_part, gate_part, up_part = swiglu_grads(
        summed[:, 0], summed[:, 1], summed[:, 2], comb_slots
    )
    slot_comb = jnp.sum(hidden_part.astype(F32) * summed[:, 2], axis=1)
    joined = lax.all_gather(
        jnp.stack([hidden_part, gate_part, up_part], axis=1), "expert", axis=2, tiled=True
    )
    hidden, grad_gate_pre, grad_up_pre = joined[:, 0], joined[:, 1], joined[:, 2]
    slot_dx = contract_last(grad_gate_pre, gate_mat) + contract_last(grad_up_pre, up_mat)
    scaled_dy = (comb_slots[:, None] * cot_slots.astype(F32)).astype(BF16)
    grad_gate = contract_first(token_slots, grad_gate_pre).astype(BF16)[None]
    grad_up = contract_first(token_slots, grad_up_pre).astype(BF16)[None]
    grad_down = contract_first(hidden, scaled_dy).astype(BF16)[None]
    back_dx = spread(slot_dx.reshape(experts, capacity, slice_width).astype(BF16)).astype(F32)
    back_comb = spread(slot_comb.reshape(experts, capacity).astype(BF16)).astype(F32)
    route_dx = back_dx.reshape(slot_total, slice_width)[places].reshape(
        tok_rows, top_routes, slice_width
    )
    token_grad = jnp.sum(route_dx, axis=1).astype(BF16)
    comb_part = back_comb.reshape(slot_total)[places].reshape(tok_rows, top_routes)
    combine_grad = lax.psum(comb_part, "expert")
    return (token_grad, combine_grad, grad_gate, grad_up, grad_down)


def body(tokens, routes, combine, cotangent, w_gate, w_up, w_down):
    tok_rows, width = tokens.shape
    experts = lax.axis_size("dp")
    capacity = 3 * tok_rows * routes.shape[1] // (2 * experts)
    fits = (
        experts == 8
        and lax.axis_size("expert") == 4
        and routes.shape[1] == 2
        and tok_rows == LANES
        and capacity % 16 == 0
        and width % 256 == 0
        and w_gate.shape[2] % 256 == 0
    )
    run = exchange_body if fits else gather_body
    return run(tokens, routes, combine, cotangent, w_gate, w_up, w_down)


def solution(mesh):
    in_specs = (
        P("dp", "expert"),
        P("dp", None),
        P("dp", None),
        P("dp", "expert"),
        P("dp", "expert", None),
        P("dp", "expert", None),
        P("dp", None, "expert"),
    )
    out_specs = (
        P("dp", "expert"),
        P("dp", None),
        P("dp", "expert", None),
        P("dp", "expert", None),
        P("dp", None, "expert"),
    )
    return jax.shard_map(body, mesh=mesh, in_specs=in_specs, out_specs=out_specs, check_vma=False)
```

time: 113 us -> 106 us (0.938)
  the two profiles are of different devices: /device:TPU:0 before, /device:TPU:13 now
where the time goes in v2:
time: 106 us; the launch traced here: 104 us
  waiting for transfers between devices  36.6 us (35%)
  starting transfers between devices  33.8 us (32%)
  Pallas kernels  24.4 us (23%)
  local copies, waits for them, and re-layouts  7.97 us (8%)
    ppermute x14, starting transfers between devices, moved(): return lax.ppermute(value, 'dp', pairs)  27.4 us
    ppermute x14, waiting for transfers between devices, moved(): return lax.ppermute(value, 'dp', pairs)  26.5 us
    ppermute x8, waiting for transfers between devices, crossed(): return lax.ppermute(value, ('expert', 'dp'), pairs)  10.1 us
    pallas_call x4, Pallas kernels, run_backward(): pl.pallas_call(functools.partial(backward_kernel, count, capacity, 256),...  8.89 us
    unnamed x18, local copies, waits for them, and re-layouts  7.92 us
    pallas_call x4, Pallas kernels, run_forward(): pl.pallas_call(functools.partial(forward_kernel, count, capacity, 256), i...  6.72 us
    ppermute x8, starting transfers between devices, crossed(): return lax.ppermute(value, ('expert', 'dp'), pairs)  6.47 us
    pallas_call x1, Pallas kernels, run_weights(): pl.pallas_call(functools.partial(weight_kernel, count, capacity, chunks),...  5.27 us
  transfers between devices with their start and end apart: 22, of which 6 were waited for; matrix products, arithmetic and copies ran while one was open for 0% of the time, Pallas kernels for 19%

profile of v2, /device:TPU:13, one launch (start us, length us, event | category | flops | bytes accessed | tf_op | source)
XLA Modules:
  0.0 104.0 jit_solution(14477603253079676547)
XLA Ops:
  7.2 1.5 %copy-done = bf16[1,1280,768]{2,1,0:T(8,128)(2,1)S(1)} copy-done((bf16[1,1280,768]{2,1,0:T(8,128)(2,1)S(1)}, bf16[1,1280,768]{2,1,0:T(8,128)(2,1)}, u32[]{:S(2)}) %copy-start) | copy-done | bytes 1966104
  8.7 1.5 %copy-done.1 = bf16[1,1280,768]{2,1,0:T(8,128)(2,1)S(1)} copy-done((bf16[1,1280,768]{2,1,0:T(8,128)(2,1)S(1)}, bf16[1,1280,768]{2,1,0:T(8,128)(2,1)}, u32[]{:S(2)}) %copy-start.1) | copy-done | bytes 1966104
  10.3 1.5 %copy-done.2 = bf16[1,768,1280]{2,1,0:T(8,128)(2,1)S(1)} copy-done((bf16[1,768,1280]{2,1,0:T(8,128)(2,1)S(1)}, bf16[1,768,1280]{2,1,0:T(8,128)(2,1)}, u32[]{:S(2)}) %copy-start.2) | copy-done | bytes 1966104
  12.8 1.7 %shard_map.112 = bf16[3,96,768]{2,1,0:T(8,128)(2,1)S(1)} custom-call(bf16[96,1280]{1,0:T(8,128)(2,1)S(1)} %get-tuple-element.38.refs_0_, bf16[96,1280]{1,0:T(8,128)(2,1)S(1)} %collective-permute-done.refs_1_, bf16[1,1280,768]{2,1,0:T(8,128)(2,1)S(1)} %get-tuple-element.40.refs_2_.gate_ref, bf16[1,1280,768]{2,1,0:T(8,128)(2,1)S(1)} %get-tuple-element.41.refs_3_.up_ref, ...), custom_call_target="tpu_custom_call" | custom-call | flops 1 | bytes 1 | tf_op jit(solution)/shard_map/pallas_call | solution.py:269
  14.9 3.8 %collective-permute-done.3.refs_0_.refs_2_ = bf16[192,1280]{1,0:T(8,128)(2,1)S(1)} collective-permute-done((bf16[192,1280]{1,0:T(8,128)(2,1)S(1)}, bf16[192,1280]{1,0:T(8,128)(2,1)S(1)}, u32[]{:S(2)}, u32[]{:S(2)}) %collective-permute-start.3) | collective-permute-done | bytes 491552 | tf_op jit(solution)/shard_map/ppermute | solution.py:231
  20.1 1.9 %collective-permute-done.1 = bf16[3,96,768]{2,1,0:T(8,128)(2,1)S(1)} collective-permute-done((bf16[3,96,768]{2,1,0:T(8,128)(2,1)S(1)}, bf16[3,96,768]{2,1,0:T(8,128)(2,1)S(1)}, u32[]{:S(2)}, u32[]{:S(2)}) %collective-permute-start.1) | collective-permute-done | bytes 442400 | tf_op jit(solution)/shard_map/ppermute | solution.py:221
  23.3 1.7 %shard_map.113.refs_0_ = bf16[3,96,768]{2,1,0:T(8,128)(2,1)S(1)} custom-call(bf16[192,1280]{1,0:T(8,128)(2,1)S(1)} %collective-permute-done.3.refs_0_.refs_2_, bf16[96,1280]{1,0:T(8,128)(2,1)S(1)} %collective-permute-done.4.refs_1_.refs_3_, bf16[1,1280,768]{2,1,0:T(8,128)(2,1)S(1)} %get-tuple-element.40.refs_2_.gate_ref, ...), custom_call_target="tpu_custom_call" | custom-call | flops 1 | bytes 1 | tf_op jit(solution)/shard_map/pallas_call | solution.py:269
  25.3 10.5 %collective-permute-start.14 = (bf16[192,1280]{1,0:T(8,128)(2,1)S(1)}, bf16[192,1280]{1,0:T(8,128)(2,1)S(1)}, u32[]{:S(2)}, u32[]{:S(2)}) collective-permute-start(bf16[192,1280]{1,0:T(8,128)(2,1)S(1)} %get-tuple-element.50), channel_id=1, source_target_pairs={{0,4},{1,5},{2,6},{3,7},{4,0},{5,1},{6,2},{7,3},{8,12},{9,13},{10,... | collective-permute-start | bytes 1474568 | tf_op jit(solution)/shard_map/ppermute | solution.py:231
  35.9 1.7 %collective-permute-start.9 = (bf16[96,1280]{1,0:T(8,128)(2,1)S(1)}, bf16[96,1280]{1,0:T(8,128)(2,1)S(1)}, u32[]{:S(2)}, u32[]{:S(2)}) collective-permute-start(bf16[96,1280]{1,0:T(8,128)(2,1)S(1)} %slice.13), channel_id=1, source_target_pairs={{0,1},{1,0},{2,3},{3,2},{4,5},{5,4},{6,7},{7,6},{8,9},{9,8},{10,11... | collective-permute-start | bytes 737288 | tf_op jit(solution)/shard_map/ppermute | solution.py:231
  37.6 2.2 %shard_map.114 = (bf16[96,768]{1,0:T(8,128)(2,1)S(1)}, bf16[96,768]{1,0:T(8,128)(2,1)S(1)}, bf16[96,768]{1,0:T(8,128)(2,1)S(1)}, bf16[496,128]{1,0:T(8,128)(2,1)S(1)}, bf16[496,128]{1,0:T(8,128)(2,1)S(1)}) custom-call(bf16[3,96,768]{2,1,0:T(8,128)(2,1)S(1)} %add_convert_fusion.3.refs_5_.own_ref, bf16[3,96,768]{2,1,0:T(8,128)(2,1)S(1)} %collective-permute-done.2.got_ref, ...), custom_call_target="tpu_custom_call" | custom-call | flops 1 | bytes 1 | tf_op jit(solution)/shard_map/pallas_call | solution.py:283
  40.3 1.7 %shard_map.115.refs_0_ = bf16[3,96,768]{2,1,0:T(8,128)(2,1)S(1)} custom-call(bf16[192,1280]{1,0:T(8,128)(2,1)S(1)} %collective-permute-done.8.refs_0_.refs_4_, bf16[96,1280]{1,0:T(8,128)(2,1)S(1)} %collective-permute-done.9.refs_1_.refs_5_, bf16[1,1280,768]{2,1,0:T(8,128)(2,1)S(1)} %get-tuple-element.40.refs_2_.gate_ref, ...), custom_call_target="tpu_custom_call" | custom-call | flops 1 | bytes 1 | tf_op jit(solution)/shard_map/pallas_call | solution.py:269
  42.5 14.7 %collective-permute-done.14.refs_0_.refs_6_ = bf16[192,1280]{1,0:T(8,128)(2,1)S(1)} collective-permute-done((bf16[192,1280]{1,0:T(8,128)(2,1)S(1)}, bf16[192,1280]{1,0:T(8,128)(2,1)S(1)}, u32[]{:S(2)}, u32[]{:S(2)}) %collective-permute-start.14) | collective-permute-done | bytes 491552 | tf_op jit(solution)/shard_map/ppermute | solution.py:231
  57.8 2.2 %shard_map.116 = (bf16[96,768]{1,0:T(8,128)(2,1)S(1)}, bf16[96,768]{1,0:T(8,128)(2,1)S(1)}, bf16[96,768]{1,0:T(8,128)(2,1)S(1)}, bf16[496,128]{1,0:T(8,128)(2,1)S(1)}, bf16[496,128]{1,0:T(8,128)(2,1)S(1)}) custom-call(bf16[3,96,768]{2,1,0:T(8,128)(2,1)S(1)} %add_convert_fusion.2.refs_5_.own_ref, bf16[3,96,768]{2,1,0:T(8,128)(2,1)S(1)} %collective-permute-done.7.got_ref, ...), custom_call_target="tpu_custom_call" | custom-call | flops 1 | bytes 1 | tf_op jit(solution)/shard_map/pallas_call | solution.py:283
  60.1 1.7 %shard_map.117.refs_0_ = bf16[3,96,768]{2,1,0:T(8,128)(2,1)S(1)} custom-call(bf16[192,1280]{1,0:T(8,128)(2,1)S(1)} %collective-permute-done.14.refs_0_.refs_6_, bf16[96,1280]{1,0:T(8,128)(2,1)S(1)} %collective-permute-done.15.refs_1_.refs_7_, bf16[1,1280,768]{2,1,0:T(8,128)(2,1)S(1)} %get-tuple-element.40.refs_2_.gate_ref, ...), custom_call_target="tpu_custom_call" | custom-call | flops 1 | bytes 1 | tf_op jit(solution)/shard_map/pallas_call | solution.py:269
  64.1 8.2 %collective-permute-done.18 = bf16[3,96,768]{2,1,0:T(8,128)(2,1)S(1)} collective-permute-done((bf16[3,96,768]{2,1,0:T(8,128)(2,1)S(1)}, bf16[3,96,768]{2,1,0:T(8,128)(2,1)S(1)}, u32[]{:S(2)}, u32[]{:S(2)}) %collective-permute-start.18) | collective-permute-done | bytes 442400 | tf_op jit(solution)/shard_map/ppermute | solution.py:221
  72.4 1.5 %collective-permute-start.19 = (bf16[3,96,768]{2,1,0:T(8,128)(2,1)S(1)}, bf16[3,96,768]{2,1,0:T(8,128)(2,1)S(1)}, u32[]{:S(2)}, u32[]{:S(2)}) collective-permute-start(bf16[3,96,768]{2,1,0:T(8,128)(2,1)S(1)} %add_convert_fusion.own_ref), channel_id=1, source_target_pairs={{0,16},{1,9},{2,18},{3,11},{4,20},{5,13},{6,22},{7,15},{8,24},{9,1... | collective-permute-start | bytes 1327112 | tf_op jit(solution)/shard_map/ppermute | solution.py:221
  73.9 2.5 %collective-permute-start.5 = (bf16[496,128]{1,0:T(8,128)(2,1)S(1)}, bf16[496,128]{1,0:T(8,128)(2,1)S(1)}, u32[]{:S(2)}, u32[]{:S(2)}) collective-permute-start(bf16[496,128]{1,0:T(8,128)(2,1)S(1)} %get-tuple-element.45), channel_id=1, source_target_pairs={{0,1},{1,0},{2,3},{3,2},{4,5},{5,4},{6,7},{7,6},{8,9},{9,8},{10,11... | collective-permute-start | bytes 380936 | tf_op jit(solution)/shard_map/ppermute | solution.py:231
  77.4 3.4 %collective-permute-start.11 = (bf16[496,128]{1,0:T(8,128)(2,1)S(1)}, bf16[496,128]{1,0:T(8,128)(2,1)S(1)}, u32[]{:S(2)}, u32[]{:S(2)}) collective-permute-start(bf16[496,128]{1,0:T(8,128)(2,1)S(1)} %get-tuple-element.49), channel_id=1, source_target_pairs={{0,7},{1,6},{2,1},{3,0},{4,3},{5,2},{6,5},{7,4},{8,15},{9,14},{10,... | collective-permute-start | bytes 380936 | tf_op jit(solution)/shard_map/ppermute | solution.py:231
  80.9 2.2 %shard_map.118 = (bf16[96,768]{1,0:T(8,128)(2,1)S(1)}, bf16[96,768]{1,0:T(8,128)(2,1)S(1)}, bf16[96,768]{1,0:T(8,128)(2,1)S(1)}, bf16[496,128]{1,0:T(8,128)(2,1)S(1)}, bf16[496,128]{1,0:T(8,128)(2,1)S(1)}) custom-call(bf16[3,96,768]{2,1,0:T(8,128)(2,1)S(1)} %add_convert_fusion.1.refs_5_.own_ref, bf16[3,96,768]{2,1,0:T(8,128)(2,1)S(1)} %collective-permute-done.13.got_ref, ...), custom_call_target="tpu_custom_call" | custom-call | flops 1 | bytes 1 | tf_op jit(solution)/shard_map/pallas_call | solution.py:283
  83.2 2.2 %shard_map.119 = (bf16[96,768]{1,0:T(8,128)(2,1)S(1)}, bf16[96,768]{1,0:T(8,128)(2,1)S(1)}, bf16[96,768]{1,0:T(8,128)(2,1)S(1)}, bf16[496,128]{1,0:T(8,128)(2,1)S(1)}, bf16[496,128]{1,0:T(8,128)(2,1)S(1)}) custom-call(bf16[3,96,768]{2,1,0:T(8,128)(2,1)S(1)} %add_convert_fusion.own_ref, bf16[3,96,768]{2,1,0:T(8,128)(2,1)S(1)} %collective-permute-done.19.got_ref, ...), custom_call_target="tpu_custom_call" | custom-call | flops 1 | bytes 1 | tf_op jit(solution)/shard_map/pallas_call | solution.py:283
  85.5 3.9 %collective-permute-start.20 = (bf16[496,128]{1,0:T(8,128)(2,1)S(1)}, bf16[496,128]{1,0:T(8,128)(2,1)S(1)}, u32[]{:S(2)}, u32[]{:S(2)}) collective-permute-start(bf16[496,128]{1,0:T(8,128)(2,1)S(1)} %get-tuple-element.55), channel_id=1, source_target_pairs={{0,4},{1,5},{2,6},{3,7},{4,0},{5,1},{6,2},{7,3},{8,12},{9,13},{10,... | collective-permute-start | bytes 380936 | tf_op jit(solution)/shard_map/ppermute | solution.py:231
  89.4 5.3 %shard_map.121 = (bf16[1,1280,768]{2,1,0:T(8,128)(2,1)}, bf16[1,1280,768]{2,1,0:T(8,128)(2,1)}, bf16[1,768,1280]{2,1,0:T(8,128)(2,1)}) custom-call(bf16[96,1280]{1,0:T(8,128)(2,1)S(1)} %get-tuple-element.38.refs_0_, bf16[96,1280]{1,0:T(8,128)(2,1)S(1)} %collective-permute-done.refs_1_, bf16[192,1280]{1,0:T(8,128)(2,1)S(1)} %collective-permute-done.3.refs_0_.refs_2_, ...), custom_call_target="tpu_custom_call" | custom-call | flops 1 | bytes 1 | tf_op jit(solution)/shard_map/pallas_call | solution.py:301
  94.7 5.2 %collective-permute-done.20.refs_8_ = bf16[496,128]{1,0:T(8,128)(2,1)S(1)} collective-permute-done((bf16[496,128]{1,0:T(8,128)(2,1)S(1)}, bf16[496,128]{1,0:T(8,128)(2,1)S(1)}, u32[]{:S(2)}, u32[]{:S(2)}) %collective-permute-start.20) | collective-permute-done | bytes 127008 | tf_op jit(solution)/shard_map/ppermute | solution.py:231
  100.0 2.7 %collective-permute-done.21.refs_9_ = bf16[496,128]{1,0:T(8,128)(2,1)S(1)} collective-permute-done((bf16[496,128]{1,0:T(8,128)(2,1)S(1)}, bf16[496,128]{1,0:T(8,128)(2,1)S(1)}, u32[]{:S(2)}, u32[]{:S(2)}) %collective-permute-start.21) | collective-permute-done | bytes 127008 | tf_op jit(solution)/shard_map/ppermute | solution.py:231
  (57 shorter events, 17.5 us)
Async XLA Ops:
  5.2 7.6 %collective-permute-start = (bf16[96,1280]{1,0:T(8,128)(2,1)S(1)}, bf16[96,1280]{1,0:T(8,128)(2,1)S(1)}, u32[]{:S(2)}, u32[]{:S(2)}) collective-permute-start(bf16[96,1280]{1,0:T(8,128)(2,1)S(1)} %get-tuple-element.39), channel_id=1, source_target_pairs={{0,1},{1,0},{2,3},{3,2},{4,5},{5,4},{6,7},{7,6},{8,9},{9,8},{10,11... | collective-permute-start | bytes 737288 | tf_op jit(solution)/shard_map/ppermute | solution.py:231
  5.9 12.8 %collective-permute-start.3 = (bf16[192,1280]{1,0:T(8,128)(2,1)S(1)}, bf16[192,1280]{1,0:T(8,128)(2,1)S(1)}, u32[]{:S(2)}, u32[]{:S(2)}) collective-permute-start(bf16[192,1280]{1,0:T(8,128)(2,1)S(1)} %get-tuple-element.43), channel_id=1, source_target_pairs={{0,2},{1,3},{2,4},{3,5},{4,6},{5,7},{6,0},{7,1},{8,10},{9,11},{10,... | collective-permute-start | bytes 1474568 | tf_op jit(solution)/shard_map/ppermute | solution.py:231
  14.4 7.5 %collective-permute-start.1 = (bf16[3,96,768]{2,1,0:T(8,128)(2,1)S(1)}, bf16[3,96,768]{2,1,0:T(8,128)(2,1)S(1)}, u32[]{:S(2)}, u32[]{:S(2)}) collective-permute-start(bf16[3,96,768]{2,1,0:T(8,128)(2,1)S(1)} %shard_map.112), channel_id=1, source_target_pairs={{0,8},{1,17},{2,10},{3,19},{4,12},{5,21},{6,14},{7,23},{8,0},{9,25... | collective-permute-start | bytes 1327112 | tf_op jit(solution)/shard_map/ppermute | solution.py:221
  14.7 21.1 %collective-permute-start.8 = (bf16[192,1280]{1,0:T(8,128)(2,1)S(1)}, bf16[192,1280]{1,0:T(8,128)(2,1)S(1)}, u32[]{:S(2)}, u32[]{:S(2)}) collective-permute-start(bf16[192,1280]{1,0:T(8,128)(2,1)S(1)} %get-tuple-element.46), channel_id=1, source_target_pairs={{0,6},{1,7},{2,0},{3,1},{4,2},{5,3},{6,4},{7,5},{8,14},{9,15},{10,... | collective-permute-start | bytes 1474568 | tf_op jit(solution)/shard_map/ppermute | solution.py:231
  18.7 4.6 %collective-permute-start.4 = (bf16[96,1280]{1,0:T(8,128)(2,1)S(1)}, bf16[96,1280]{1,0:T(8,128)(2,1)S(1)}, u32[]{:S(2)}, u32[]{:S(2)}) collective-permute-start(bf16[96,1280]{1,0:T(8,128)(2,1)S(1)} %slice.12), channel_id=1, source_target_pairs={{0,1},{1,0},{2,3},{3,2},{4,5},{5,4},{6,7},{7,6},{8,9},{9,8},{10,11... | collective-permute-start | bytes 737288 | tf_op jit(solution)/shard_map/ppermute | solution.py:231
  22.1 15.5 %collective-permute-start.2 = (bf16[3,96,768]{2,1,0:T(8,128)(2,1)S(1)}, bf16[3,96,768]{2,1,0:T(8,128)(2,1)S(1)}, u32[]{:S(2)}, u32[]{:S(2)}) collective-permute-start(bf16[3,96,768]{2,1,0:T(8,128)(2,1)S(1)} %add_convert_fusion.3.refs_5_.own_ref), channel_id=1, source_target_pairs={{0,16},{1,9},{2,18},{3,11},{4,20},{5,13},{6,22},{7,15},{8,24},{9,1... | collective-permute-start | bytes 1327112 | tf_op jit(solution)/shard_map/ppermute | solution.py:221
  25.0 14.8 %collective-permute-start.6 = (bf16[3,96,768]{2,1,0:T(8,128)(2,1)S(1)}, bf16[3,96,768]{2,1,0:T(8,128)(2,1)S(1)}, u32[]{:S(2)}, u32[]{:S(2)}) collective-permute-start(bf16[3,96,768]{2,1,0:T(8,128)(2,1)S(1)} %shard_map.113.refs_0_), channel_id=1, source_target_pairs={{0,8},{1,17},{2,10},{3,19},{4,12},{5,21},{6,14},{7,23},{8,0},{9,25... | collective-permute-start | bytes 1327112 | tf_op jit(solution)/shard_map/ppermute | solution.py:221
  25.3 31.9 %collective-permute-start.14 = (bf16[192,1280]{1,0:T(8,128)(2,1)S(1)}, bf16[192,1280]{1,0:T(8,128)(2,1)S(1)}, u32[]{:S(2)}, u32[]{:S(2)}) collective-permute-start(bf16[192,1280]{1,0:T(8,128)(2,1)S(1)} %get-tuple-element.50), channel_id=1, source_target_pairs={{0,4},{1,5},{2,6},{3,7},{4,0},{5,1},{6,2},{7,3},{8,12},{9,13},{10,... | collective-permute-start | bytes 1474568 | tf_op jit(solution)/shard_map/ppermute | solution.py:231
  35.9 4.4 %collective-permute-start.9 = (bf16[96,1280]{1,0:T(8,128)(2,1)S(1)}, bf16[96,1280]{1,0:T(8,128)(2,1)S(1)}, u32[]{:S(2)}, u32[]{:S(2)}) collective-permute-start(bf16[96,1280]{1,0:T(8,128)(2,1)S(1)} %slice.13), channel_id=1, source_target_pairs={{0,1},{1,0},{2,3},{3,2},{4,5},{5,4},{6,7},{7,6},{8,9},{9,8},{10,11... | collective-permute-start | bytes 737288 | tf_op jit(solution)/shard_map/ppermute | solution.py:231
  39.9 17.8 %collective-permute-start.7 = (bf16[3,96,768]{2,1,0:T(8,128)(2,1)S(1)}, bf16[3,96,768]{2,1,0:T(8,128)(2,1)S(1)}, u32[]{:S(2)}, u32[]{:S(2)}) collective-permute-start(bf16[3,96,768]{2,1,0:T(8,128)(2,1)S(1)} %add_convert_fusion.2.refs_5_.own_ref), channel_id=1, source_target_pairs={{0,16},{1,9},{2,18},{3,11},{4,20},{5,13},{6,22},{7,15},{8,24},{9,1... | collective-permute-start | bytes 1327112 | tf_op jit(solution)/shard_map/ppermute | solution.py:221
  42.0 18.1 %collective-permute-start.12 = (bf16[3,96,768]{2,1,0:T(8,128)(2,1)S(1)}, bf16[3,96,768]{2,1,0:T(8,128)(2,1)S(1)}, u32[]{:S(2)}, u32[]{:S(2)}) collective-permute-start(bf16[3,96,768]{2,1,0:T(8,128)(2,1)S(1)} %shard_map.115.refs_0_), channel_id=1, source_target_pairs={{0,8},{1,17},{2,10},{3,19},{4,12},{5,21},{6,14},{7,23},{8,0},{9,25... | collective-permute-start | bytes 1327112 | tf_op jit(solution)/shard_map/ppermute | solution.py:221
  57.2 2.9 %collective-permute-start.15 = (bf16[96,1280]{1,0:T(8,128)(2,1)S(1)}, bf16[96,1280]{1,0:T(8,128)(2,1)S(1)}, u32[]{:S(2)}, u32[]{:S(2)}) collective-permute-start(bf16[96,1280]{1,0:T(8,128)(2,1)S(1)} %slice.14), channel_id=1, source_target_pairs={{0,1},{1,0},{2,3},{3,2},{4,5},{5,4},{6,7},{7,6},{8,9},{9,8},{10,11... | collective-permute-start | bytes 737288 | tf_op jit(solution)/shard_map/ppermute | solution.py:231
  61.8 10.5 %collective-permute-start.18 = (bf16[3,96,768]{2,1,0:T(8,128)(2,1)S(1)}, bf16[3,96,768]{2,1,0:T(8,128)(2,1)S(1)}, u32[]{:S(2)}, u32[]{:S(2)}) collective-permute-start(bf16[3,96,768]{2,1,0:T(8,128)(2,1)S(1)} %shard_map.117.refs_0_), channel_id=1, source_target_pairs={{0,8},{1,17},{2,10},{3,19},{4,12},{5,21},{6,14},{7,23},{8,0},{9,25... | collective-permute-start | bytes 1327112 | tf_op jit(solution)/shard_map/ppermute | solution.py:221
  63.1 17.7 %collective-permute-start.13 = (bf16[3,96,768]{2,1,0:T(8,128)(2,1)S(1)}, bf16[3,96,768]{2,1,0:T(8,128)(2,1)S(1)}, u32[]{:S(2)}, u32[]{:S(2)}) collective-permute-start(bf16[3,96,768]{2,1,0:T(8,128)(2,1)S(1)} %add_convert_fusion.1.refs_5_.own_ref), channel_id=1, source_target_pairs={{0,16},{1,9},{2,18},{3,11},{4,20},{5,13},{6,22},{7,15},{8,24},{9,1... | collective-permute-start | bytes 1327112 | tf_op jit(solution)/shard_map/ppermute | solution.py:221
  72.4 10.7 %collective-permute-start.19 = (bf16[3,96,768]{2,1,0:T(8,128)(2,1)S(1)}, bf16[3,96,768]{2,1,0:T(8,128)(2,1)S(1)}, u32[]{:S(2)}, u32[]{:S(2)}) collective-permute-start(bf16[3,96,768]{2,1,0:T(8,128)(2,1)S(1)} %add_convert_fusion.own_ref), channel_id=1, source_target_pairs={{0,16},{1,9},{2,18},{3,11},{4,20},{5,13},{6,22},{7,15},{8,24},{9,1... | collective-permute-start | bytes 1327112 | tf_op jit(solution)/shard_map/ppermute | solution.py:221
  73.9 11.6 %collective-permute-start.5 = (bf16[496,128]{1,0:T(8,128)(2,1)S(1)}, bf16[496,128]{1,0:T(8,128)(2,1)S(1)}, u32[]{:S(2)}, u32[]{:S(2)}) collective-permute-start(bf16[496,128]{1,0:T(8,128)(2,1)S(1)} %get-tuple-element.45), channel_id=1, source_target_pairs={{0,1},{1,0},{2,3},{3,2},{4,5},{5,4},{6,7},{7,6},{8,9},{9,8},{10,11... | collective-permute-start | bytes 380936 | tf_op jit(solution)/shard_map/ppermute | solution.py:231
  76.4 13.0 %collective-permute-start.10 = (bf16[496,128]{1,0:T(8,128)(2,1)S(1)}, bf16[496,128]{1,0:T(8,128)(2,1)S(1)}, u32[]{:S(2)}, u32[]{:S(2)}) collective-permute-start(bf16[496,128]{1,0:T(8,128)(2,1)S(1)} %get-tuple-element.48), channel_id=1, source_target_pairs={{0,6},{1,7},{2,0},{3,1},{4,2},{5,3},{6,4},{7,5},{8,14},{9,15},{10,... | collective-permute-start | bytes 380936 | tf_op jit(solution)/shard_map/ppermute | solution.py:231
  77.4 17.3 %collective-permute-start.11 = (bf16[496,128]{1,0:T(8,128)(2,1)S(1)}, bf16[496,128]{1,0:T(8,128)(2,1)S(1)}, u32[]{:S(2)}, u32[]{:S(2)}) collective-permute-start(bf16[496,128]{1,0:T(8,128)(2,1)S(1)} %get-tuple-element.49), channel_id=1, source_target_pairs={{0,7},{1,6},{2,1},{3,0},{4,3},{5,2},{6,5},{7,4},{8,15},{9,14},{10,... | collective-permute-start | bytes 380936 | tf_op jit(solution)/shard_map/ppermute | solution.py:231
  83.1 11.6 %collective-permute-start.16 = (bf16[496,128]{1,0:T(8,128)(2,1)S(1)}, bf16[496,128]{1,0:T(8,128)(2,1)S(1)}, u32[]{:S(2)}, u32[]{:S(2)}) collective-permute-start(bf16[496,128]{1,0:T(8,128)(2,1)S(1)} %get-tuple-element.52), channel_id=1, source_target_pairs={{0,2},{1,3},{2,4},{3,5},{4,6},{5,7},{6,0},{7,1},{8,10},{9,11},{10,... | collective-permute-start | bytes 380936 | tf_op jit(solution)/shard_map/ppermute | solution.py:231
  83.2 11.5 %collective-permute-start.17 = (bf16[496,128]{1,0:T(8,128)(2,1)S(1)}, bf16[496,128]{1,0:T(8,128)(2,1)S(1)}, u32[]{:S(2)}, u32[]{:S(2)}) collective-permute-start(bf16[496,128]{1,0:T(8,128)(2,1)S(1)} %get-tuple-element.53), channel_id=1, source_target_pairs={{0,3},{1,2},{2,5},{3,4},{4,7},{5,6},{6,1},{7,0},{8,11},{9,10},{10,... | collective-permute-start | bytes 380936 | tf_op jit(solution)/shard_map/ppermute | solution.py:231
  85.5 14.5 %collective-permute-start.20 = (bf16[496,128]{1,0:T(8,128)(2,1)S(1)}, bf16[496,128]{1,0:T(8,128)(2,1)S(1)}, u32[]{:S(2)}, u32[]{:S(2)}) collective-permute-start(bf16[496,128]{1,0:T(8,128)(2,1)S(1)} %get-tuple-element.55), channel_id=1, source_target_pairs={{0,4},{1,5},{2,6},{3,7},{4,0},{5,1},{6,2},{7,3},{8,12},{9,13},{10,... | collective-permute-start | bytes 380936 | tf_op jit(solution)/shard_map/ppermute | solution.py:231
  89.4 13.3 %collective-permute-start.21 = (bf16[496,128]{1,0:T(8,128)(2,1)S(1)}, bf16[496,128]{1,0:T(8,128)(2,1)S(1)}, u32[]{:S(2)}, u32[]{:S(2)}) collective-permute-start(bf16[496,128]{1,0:T(8,128)(2,1)S(1)} %get-tuple-element.56), channel_id=1, source_target_pairs={{0,5},{1,4},{2,7},{3,6},{4,1},{5,0},{6,3},{7,2},{8,13},{9,12},{10,... | collective-permute-start | bytes 380936 | tf_op jit(solution)/shard_map/ppermute | solution.py:231
  89.4 13.3 %copy-start.6 = (s32[128,2]{0,1:T(2,128)S(1)}, s32[128,2]{0,1:T(2,128)}, u32[]{:S(2)}) copy-start(s32[128,2]{0,1:T(2,128)} %param.8) | copy-start | bytes 3076
  89.4 13.3 %copy-start.8 = (bf16[128,2]{0,1:T(2,128)(2,1)S(1)}, bf16[128,2]{0,1:T(2,128)(2,1)}, u32[]{:S(2)}) copy-start(bf16[128,2]{0,1:T(2,128)(2,1)} %param.9) | copy-start | bytes 1540
  (7 other events, 7.9 us)

commit v3 on v2

--- a/solution.py
+++ b/solution.py
@@ -37,13 +37,18 @@
 HBM = pltpu.MemorySpace.HBM
 
 
+def chip_after(chip, shift, chips):
+    place = (chip ^ (chip >> 1)) + shift & chips - 1
+    return place ^ (place >> 1)
+
+
 def slot_masks(routes, messages, capacity, experts):
     me = lax.axis_index("dp")
     tok_rows = routes.shape[1]
     row = lax.broadcasted_iota(jnp.int32, (len(messages), tok_rows), 0)
     expert = jnp.zeros((len(messages), tok_rows), jnp.int32)
     for k, (shift, flip) in enumerate(messages):
-        target = lax.rem((me // 2) + shift, experts // 2) * 2 + jnp.bitwise_xor(me % 2, flip)
+        target = chip_after(me // 2, shift, experts // 2) * 2 + jnp.bitwise_xor(me % 2, flip)
         expert = jnp.where(row == k, target, expert)
     first = routes[0:1, :] == expert
     second = routes[1:2, :] == expert
@@ -225,7 +230,7 @@
     shift, flip = message
     size = lax.axis_size("dp")
     chips = size // 2
-    pairs = [(i, (i // 2 + shift) % chips * 2 + (i % 2 ^ flip)) for i in range(size)]
+    pairs = [(i, chip_after(i // 2, shift, chips) * 2 + (i % 2 ^ flip)) for i in range(size)]
     if back:
         pairs = sorted((b, a) for a, b in pairs)
     return lax.ppermute(value, "dp", pairs)
@@ -245,6 +250,10 @@
 
 def in_vmem(count):
     return [pl.BlockSpec(memory_space=pltpu.MemorySpace.VMEM)] * count
+
+
+def kept_in_hbm(value):
+    return pltpu.with_memory_space_constraint(value, HBM)
 
 
 def anywhere(count):
@@ -260,7 +269,7 @@
         scratch_shapes=[pltpu.SemaphoreType.DMA((len(weights),))],
         compiler_params=vmem(16),
         cost_estimate=NO_COST,
-    )(*weights)
+    )(*map(kept_in_hbm, weights))
 
 
 def run_forward(blocks, capacity, weights, *earlier):
@@ -342,7 +351,7 @@
         ],
         compiler_params=vmem(32),
         cost_estimate=NO_COST,
-    )(routes_t, combine_t, tokens, cotangent)
+    )(*map(kept_in_hbm, (routes_t, combine_t, tokens, cotangent)))
     blocks = [(sends[0], moved(sends[1], (0, 1)))]
     for shift, value in zip(SHIFTS[1:], sends[2:]):
         whole = moved(value, (shift, 0))

time: 106 us -> 101 us (0.953); the launches traced: 104 us -> 101 us
  waiting for transfers between devices: 36.6 us -> 48.6 us
  starting transfers between devices: 33.8 us -> 23.9 us
  local copies, waits for them, and re-layouts: 7.97 us -> 0.06 us
  Pallas kernels: 24.4 us -> 26.9 us
    ppermute x14, starting transfers between devices: 27.4 us -> 16.4 us  [moved(): return lax.ppermute(value, 'dp', pairs)]
    ppermute x14, waiting for transfers between devices: 26.5 us -> 34.9 us  [moved(): return lax.ppermute(value, 'dp', pairs)]
    unnamed x18 -> x4, local copies, waits for them, and re-layouts: 7.92 us -> 0.01 us
    ppermute x8, waiting for transfers between devices: 10.1 us -> 13.7 us  [crossed(): return lax.ppermute(value, ('expert', 'dp'), pairs)]
    pallas_call x1, Pallas kernels: 0.91 us -> 2.76 us  [run_hold(): pl.pallas_call(hold_kernel, in_specs=in_hbm(len(weights)), out_specs=in_v...]
  transfers between devices with their start and end apart: 22 -> 22, of which waited for: 6 -> 7; matrix products, arithmetic and copies ran while one was open for 0% -> 0% of each run, Pallas kernels for 19% -> 22%
where the time goes in v3:
time: 101 us
  waiting for transfers between devices  48.6 us (48%)
  Pallas kernels  26.9 us (27%)
  starting transfers between devices  23.9 us (24%)
    ppermute x14, waiting for transfers between devices, moved(): return lax.ppermute(value, 'dp', pairs)  34.9 us
    ppermute x14, starting transfers between devices, moved(): return lax.ppermute(value, 'dp', pairs)  16.4 us
    ppermute x8, waiting for transfers between devices, crossed(): return lax.ppermute(value, ('expert', 'dp'), pairs)  13.7 us
    pallas_call x4, Pallas kernels, run_backward(): pl.pallas_call(functools.partial(backward_kernel, count, capacity, 256),...  8.87 us
    ppermute x8, starting transfers between devices, crossed(): return lax.ppermute(value, ('expert', 'dp'), pairs)  7.51 us
    pallas_call x4, Pallas kernels, run_forward(): pl.pallas_call(functools.partial(forward_kernel, count, capacity, 256), i...  6.72 us
    pallas_call x1, Pallas kernels, run_weights(): pl.pallas_call(functools.partial(weight_kernel, count, capacity, chunks),...  5.24 us
    pallas_call x1, Pallas kernels, run_hold(): pl.pallas_call(hold_kernel, in_specs=in_hbm(len(weights)), out_specs=in_v...  2.76 us
  transfers between devices with their start and end apart: 22, of which 7 were waited for; matrix products, arithmetic and copies ran while one was open for 0% of the time, Pallas kernels for 22%

profile of v3, /device:TPU:13, one launch (start us, length us, event | category | flops | bytes accessed | tf_op | source)
XLA Modules:
  0.0 100.7 jit_solution(10523597467206169619)
XLA Ops:
  0.6 2.0 %shard_map.110 = (bf16[96,1280]{1,0:T(8,128)(2,1)S(1)}, bf16[96,1280]{1,0:T(8,128)(2,1)S(1)}, bf16[192,1280]{1,0:T(8,128)(2,1)S(1)}, bf16[192,1280]{1,0:T(8,128)(2,1)S(1)}, bf16[192,1280]{1,0:T(8,128)(2,1)S(1)}) custom-call(s32[2,128]{1,0:T(2,128)} %bitcast.3, bf16[2,128]{1,0:T(2,128)(2,1)} %bitcast.5, bf16[128,1280]{1,0:T(8,128)(2,1)} %tokens_hbm.1, ...), custom_call_target="tpu_custom_call" | custom-call | flops 1 | bytes 1 | tf_op jit(solution)/shard_map/pallas_call | solution.py:339
  3.4 2.3 %collective-permute-start.3 = (bf16[192,1280]{1,0:T(8,128)(2,1)S(1)}, bf16[192,1280]{1,0:T(8,128)(2,1)S(1)}, u32[]{:S(2)}, u32[]{:S(2)}) collective-permute-start(bf16[192,1280]{1,0:T(8,128)(2,1)S(1)} %get-tuple-element.43), channel_id=1, source_target_pairs={{0,2},{1,3},{2,6},{3,7},{4,0},{5,1},{6,4},{7,5},{8,10},{9,11},{10,... | collective-permute-start | bytes 1474568 | tf_op jit(solution)/shard_map/ppermute | solution.py:236
  5.7 2.8 %shard_map.111 = (bf16[1,1280,768]{2,1,0:T(8,128)(2,1)S(1)}, bf16[1,1280,768]{2,1,0:T(8,128)(2,1)S(1)}, bf16[1,768,1280]{2,1,0:T(8,128)(2,1)S(1)}) custom-call(bf16[1,1280,768]{2,1,0:T(8,128)(2,1)} %refs_0_.1, bf16[1,1280,768]{2,1,0:T(8,128)(2,1)} %refs_1_.1, bf16[1,768,1280]{2,1,0:T(8,128)(2,1)} %refs_2_.1), custom_call_target="tpu_custom_call" | custom-call | flops 1 | bytes 1 | tf_op jit(solution)/shard_map/pallas_call | solution.py:264
  8.4 1.7 %shard_map.112 = bf16[3,96,768]{2,1,0:T(8,128)(2,1)S(1)} custom-call(bf16[96,1280]{1,0:T(8,128)(2,1)S(1)} %get-tuple-element.38.refs_0_, bf16[96,1280]{1,0:T(8,128)(2,1)S(1)} %collective-permute-done.refs_1_, bf16[1,1280,768]{2,1,0:T(8,128)(2,1)S(1)} %get-tuple-element.40.refs_2_.gate_ref, bf16[1,1280,768]{2,1,0:T(8,128)(2,1)S(1)} %get-tuple-element.41.refs_3_.up_ref, ...), custom_call_target="tpu_custom_call" | custom-call | flops 1 | bytes 1 | tf_op jit(solution)/shard_map/pallas_call | solution.py:278
  10.4 16.3 %collective-permute-done.3.refs_0_.refs_2_ = bf16[192,1280]{1,0:T(8,128)(2,1)S(1)} collective-permute-done((bf16[192,1280]{1,0:T(8,128)(2,1)S(1)}, bf16[192,1280]{1,0:T(8,128)(2,1)S(1)}, u32[]{:S(2)}, u32[]{:S(2)}) %collective-permute-start.3) | collective-permute-done | bytes 491552 | tf_op jit(solution)/shard_map/ppermute | solution.py:236
  29.2 1.7 %shard_map.113.refs_0_ = bf16[3,96,768]{2,1,0:T(8,128)(2,1)S(1)} custom-call(bf16[192,1280]{1,0:T(8,128)(2,1)S(1)} %collective-permute-done.3.refs_0_.refs_2_, bf16[96,1280]{1,0:T(8,128)(2,1)S(1)} %collective-permute-done.4.refs_1_.refs_3_, bf16[1,1280,768]{2,1,0:T(8,128)(2,1)S(1)} %get-tuple-element.40.refs_2_.gate_ref, ...), custom_call_target="tpu_custom_call" | custom-call | flops 1 | bytes 1 | tf_op jit(solution)/shard_map/pallas_call | solution.py:278
  32.6 3.9 %collective-permute-done.2.got_ref = bf16[3,96,768]{2,1,0:T(8,128)(2,1)S(1)} collective-permute-done((bf16[3,96,768]{2,1,0:T(8,128)(2,1)S(1)}, bf16[3,96,768]{2,1,0:T(8,128)(2,1)S(1)}, u32[]{:S(2)}, u32[]{:S(2)}) %collective-permute-start.2) | collective-permute-done | bytes 442400 | tf_op jit(solution)/shard_map/ppermute | solution.py:226
  36.5 2.2 %shard_map.114 = (bf16[96,768]{1,0:T(8,128)(2,1)S(1)}, bf16[96,768]{1,0:T(8,128)(2,1)S(1)}, bf16[96,768]{1,0:T(8,128)(2,1)S(1)}, bf16[496,128]{1,0:T(8,128)(2,1)S(1)}, bf16[496,128]{1,0:T(8,128)(2,1)S(1)}) custom-call(bf16[3,96,768]{2,1,0:T(8,128)(2,1)S(1)} %add_convert_fusion.3.refs_5_.own_ref, bf16[3,96,768]{2,1,0:T(8,128)(2,1)S(1)} %collective-permute-done.2.got_ref, ...), custom_call_target="tpu_custom_call" | custom-call | flops 1 | bytes 1 | tf_op jit(solution)/shard_map/pallas_call | solution.py:292
  38.7 1.6 %collective-permute-done.6 = bf16[3,96,768]{2,1,0:T(8,128)(2,1)S(1)} collective-permute-done((bf16[3,96,768]{2,1,0:T(8,128)(2,1)S(1)}, bf16[3,96,768]{2,1,0:T(8,128)(2,1)S(1)}, u32[]{:S(2)}, u32[]{:S(2)}) %collective-permute-start.6) | collective-permute-done | bytes 442400 | tf_op jit(solution)/shard_map/ppermute | solution.py:226
  40.4 1.6 %collective-permute-start.7 = (bf16[3,96,768]{2,1,0:T(8,128)(2,1)S(1)}, bf16[3,96,768]{2,1,0:T(8,128)(2,1)S(1)}, u32[]{:S(2)}, u32[]{:S(2)}) collective-permute-start(bf16[3,96,768]{2,1,0:T(8,128)(2,1)S(1)} %add_convert_fusion.2.refs_5_.own_ref), channel_id=1, source_target_pairs={{0,16},{1,9},{2,18},{3,11},{4,20},{5,13},{6,22},{7,15},{8,24},{9,1... | collective-permute-start | bytes 1327112 | tf_op jit(solution)/shard_map/ppermute | solution.py:226
  42.0 1.7 %shard_map.115.refs_0_ = bf16[3,96,768]{2,1,0:T(8,128)(2,1)S(1)} custom-call(bf16[192,1280]{1,0:T(8,128)(2,1)S(1)} %collective-permute-done.8.refs_0_.refs_4_, bf16[96,1280]{1,0:T(8,128)(2,1)S(1)} %collective-permute-done.9.refs_1_.refs_5_, bf16[1,1280,768]{2,1,0:T(8,128)(2,1)S(1)} %get-tuple-element.40.refs_2_.gate_ref, ...), custom_call_target="tpu_custom_call" | custom-call | flops 1 | bytes 1 | tf_op jit(solution)/shard_map/pallas_call | solution.py:278
  44.0 9.1 %collective-permute-done.14.refs_0_.refs_6_ = bf16[192,1280]{1,0:T(8,128)(2,1)S(1)} collective-permute-done((bf16[192,1280]{1,0:T(8,128)(2,1)S(1)}, bf16[192,1280]{1,0:T(8,128)(2,1)S(1)}, u32[]{:S(2)}, u32[]{:S(2)}) %collective-permute-start.14) | collective-permute-done | bytes 491552 | tf_op jit(solution)/shard_map/ppermute | solution.py:236
  53.1 2.3 %collective-permute-start.15 = (bf16[96,1280]{1,0:T(8,128)(2,1)S(1)}, bf16[96,1280]{1,0:T(8,128)(2,1)S(1)}, u32[]{:S(2)}, u32[]{:S(2)}) collective-permute-start(bf16[96,1280]{1,0:T(8,128)(2,1)S(1)} %slice.14), channel_id=1, source_target_pairs={{0,1},{1,0},{2,3},{3,2},{4,5},{5,4},{6,7},{7,6},{8,9},{9,8},{10,11... | collective-permute-start | bytes 737288 | tf_op jit(solution)/shard_map/ppermute | solution.py:236
  55.4 2.2 %shard_map.116 = (bf16[96,768]{1,0:T(8,128)(2,1)S(1)}, bf16[96,768]{1,0:T(8,128)(2,1)S(1)}, bf16[96,768]{1,0:T(8,128)(2,1)S(1)}, bf16[496,128]{1,0:T(8,128)(2,1)S(1)}, bf16[496,128]{1,0:T(8,128)(2,1)S(1)}) custom-call(bf16[3,96,768]{2,1,0:T(8,128)(2,1)S(1)} %add_convert_fusion.2.refs_5_.own_ref, bf16[3,96,768]{2,1,0:T(8,128)(2,1)S(1)} %collective-permute-done.7.got_ref, ...), custom_call_target="tpu_custom_call" | custom-call | flops 1 | bytes 1 | tf_op jit(solution)/shard_map/pallas_call | solution.py:292
  57.8 1.7 %shard_map.117.refs_0_ = bf16[3,96,768]{2,1,0:T(8,128)(2,1)S(1)} custom-call(bf16[192,1280]{1,0:T(8,128)(2,1)S(1)} %collective-permute-done.14.refs_0_.refs_6_, bf16[96,1280]{1,0:T(8,128)(2,1)S(1)} %collective-permute-done.15.refs_1_.refs_7_, bf16[1,1280,768]{2,1,0:T(8,128)(2,1)S(1)} %get-tuple-element.40.refs_2_.gate_ref, ...), custom_call_target="tpu_custom_call" | custom-call | flops 1 | bytes 1 | tf_op jit(solution)/shard_map/pallas_call | solution.py:278
  61.7 8.2 %collective-permute-done.18 = bf16[3,96,768]{2,1,0:T(8,128)(2,1)S(1)} collective-permute-done((bf16[3,96,768]{2,1,0:T(8,128)(2,1)S(1)}, bf16[3,96,768]{2,1,0:T(8,128)(2,1)S(1)}, u32[]{:S(2)}, u32[]{:S(2)}) %collective-permute-start.18) | collective-permute-done | bytes 442400 | tf_op jit(solution)/shard_map/ppermute | solution.py:226
  71.5 2.5 %collective-permute-start.5 = (bf16[496,128]{1,0:T(8,128)(2,1)S(1)}, bf16[496,128]{1,0:T(8,128)(2,1)S(1)}, u32[]{:S(2)}, u32[]{:S(2)}) collective-permute-start(bf16[496,128]{1,0:T(8,128)(2,1)S(1)} %get-tuple-element.45), channel_id=1, source_target_pairs={{0,1},{1,0},{2,3},{3,2},{4,5},{5,4},{6,7},{7,6},{8,9},{9,8},{10,11... | collective-permute-start | bytes 380936 | tf_op jit(solution)/shard_map/ppermute | solution.py:236
  75.4 2.2 %shard_map.118 = (bf16[96,768]{1,0:T(8,128)(2,1)S(1)}, bf16[96,768]{1,0:T(8,128)(2,1)S(1)}, bf16[96,768]{1,0:T(8,128)(2,1)S(1)}, bf16[496,128]{1,0:T(8,128)(2,1)S(1)}, bf16[496,128]{1,0:T(8,128)(2,1)S(1)}) custom-call(bf16[3,96,768]{2,1,0:T(8,128)(2,1)S(1)} %add_convert_fusion.1.refs_5_.own_ref, bf16[3,96,768]{2,1,0:T(8,128)(2,1)S(1)} %collective-permute-done.13.got_ref, ...), custom_call_target="tpu_custom_call" | custom-call | flops 1 | bytes 1 | tf_op jit(solution)/shard_map/pallas_call | solution.py:292
  78.7 2.0 %collective-permute-start.17 = (bf16[496,128]{1,0:T(8,128)(2,1)S(1)}, bf16[496,128]{1,0:T(8,128)(2,1)S(1)}, u32[]{:S(2)}, u32[]{:S(2)}) collective-permute-start(bf16[496,128]{1,0:T(8,128)(2,1)S(1)} %get-tuple-element.53), channel_id=1, source_target_pairs={{0,3},{1,2},{2,7},{3,6},{4,1},{5,0},{6,5},{7,4},{8,11},{9,10},{10,... | collective-permute-start | bytes 380936 | tf_op jit(solution)/shard_map/ppermute | solution.py:236
  80.7 2.2 %shard_map.119 = (bf16[96,768]{1,0:T(8,128)(2,1)S(1)}, bf16[96,768]{1,0:T(8,128)(2,1)S(1)}, bf16[96,768]{1,0:T(8,128)(2,1)S(1)}, bf16[496,128]{1,0:T(8,128)(2,1)S(1)}, bf16[496,128]{1,0:T(8,128)(2,1)S(1)}) custom-call(bf16[3,96,768]{2,1,0:T(8,128)(2,1)S(1)} %add_convert_fusion.own_ref, bf16[3,96,768]{2,1,0:T(8,128)(2,1)S(1)} %collective-permute-done.19.got_ref, ...), custom_call_target="tpu_custom_call" | custom-call | flops 1 | bytes 1 | tf_op jit(solution)/shard_map/pallas_call | solution.py:292
  83.0 1.6 %collective-permute-start.21 = (bf16[496,128]{1,0:T(8,128)(2,1)S(1)}, bf16[496,128]{1,0:T(8,128)(2,1)S(1)}, u32[]{:S(2)}, u32[]{:S(2)}) collective-permute-start(bf16[496,128]{1,0:T(8,128)(2,1)S(1)} %get-tuple-element.56), channel_id=1, source_target_pairs={{0,7},{1,6},{2,5},{3,4},{4,3},{5,2},{6,1},{7,0},{8,15},{9,14},{10,... | collective-permute-start | bytes 380936 | tf_op jit(solution)/shard_map/ppermute | solution.py:236
  84.6 5.2 %shard_map.121 = (bf16[1,1280,768]{2,1,0:T(8,128)(2,1)}, bf16[1,1280,768]{2,1,0:T(8,128)(2,1)}, bf16[1,768,1280]{2,1,0:T(8,128)(2,1)}) custom-call(bf16[96,1280]{1,0:T(8,128)(2,1)S(1)} %get-tuple-element.38.refs_0_, bf16[96,1280]{1,0:T(8,128)(2,1)S(1)} %collective-permute-done.refs_1_, bf16[192,1280]{1,0:T(8,128)(2,1)S(1)} %collective-permute-done.3.refs_0_.refs_2_, ...), custom_call_target="tpu_custom_call" | custom-call | flops 1 | bytes 1 | tf_op jit(solution)/shard_map/pallas_call | solution.py:310
  89.9 6.7 %collective-permute-done.20.refs_8_ = bf16[496,128]{1,0:T(8,128)(2,1)S(1)} collective-permute-done((bf16[496,128]{1,0:T(8,128)(2,1)S(1)}, bf16[496,128]{1,0:T(8,128)(2,1)S(1)}, u32[]{:S(2)}, u32[]{:S(2)}) %collective-permute-start.20) | collective-permute-done | bytes 127008 | tf_op jit(solution)/shard_map/ppermute | solution.py:236
  96.6 2.7 %collective-permute-done.21.refs_9_ = bf16[496,128]{1,0:T(8,128)(2,1)S(1)} collective-permute-done((bf16[496,128]{1,0:T(8,128)(2,1)S(1)}, bf16[496,128]{1,0:T(8,128)(2,1)S(1)}, u32[]{:S(2)}, u32[]{:S(2)}) %collective-permute-start.21) | collective-permute-done | bytes 127008 | tf_op jit(solution)/shard_map/ppermute | solution.py:236
  (43 shorter events, 13.5 us)
Async XLA Ops:
  2.6 5.8 %collective-permute-start = (bf16[96,1280]{1,0:T(8,128)(2,1)S(1)}, bf16[96,1280]{1,0:T(8,128)(2,1)S(1)}, u32[]{:S(2)}, u32[]{:S(2)}) collective-permute-start(bf16[96,1280]{1,0:T(8,128)(2,1)S(1)} %get-tuple-element.39), channel_id=1, source_target_pairs={{0,1},{1,0},{2,3},{3,2},{4,5},{5,4},{6,7},{7,6},{8,9},{9,8},{10,11... | collective-permute-start | bytes 737288 | tf_op jit(solution)/shard_map/ppermute | solution.py:236
  3.4 23.3 %collective-permute-start.3 = (bf16[192,1280]{1,0:T(8,128)(2,1)S(1)}, bf16[192,1280]{1,0:T(8,128)(2,1)S(1)}, u32[]{:S(2)}, u32[]{:S(2)}) collective-permute-start(bf16[192,1280]{1,0:T(8,128)(2,1)S(1)} %get-tuple-element.43), channel_id=1, source_target_pairs={{0,2},{1,3},{2,6},{3,7},{4,0},{5,1},{6,4},{7,5},{8,10},{9,11},{10,... | collective-permute-start | bytes 1474568 | tf_op jit(solution)/shard_map/ppermute | solution.py:236
  10.1 17.6 %collective-permute-start.1 = (bf16[3,96,768]{2,1,0:T(8,128)(2,1)S(1)}, bf16[3,96,768]{2,1,0:T(8,128)(2,1)S(1)}, u32[]{:S(2)}, u32[]{:S(2)}) collective-permute-start(bf16[3,96,768]{2,1,0:T(8,128)(2,1)S(1)} %shard_map.112), channel_id=1, source_target_pairs={{0,8},{1,17},{2,10},{3,19},{4,12},{5,21},{6,14},{7,23},{8,0},{9,25... | collective-permute-start | bytes 1327112 | tf_op jit(solution)/shard_map/ppermute | solution.py:226
  10.4 20.7 %collective-permute-start.8 = (bf16[192,1280]{1,0:T(8,128)(2,1)S(1)}, bf16[192,1280]{1,0:T(8,128)(2,1)S(1)}, u32[]{:S(2)}, u32[]{:S(2)}) collective-permute-start(bf16[192,1280]{1,0:T(8,128)(2,1)S(1)} %get-tuple-element.46), channel_id=1, source_target_pairs={{0,4},{1,5},{2,0},{3,1},{4,6},{5,7},{6,2},{7,3},{8,12},{9,13},{10,... | collective-permute-start | bytes 1474568 | tf_op jit(solution)/shard_map/ppermute | solution.py:236
  26.7 2.4 %collective-permute-start.4 = (bf16[96,1280]{1,0:T(8,128)(2,1)S(1)}, bf16[96,1280]{1,0:T(8,128)(2,1)S(1)}, u32[]{:S(2)}, u32[]{:S(2)}) collective-permute-start(bf16[96,1280]{1,0:T(8,128)(2,1)S(1)} %slice.12), channel_id=1, source_target_pairs={{0,1},{1,0},{2,3},{3,2},{4,5},{5,4},{6,7},{7,6},{8,9},{9,8},{10,11... | collective-permute-start | bytes 737288 | tf_op jit(solution)/shard_map/ppermute | solution.py:236
  27.9 8.6 %collective-permute-start.2 = (bf16[3,96,768]{2,1,0:T(8,128)(2,1)S(1)}, bf16[3,96,768]{2,1,0:T(8,128)(2,1)S(1)}, u32[]{:S(2)}, u32[]{:S(2)}) collective-permute-start(bf16[3,96,768]{2,1,0:T(8,128)(2,1)S(1)} %add_convert_fusion.3.refs_5_.own_ref), channel_id=1, source_target_pairs={{0,16},{1,9},{2,18},{3,11},{4,20},{5,13},{6,22},{7,15},{8,24},{9,1... | collective-permute-start | bytes 1327112 | tf_op jit(solution)/shard_map/ppermute | solution.py:226
  30.8 9.5 %collective-permute-start.6 = (bf16[3,96,768]{2,1,0:T(8,128)(2,1)S(1)}, bf16[3,96,768]{2,1,0:T(8,128)(2,1)S(1)}, u32[]{:S(2)}, u32[]{:S(2)}) collective-permute-start(bf16[3,96,768]{2,1,0:T(8,128)(2,1)S(1)} %shard_map.113.refs_0_), channel_id=1, source_target_pairs={{0,8},{1,17},{2,10},{3,19},{4,12},{5,21},{6,14},{7,23},{8,0},{9,25... | collective-permute-start | bytes 1327112 | tf_op jit(solution)/shard_map/ppermute | solution.py:226
  31.1 22.0 %collective-permute-start.14 = (bf16[192,1280]{1,0:T(8,128)(2,1)S(1)}, bf16[192,1280]{1,0:T(8,128)(2,1)S(1)}, u32[]{:S(2)}, u32[]{:S(2)}) collective-permute-start(bf16[192,1280]{1,0:T(8,128)(2,1)S(1)} %get-tuple-element.50), channel_id=1, source_target_pairs={{0,6},{1,7},{2,4},{3,5},{4,2},{5,3},{6,0},{7,1},{8,14},{9,15},{10,... | collective-permute-start | bytes 1474568 | tf_op jit(solution)/shard_map/ppermute | solution.py:236
  31.2 10.8 %collective-permute-start.9 = (bf16[96,1280]{1,0:T(8,128)(2,1)S(1)}, bf16[96,1280]{1,0:T(8,128)(2,1)S(1)}, u32[]{:S(2)}, u32[]{:S(2)}) collective-permute-start(bf16[96,1280]{1,0:T(8,128)(2,1)S(1)} %slice.13), channel_id=1, source_target_pairs={{0,1},{1,0},{2,3},{3,2},{4,5},{5,4},{6,7},{7,6},{8,9},{9,8},{10,11... | collective-permute-start | bytes 737288 | tf_op jit(solution)/shard_map/ppermute | solution.py:236
  40.4 15.0 %collective-permute-start.7 = (bf16[3,96,768]{2,1,0:T(8,128)(2,1)S(1)}, bf16[3,96,768]{2,1,0:T(8,128)(2,1)S(1)}, u32[]{:S(2)}, u32[]{:S(2)}) collective-permute-start(bf16[3,96,768]{2,1,0:T(8,128)(2,1)S(1)} %add_convert_fusion.2.refs_5_.own_ref), channel_id=1, source_target_pairs={{0,16},{1,9},{2,18},{3,11},{4,20},{5,13},{6,22},{7,15},{8,24},{9,1... | collective-permute-start | bytes 1327112 | tf_op jit(solution)/shard_map/ppermute | solution.py:226
  43.7 13.9 %collective-permute-start.12 = (bf16[3,96,768]{2,1,0:T(8,128)(2,1)S(1)}, bf16[3,96,768]{2,1,0:T(8,128)(2,1)S(1)}, u32[]{:S(2)}, u32[]{:S(2)}) collective-permute-start(bf16[3,96,768]{2,1,0:T(8,128)(2,1)S(1)} %shard_map.115.refs_0_), channel_id=1, source_target_pairs={{0,8},{1,17},{2,10},{3,19},{4,12},{5,21},{6,14},{7,23},{8,0},{9,25... | collective-permute-start | bytes 1327112 | tf_op jit(solution)/shard_map/ppermute | solution.py:226
  53.1 4.6 %collective-permute-start.15 = (bf16[96,1280]{1,0:T(8,128)(2,1)S(1)}, bf16[96,1280]{1,0:T(8,128)(2,1)S(1)}, u32[]{:S(2)}, u32[]{:S(2)}) collective-permute-start(bf16[96,1280]{1,0:T(8,128)(2,1)S(1)} %slice.14), channel_id=1, source_target_pairs={{0,1},{1,0},{2,3},{3,2},{4,5},{5,4},{6,7},{7,6},{8,9},{9,8},{10,11... | collective-permute-start | bytes 737288 | tf_op jit(solution)/shard_map/ppermute | solution.py:236
  59.4 10.5 %collective-permute-start.18 = (bf16[3,96,768]{2,1,0:T(8,128)(2,1)S(1)}, bf16[3,96,768]{2,1,0:T(8,128)(2,1)S(1)}, u32[]{:S(2)}, u32[]{:S(2)}) collective-permute-start(bf16[3,96,768]{2,1,0:T(8,128)(2,1)S(1)} %shard_map.117.refs_0_), channel_id=1, source_target_pairs={{0,8},{1,17},{2,10},{3,19},{4,12},{5,21},{6,14},{7,23},{8,0},{9,25... | collective-permute-start | bytes 1327112 | tf_op jit(solution)/shard_map/ppermute | solution.py:226
  60.8 14.6 %collective-permute-start.13 = (bf16[3,96,768]{2,1,0:T(8,128)(2,1)S(1)}, bf16[3,96,768]{2,1,0:T(8,128)(2,1)S(1)}, u32[]{:S(2)}, u32[]{:S(2)}) collective-permute-start(bf16[3,96,768]{2,1,0:T(8,128)(2,1)S(1)} %add_convert_fusion.1.refs_5_.own_ref), channel_id=1, source_target_pairs={{0,16},{1,9},{2,18},{3,11},{4,20},{5,13},{6,22},{7,15},{8,24},{9,1... | collective-permute-start | bytes 1327112 | tf_op jit(solution)/shard_map/ppermute | solution.py:226
  70.0 8.7 %collective-permute-start.19 = (bf16[3,96,768]{2,1,0:T(8,128)(2,1)S(1)}, bf16[3,96,768]{2,1,0:T(8,128)(2,1)S(1)}, u32[]{:S(2)}, u32[]{:S(2)}) collective-permute-start(bf16[3,96,768]{2,1,0:T(8,128)(2,1)S(1)} %add_convert_fusion.own_ref), channel_id=1, source_target_pairs={{0,16},{1,9},{2,18},{3,11},{4,20},{5,13},{6,22},{7,15},{8,24},{9,1... | collective-permute-start | bytes 1327112 | tf_op jit(solution)/shard_map/ppermute | solution.py:226
  71.5 11.4 %collective-permute-start.5 = (bf16[496,128]{1,0:T(8,128)(2,1)S(1)}, bf16[496,128]{1,0:T(8,128)(2,1)S(1)}, u32[]{:S(2)}, u32[]{:S(2)}) collective-permute-start(bf16[496,128]{1,0:T(8,128)(2,1)S(1)} %get-tuple-element.45), channel_id=1, source_target_pairs={{0,1},{1,0},{2,3},{3,2},{4,5},{5,4},{6,7},{7,6},{8,9},{9,8},{10,11... | collective-permute-start | bytes 380936 | tf_op jit(solution)/shard_map/ppermute | solution.py:236
  74.0 9.0 %collective-permute-start.10 = (bf16[496,128]{1,0:T(8,128)(2,1)S(1)}, bf16[496,128]{1,0:T(8,128)(2,1)S(1)}, u32[]{:S(2)}, u32[]{:S(2)}) collective-permute-start(bf16[496,128]{1,0:T(8,128)(2,1)S(1)} %get-tuple-element.48), channel_id=1, source_target_pairs={{0,4},{1,5},{2,0},{3,1},{4,6},{5,7},{6,2},{7,3},{8,12},{9,13},{10,... | collective-permute-start | bytes 380936 | tf_op jit(solution)/shard_map/ppermute | solution.py:236
  74.0 15.9 %collective-permute-start.11 = (bf16[496,128]{1,0:T(8,128)(2,1)S(1)}, bf16[496,128]{1,0:T(8,128)(2,1)S(1)}, u32[]{:S(2)}, u32[]{:S(2)}) collective-permute-start(bf16[496,128]{1,0:T(8,128)(2,1)S(1)} %get-tuple-element.49), channel_id=1, source_target_pairs={{0,5},{1,4},{2,1},{3,0},{4,7},{5,6},{6,3},{7,2},{8,13},{9,12},{10,... | collective-permute-start | bytes 380936 | tf_op jit(solution)/shard_map/ppermute | solution.py:236
  77.6 12.3 %collective-permute-start.16 = (bf16[496,128]{1,0:T(8,128)(2,1)S(1)}, bf16[496,128]{1,0:T(8,128)(2,1)S(1)}, u32[]{:S(2)}, u32[]{:S(2)}) collective-permute-start(bf16[496,128]{1,0:T(8,128)(2,1)S(1)} %get-tuple-element.52), channel_id=1, source_target_pairs={{0,2},{1,3},{2,6},{3,7},{4,0},{5,1},{6,4},{7,5},{8,10},{9,11},{10,... | collective-permute-start | bytes 380936 | tf_op jit(solution)/shard_map/ppermute | solution.py:236
  78.7 11.2 %collective-permute-start.17 = (bf16[496,128]{1,0:T(8,128)(2,1)S(1)}, bf16[496,128]{1,0:T(8,128)(2,1)S(1)}, u32[]{:S(2)}, u32[]{:S(2)}) collective-permute-start(bf16[496,128]{1,0:T(8,128)(2,1)S(1)} %get-tuple-element.53), channel_id=1, source_target_pairs={{0,3},{1,2},{2,7},{3,6},{4,1},{5,0},{6,5},{7,4},{8,11},{9,10},{10,... | collective-permute-start | bytes 380936 | tf_op jit(solution)/shard_map/ppermute | solution.py:236
  82.9 13.7 %collective-permute-start.20 = (bf16[496,128]{1,0:T(8,128)(2,1)S(1)}, bf16[496,128]{1,0:T(8,128)(2,1)S(1)}, u32[]{:S(2)}, u32[]{:S(2)}) collective-permute-start(bf16[496,128]{1,0:T(8,128)(2,1)S(1)} %get-tuple-element.55), channel_id=1, source_target_pairs={{0,6},{1,7},{2,4},{3,5},{4,2},{5,3},{6,0},{7,1},{8,14},{9,15},{10,... | collective-permute-start | bytes 380936 | tf_op jit(solution)/shard_map/ppermute | solution.py:236
  83.0 16.3 %collective-permute-start.21 = (bf16[496,128]{1,0:T(8,128)(2,1)S(1)}, bf16[496,128]{1,0:T(8,128)(2,1)S(1)}, u32[]{:S(2)}, u32[]{:S(2)}) collective-permute-start(bf16[496,128]{1,0:T(8,128)(2,1)S(1)} %get-tuple-element.56), channel_id=1, source_target_pairs={{0,7},{1,6},{2,5},{3,4},{4,3},{5,2},{6,1},{7,0},{8,15},{9,14},{10,... | collective-permute-start | bytes 380936 | tf_op jit(solution)/shard_map/ppermute | solution.py:236
  84.6 14.7 %copy-start = (s32[128,2]{0,1:T(2,128)S(1)}, s32[128,2]{0,1:T(2,128)}, u32[]{:S(2)}) copy-start(s32[128,2]{0,1:T(2,128)} %param.8) | copy-start | bytes 3076
  84.6 14.7 %copy-start.1 = (bf16[128,2]{0,1:T(2,128)(2,1)S(1)}, bf16[128,2]{0,1:T(2,128)(2,1)}, u32[]{:S(2)}) copy-start(bf16[128,2]{0,1:T(2,128)(2,1)} %param.9) | copy-start | bytes 1540

commit v4 on v3

--- a/solution.py
+++ b/solution.py
@@ -106,6 +106,10 @@
         copy.start()
     for copy in copies:
         copy.wait()
+
+
+def relay_kernel(rows, whole_ref, *refs):
+    refs[-1][...] = whole_ref[rows:, :]
 
 
 def forward_kernel(blocks, capacity, tile, *refs):
@@ -181,7 +185,7 @@
     hid_refs = refs[blocks : blocks + chunks]
     gg_refs = refs[blocks + chunks : blocks + 2 * chunks]
     gu_refs = refs[blocks + 2 * chunks : blocks + 3 * chunks]
-    gate_ref, up_ref, down_ref = refs[blocks + 3 * chunks :]
+    gate_ref, up_ref, down_ref = refs[-3:]
     tok = jnp.concatenate([ref[0:capacity, :] for ref in block_refs], axis=0)
     cot = jnp.concatenate([ref[capacity : 2 * capacity, :] for ref in block_refs], axis=0)
     join = lambda part: jnp.concatenate([ref[...] for ref in part], axis=0)
@@ -272,6 +276,18 @@
     )(*map(kept_in_hbm, weights))
 
 
+def run_relay(whole, *earlier):
+    rows, width = whole.shape[0] // 2, whole.shape[1]
+    return pl.pallas_call(
+        functools.partial(relay_kernel, rows),
+        in_specs=in_vmem(1) + anywhere(len(earlier)),
+        out_specs=in_vmem(1)[0],
+        out_shape=shape_of(rows, width),
+        compiler_params=vmem(16),
+        cost_estimate=NO_COST,
+    )(whole, *earlier)
+
+
 def run_forward(blocks, capacity, weights, *earlier):
     count = len(blocks)
     _, width, hidden = weights[0].shape
@@ -299,7 +315,7 @@
     )(*sums, w_gate, w_up, *earlier)
 
 
-def run_weights(blocks, capacity, kept, hidden):
+def run_weights(blocks, capacity, kept, hidden, *earlier):
     count, chunks = len(blocks), len(kept)
     width = blocks[0].shape[1]
     tile = 256
@@ -310,22 +326,28 @@
     return pl.pallas_call(
         functools.partial(weight_kernel, count, capacity, chunks),
         grid=(width // tile,),
-        in_specs=[column] * count + held,
+        in_specs=[column] * count + held + anywhere(len(earlier)),
         out_specs=[row, row, pl.BlockSpec((1, hidden, tile), lambda j: (0, 0, j))],
         out_shape=[shape_of(1, width, hidden)] * 2 + [shape_of(1, hidden, width)],
         compiler_params=vmem(40),
         cost_estimate=NO_COST,
-    )(*blocks, *flat)
-
-
-def expert_total(part):
+    )(*blocks, *flat, *earlier)
+
+
+def expert_total(part, *earlier):
     got = crossed(part, (1, 2))
+    if earlier:
+        got = lax.optimization_barrier((got, *earlier))[0]
     pair = (part.astype(F32) + got.astype(F32)).astype(BF16)
     return pair, crossed(pair, (2, 1))
 
 
-SHIFTS = (0, 1, 3, 2)
+SHIFTS = (0, 3, 1, 2)
 MESSAGES = tuple((shift, flip) for shift in SHIFTS for flip in (0, 1))
+
+
+def after(value, *others):
+    return lax.optimization_barrier((value, *others))[0]
 
 
 def exchange_body(tokens, routes, combine, cotangent, w_gate, w_up, w_down):
@@ -352,12 +374,21 @@
         compiler_params=vmem(32),
         cost_estimate=NO_COST,
     )(*map(kept_in_hbm, (routes_t, combine_t, tokens, cotangent)))
-    blocks = [(sends[0], moved(sends[1], (0, 1)))]
+    weights = run_hold(w_gate, w_up, w_down)
+    wholes = [sends[0]]
     for shift, value in zip(SHIFTS[1:], sends[2:]):
-        whole = moved(value, (shift, 0))
-        blocks.append((whole, moved(whole[2 * capacity :], (0, 1))))
-    weights = run_hold(w_gate, w_up, w_down)
-    sums, kept, backs = [], [], []
+        wholes.append(moved(value, (shift, 0)))
+    blocks, parts, sums, kept, backs = [], [], [], [], []
+
+    def receive(i, *earlier):
+        other = run_relay(wholes[i], *earlier) if i else sends[1]
+        blocks.append((wholes[i], moved(other, (0, 1))))
+
+    def forward(i, *earlier):
+        parts.append(run_forward(blocks[i], capacity, weights, *earlier))
+
+    def exchange(i, *earlier):
+        sums.append(expert_total(parts[i], *earlier))
 
     def backward(i, *earlier):
         out = run_backward(sums[i], 2, capacity, *weights[:2], *earlier)
@@ -365,13 +396,22 @@
         for message, value in zip(MESSAGES[2 * i : 2 * i + 2], out[3:]):
             backs.append(value if message == (0, 0) else moved(value, message, back=True))
 
-    for i, pair in enumerate(blocks):
-        earlier = [done[0] for done in sums[-1:]] + [done[0] for done in kept[-1:]]
-        part = run_forward(pair, capacity, weights, *earlier)
-        sums.append(expert_total(part))
-        if i:
-            backward(i - 1, part)
-    backward(chunks - 1, kept[-1][0])
+    receive(0)
+    receive(1)
+    receive(2)
+    forward(0)
+    exchange(0)
+    forward(1, sums[0][0])
+    exchange(1)
+    backward(0, parts[1])
+    forward(2, sums[1][0], kept[0][0])
+    exchange(2)
+    backward(1, parts[2])
+    receive(3, kept[1][0])
+    forward(3, sums[2][0], kept[1][0])
+    backward(2, parts[3])
+    exchange(3, *backs[2:4], kept[2][0])
+    backward(3, kept[2][0])
     flat = [block for pair in blocks for block in pair]
     grad_gate, grad_up, grad_down = run_weights(flat, capacity, kept, hidden)
     token_grad, comb_grad = pl.pallas_call(

time: 101 us -> 86.9 us (0.86)
  waiting for transfers between devices: 48.6 us -> 32.6 us
  starting transfers between devices: 23.9 us -> 25.9 us
    ppermute x14, waiting for transfers between devices: 34.9 us -> 24.3 us  [moved(): return lax.ppermute(value, 'dp', pairs)]
    ppermute x8, waiting for transfers between devices: 13.7 us -> 8.38 us  [crossed(): return lax.ppermute(value, ('expert', 'dp'), pairs)]
    ppermute x14, starting transfers between devices: 16.4 us -> 18 us  [moved(): return lax.ppermute(value, 'dp', pairs)]
  transfers between devices with their start and end apart: 22 -> 22, of which waited for: 7 -> 12; matrix products, arithmetic and copies ran while one was open for 0% -> 0% of each run, Pallas kernels for 22% -> 27%
where the time goes in v4:
time: 86.9 us; the launch traced here: 86.7 us
  waiting for transfers between devices  32.6 us (38%)
  Pallas kernels  27 us (31%)
  starting transfers between devices  25.9 us (30%)
    ppermute x14, waiting for transfers between devices, moved(): return lax.ppermute(value, 'dp', pairs)  24.3 us
    ppermute x14, starting transfers between devices, moved(): return lax.ppermute(value, 'dp', pairs)  18 us
    pallas_call x4, Pallas kernels, run_backward(): pl.pallas_call(functools.partial(backward_kernel, count, capacity, 256),...  8.88 us
    ppermute x8, waiting for transfers between devices, crossed(): return lax.ppermute(value, ('expert', 'dp'), pairs)  8.38 us
    ppermute x8, starting transfers between devices, crossed(): return lax.ppermute(value, ('expert', 'dp'), pairs)  7.9 us
    pallas_call x4, Pallas kernels, run_forward(): pl.pallas_call(functools.partial(forward_kernel, count, capacity, 256), i...  6.72 us
    pallas_call x1, Pallas kernels, run_weights(): pl.pallas_call(functools.partial(weight_kernel, count, capacity, chunks),...  5.23 us
    pallas_call x1, Pallas kernels, run_hold(): pl.pallas_call(hold_kernel, in_specs=in_hbm(len(weights)), out_specs=in_v...  2.76 us
  transfers between devices with their start and end apart: 22, of which 12 were waited for; matrix products, arithmetic and copies ran while one was open for 0% of the time, Pallas kernels for 27%

profile of v4, /device:TPU:13, one launch (start us, length us, event | category | flops | bytes accessed | tf_op | source)
XLA Modules:
  0.0 86.7 jit_solution(3228672264459003496)
XLA Ops:
  0.6 2.0 %shard_map.110 = (bf16[96,1280]{1,0:T(8,128)(2,1)S(1)}, bf16[96,1280]{1,0:T(8,128)(2,1)S(1)}, bf16[192,1280]{1,0:T(8,128)(2,1)S(1)}, bf16[192,1280]{1,0:T(8,128)(2,1)S(1)}, bf16[192,1280]{1,0:T(8,128)(2,1)S(1)}) custom-call(s32[2,128]{1,0:T(2,128)} %bitcast.3, bf16[2,128]{1,0:T(2,128)(2,1)} %bitcast.5, bf16[128,1280]{1,0:T(8,128)(2,1)} %tokens_hbm.1, ...), custom_call_target="tpu_custom_call" | custom-call | flops 1 | bytes 1 | tf_op jit(solution)/shard_map/pallas_call | solution.py:361
  3.5 2.8 %shard_map.111 = (bf16[1,1280,768]{2,1,0:T(8,128)(2,1)S(1)}, bf16[1,1280,768]{2,1,0:T(8,128)(2,1)S(1)}, bf16[1,768,1280]{2,1,0:T(8,128)(2,1)S(1)}) custom-call(bf16[1,1280,768]{2,1,0:T(8,128)(2,1)} %refs_0_.1, bf16[1,1280,768]{2,1,0:T(8,128)(2,1)} %refs_1_.1, bf16[1,768,1280]{2,1,0:T(8,128)(2,1)} %refs_2_.1), custom_call_target="tpu_custom_call" | custom-call | flops 1 | bytes 1 | tf_op jit(solution)/shard_map/pallas_call | solution.py:268
  6.3 1.7 %shard_map.112 = bf16[3,96,768]{2,1,0:T(8,128)(2,1)S(1)} custom-call(bf16[96,1280]{1,0:T(8,128)(2,1)S(1)} %get-tuple-element.39.refs_0_, bf16[96,1280]{1,0:T(8,128)(2,1)S(1)} %collective-permute-done.refs_1_, bf16[1,1280,768]{2,1,0:T(8,128)(2,1)S(1)} %get-tuple-element.41.refs_2_.gate_ref, bf16[1,1280,768]{2,1,0:T(8,128)(2,1)S(1)} %get-tuple-element.42.refs_3_.up_ref, ...), custom_call_target="tpu_custom_call" | custom-call | flops 1 | bytes 1 | tf_op jit(solution)/shard_map/pallas_call | solution.py:294
  8.1 2.4 %collective-permute-start.8 = (bf16[192,1280]{1,0:T(8,128)(2,1)S(1)}, bf16[192,1280]{1,0:T(8,128)(2,1)S(1)}, u32[]{:S(2)}, u32[]{:S(2)}) collective-permute-start(bf16[192,1280]{1,0:T(8,128)(2,1)S(1)} %get-tuple-element.47), channel_id=1, source_target_pairs={{0,2},{1,3},{2,6},{3,7},{4,0},{5,1},{6,4},{7,5},{8,10},{9,11},{10,... | collective-permute-start | bytes 1474568 | tf_op jit(solution)/shard_map/ppermute | solution.py:240
  10.5 6.6 %collective-permute-done.3.whole_ref.refs_0_.refs_2_ = bf16[192,1280]{1,0:T(8,128)(2,1)S(1)} collective-permute-done((bf16[192,1280]{1,0:T(8,128)(2,1)S(1)}, bf16[192,1280]{1,0:T(8,128)(2,1)S(1)}, u32[]{:S(2)}, u32[]{:S(2)}) %collective-permute-start.3) | collective-permute-done | bytes 491552 | tf_op jit(solution)/shard_map/ppermute | solution.py:240
  17.1 1.4 %collective-permute-start.4 = (bf16[96,1280]{1,0:T(8,128)(2,1)S(1)}, bf16[96,1280]{1,0:T(8,128)(2,1)S(1)}, u32[]{:S(2)}, u32[]{:S(2)}) collective-permute-start(bf16[96,1280]{1,0:T(8,128)(2,1)S(1)} %shard_map.113), channel_id=1, source_target_pairs={{0,1},{1,0},{2,3},{3,2},{4,5},{5,4},{6,7},{7,6},{8,9},{9,8},{10,11... | collective-permute-start | bytes 737288 | tf_op jit(solution)/shard_map/ppermute | solution.py:240
  19.6 1.7 %shard_map.114.refs_0_ = bf16[3,96,768]{2,1,0:T(8,128)(2,1)S(1)} custom-call(bf16[192,1280]{1,0:T(8,128)(2,1)S(1)} %collective-permute-done.3.whole_ref.refs_0_.refs_2_, bf16[96,1280]{1,0:T(8,128)(2,1)S(1)} %collective-permute-done.4.refs_1_.refs_3_, bf16[1,1280,768]{2,1,0:T(8,128)(2,1)S(1)} %get-tuple-element.41.refs_2_.gate_ref, ...), custom_call_target="tpu_custom_call" | custom-call | flops 1 | bytes 1 | tf_op jit(solution)/shard_map/pallas_call | solution.py:294
  24.1 3.6 %collective-permute-done.8.whole_ref.refs_0_.refs_4_ = bf16[192,1280]{1,0:T(8,128)(2,1)S(1)} collective-permute-done((bf16[192,1280]{1,0:T(8,128)(2,1)S(1)}, bf16[192,1280]{1,0:T(8,128)(2,1)S(1)}, u32[]{:S(2)}, u32[]{:S(2)}) %collective-permute-start.8) | collective-permute-done | bytes 491552 | tf_op jit(solution)/shard_map/ppermute | solution.py:240
  29.1 2.0 %collective-permute-done.6 = bf16[3,96,768]{2,1,0:T(8,128)(2,1)S(1)} collective-permute-done((bf16[3,96,768]{2,1,0:T(8,128)(2,1)S(1)}, bf16[3,96,768]{2,1,0:T(8,128)(2,1)S(1)}, u32[]{:S(2)}, u32[]{:S(2)}) %collective-permute-start.6) | collective-permute-done | bytes 442400 | tf_op jit(solution)/shard_map/ppermute | solution.py:230
  31.3 2.3 %collective-permute-start.7 = (bf16[3,96,768]{2,1,0:T(8,128)(2,1)S(1)}, bf16[3,96,768]{2,1,0:T(8,128)(2,1)S(1)}, u32[]{:S(2)}, u32[]{:S(2)}) collective-permute-start(bf16[3,96,768]{2,1,0:T(8,128)(2,1)S(1)} %add_convert_fusion.2.refs_5_.own_ref), channel_id=1, source_target_pairs={{0,16},{1,9},{2,18},{3,11},{4,20},{5,13},{6,22},{7,15},{8,24},{9,1... | collective-permute-start | bytes 1327112 | tf_op jit(solution)/shard_map/ppermute | solution.py:230
  33.5 2.2 %shard_map.115 = (bf16[96,768]{1,0:T(8,128)(2,1)S(1)}, bf16[96,768]{1,0:T(8,128)(2,1)S(1)}, bf16[96,768]{1,0:T(8,128)(2,1)S(1)}, bf16[496,128]{1,0:T(8,128)(2,1)S(1)}, bf16[496,128]{1,0:T(8,128)(2,1)S(1)}) custom-call(bf16[3,96,768]{2,1,0:T(8,128)(2,1)S(1)} %add_convert_fusion.3.refs_5_.own_ref, bf16[3,96,768]{2,1,0:T(8,128)(2,1)S(1)} %collective-permute-done.2.got_ref, ...), custom_call_target="tpu_custom_call" | custom-call | flops 1 | bytes 1 | tf_op jit(solution)/shard_map/pallas_call | solution.py:308
  35.7 1.7 %shard_map.117.refs_0_ = bf16[3,96,768]{2,1,0:T(8,128)(2,1)S(1)} custom-call(bf16[192,1280]{1,0:T(8,128)(2,1)S(1)} %collective-permute-done.8.whole_ref.refs_0_.refs_4_, bf16[96,1280]{1,0:T(8,128)(2,1)S(1)} %collective-permute-done.9.refs_1_.refs_5_, bf16[1,1280,768]{2,1,0:T(8,128)(2,1)S(1)} %get-tuple-element.41.refs_2_.gate_ref, ...), custom_call_target="tpu_custom_call" | custom-call | flops 1 | bytes 1 | tf_op jit(solution)/shard_map/pallas_call | solution.py:294
  39.5 2.2 %shard_map.118 = (bf16[96,768]{1,0:T(8,128)(2,1)S(1)}, bf16[96,768]{1,0:T(8,128)(2,1)S(1)}, bf16[96,768]{1,0:T(8,128)(2,1)S(1)}, bf16[496,128]{1,0:T(8,128)(2,1)S(1)}, bf16[496,128]{1,0:T(8,128)(2,1)S(1)}) custom-call(bf16[3,96,768]{2,1,0:T(8,128)(2,1)S(1)} %add_convert_fusion.2.refs_5_.own_ref, bf16[3,96,768]{2,1,0:T(8,128)(2,1)S(1)} %collective-permute-done.7.got_ref, ...), custom_call_target="tpu_custom_call" | custom-call | flops 1 | bytes 1 | tf_op jit(solution)/shard_map/pallas_call | solution.py:308
  41.7 7.3 %collective-permute-done.14.whole_ref.refs_0_.refs_6_ = bf16[192,1280]{1,0:T(8,128)(2,1)S(1)} collective-permute-done((bf16[192,1280]{1,0:T(8,128)(2,1)S(1)}, bf16[192,1280]{1,0:T(8,128)(2,1)S(1)}, u32[]{:S(2)}, u32[]{:S(2)}) %collective-permute-start.14) | collective-permute-done | bytes 491552 | tf_op jit(solution)/shard_map/ppermute | solution.py:240
  51.0 1.7 %shard_map.120.refs_0_ = bf16[3,96,768]{2,1,0:T(8,128)(2,1)S(1)} custom-call(bf16[192,1280]{1,0:T(8,128)(2,1)S(1)} %collective-permute-done.14.whole_ref.refs_0_.refs_6_, bf16[96,1280]{1,0:T(8,128)(2,1)S(1)} %collective-permute-done.15.refs_1_.refs_7_, bf16[1,1280,768]{2,1,0:T(8,128)(2,1)S(1)} %get-tuple-element.41.refs_2_.gate_ref, ...), custom_call_target="tpu_custom_call" | custom-call | flops 1 | bytes 1 | tf_op jit(solution)/shard_map/pallas_call | solution.py:294
  53.0 4.0 %collective-permute-start.11 = (bf16[496,128]{1,0:T(8,128)(2,1)S(1)}, bf16[496,128]{1,0:T(8,128)(2,1)S(1)}, u32[]{:S(2)}, u32[]{:S(2)}) collective-permute-start(bf16[496,128]{1,0:T(8,128)(2,1)S(1)} %get-tuple-element.50), channel_id=1, source_target_pairs={{0,3},{1,2},{2,7},{3,6},{4,1},{5,0},{6,5},{7,4},{8,11},{9,10},{10,... | collective-permute-start | bytes 380936 | tf_op jit(solution)/shard_map/ppermute | solution.py:240
  58.3 2.2 %shard_map.121 = (bf16[96,768]{1,0:T(8,128)(2,1)S(1)}, bf16[96,768]{1,0:T(8,128)(2,1)S(1)}, bf16[96,768]{1,0:T(8,128)(2,1)S(1)}, bf16[496,128]{1,0:T(8,128)(2,1)S(1)}, bf16[496,128]{1,0:T(8,128)(2,1)S(1)}) custom-call(bf16[3,96,768]{2,1,0:T(8,128)(2,1)S(1)} %add_convert_fusion.1.refs_5_.own_ref, bf16[3,96,768]{2,1,0:T(8,128)(2,1)S(1)} %collective-permute-done.13.got_ref, ...), custom_call_target="tpu_custom_call" | custom-call | flops 1 | bytes 1 | tf_op jit(solution)/shard_map/pallas_call | solution.py:308
  63.6 3.0 %collective-permute-start.17 = (bf16[496,128]{1,0:T(8,128)(2,1)S(1)}, bf16[496,128]{1,0:T(8,128)(2,1)S(1)}, u32[]{:S(2)}, u32[]{:S(2)}) collective-permute-start(bf16[496,128]{1,0:T(8,128)(2,1)S(1)} %get-tuple-element.54), channel_id=1, source_target_pairs={{0,5},{1,4},{2,1},{3,0},{4,7},{5,6},{6,3},{7,2},{8,13},{9,12},{10,... | collective-permute-start | bytes 380936 | tf_op jit(solution)/shard_map/ppermute | solution.py:240
  66.7 3.1 %collective-permute-done.19.got_ref = bf16[3,96,768]{2,1,0:T(8,128)(2,1)S(1)} collective-permute-done((bf16[3,96,768]{2,1,0:T(8,128)(2,1)S(1)}, bf16[3,96,768]{2,1,0:T(8,128)(2,1)S(1)}, u32[]{:S(2)}, u32[]{:S(2)}) %collective-permute-start.19) | collective-permute-done | bytes 442400 | tf_op jit(solution)/shard_map/ppermute | solution.py:230
  69.8 2.2 %shard_map.122 = (bf16[96,768]{1,0:T(8,128)(2,1)S(1)}, bf16[96,768]{1,0:T(8,128)(2,1)S(1)}, bf16[96,768]{1,0:T(8,128)(2,1)S(1)}, bf16[496,128]{1,0:T(8,128)(2,1)S(1)}, bf16[496,128]{1,0:T(8,128)(2,1)S(1)}) custom-call(bf16[3,96,768]{2,1,0:T(8,128)(2,1)S(1)} %add_convert_fusion.own_ref, bf16[3,96,768]{2,1,0:T(8,128)(2,1)S(1)} %collective-permute-done.19.got_ref, ...), custom_call_target="tpu_custom_call" | custom-call | flops 1 | bytes 1 | tf_op jit(solution)/shard_map/pallas_call | solution.py:308
  73.4 1.6 %collective-permute-start.21 = (bf16[496,128]{1,0:T(8,128)(2,1)S(1)}, bf16[496,128]{1,0:T(8,128)(2,1)S(1)}, u32[]{:S(2)}, u32[]{:S(2)}) collective-permute-start(bf16[496,128]{1,0:T(8,128)(2,1)S(1)} %get-tuple-element.58), channel_id=1, source_target_pairs={{0,7},{1,6},{2,5},{3,4},{4,3},{5,2},{6,1},{7,0},{8,15},{9,14},{10,... | collective-permute-start | bytes 380936 | tf_op jit(solution)/shard_map/ppermute | solution.py:240
  75.0 5.2 %shard_map.124 = (bf16[1,1280,768]{2,1,0:T(8,128)(2,1)}, bf16[1,1280,768]{2,1,0:T(8,128)(2,1)}, bf16[1,768,1280]{2,1,0:T(8,128)(2,1)}) custom-call(bf16[96,1280]{1,0:T(8,128)(2,1)S(1)} %get-tuple-element.39.refs_0_, bf16[96,1280]{1,0:T(8,128)(2,1)S(1)} %collective-permute-done.refs_1_, ...), custom_call_target="tpu_custom_call" | custom-call | flops 1 | bytes 1 | tf_op jit(solution)/shard_map/pallas_call | solution.py:326
  80.2 1.8 %collective-permute-done.20.refs_8_ = bf16[496,128]{1,0:T(8,128)(2,1)S(1)} collective-permute-done((bf16[496,128]{1,0:T(8,128)(2,1)S(1)}, bf16[496,128]{1,0:T(8,128)(2,1)S(1)}, u32[]{:S(2)}, u32[]{:S(2)}) %collective-permute-start.20) | collective-permute-done | bytes 127008 | tf_op jit(solution)/shard_map/ppermute | solution.py:240
  82.0 3.4 %collective-permute-done.21.refs_9_ = bf16[496,128]{1,0:T(8,128)(2,1)S(1)} collective-permute-done((bf16[496,128]{1,0:T(8,128)(2,1)S(1)}, bf16[496,128]{1,0:T(8,128)(2,1)S(1)}, u32[]{:S(2)}, u32[]{:S(2)}) %collective-permute-start.21) | collective-permute-done | bytes 127008 | tf_op jit(solution)/shard_map/ppermute | solution.py:240
  (43 shorter events, 17.9 us)
Async XLA Ops:
  2.6 3.7 %collective-permute-start = (bf16[96,1280]{1,0:T(8,128)(2,1)S(1)}, bf16[96,1280]{1,0:T(8,128)(2,1)S(1)}, u32[]{:S(2)}, u32[]{:S(2)}) collective-permute-start(bf16[96,1280]{1,0:T(8,128)(2,1)S(1)} %get-tuple-element.40), channel_id=1, source_target_pairs={{0,1},{1,0},{2,3},{3,2},{4,5},{5,4},{6,7},{7,6},{8,9},{9,8},{10,11... | collective-permute-start | bytes 737288 | tf_op jit(solution)/shard_map/ppermute | solution.py:240
  3.4 13.7 %collective-permute-start.3 = (bf16[192,1280]{1,0:T(8,128)(2,1)S(1)}, bf16[192,1280]{1,0:T(8,128)(2,1)S(1)}, u32[]{:S(2)}, u32[]{:S(2)}) collective-permute-start(bf16[192,1280]{1,0:T(8,128)(2,1)S(1)} %get-tuple-element.44), channel_id=1, source_target_pairs={{0,4},{1,5},{2,0},{3,1},{4,6},{5,7},{6,2},{7,3},{8,12},{9,13},{10,... | collective-permute-start | bytes 1474568 | tf_op jit(solution)/shard_map/ppermute | solution.py:240
  8.0 10.5 %collective-permute-start.1 = (bf16[3,96,768]{2,1,0:T(8,128)(2,1)S(1)}, bf16[3,96,768]{2,1,0:T(8,128)(2,1)S(1)}, u32[]{:S(2)}, u32[]{:S(2)}) collective-permute-start(bf16[3,96,768]{2,1,0:T(8,128)(2,1)S(1)} %shard_map.112), channel_id=1, source_target_pairs={{0,8},{1,17},{2,10},{3,19},{4,12},{5,21},{6,14},{7,23},{8,0},{9,25... | collective-permute-start | bytes 1327112 | tf_op jit(solution)/shard_map/ppermute | solution.py:230
  8.1 19.6 %collective-permute-start.8 = (bf16[192,1280]{1,0:T(8,128)(2,1)S(1)}, bf16[192,1280]{1,0:T(8,128)(2,1)S(1)}, u32[]{:S(2)}, u32[]{:S(2)}) collective-permute-start(bf16[192,1280]{1,0:T(8,128)(2,1)S(1)} %get-tuple-element.47), channel_id=1, source_target_pairs={{0,2},{1,3},{2,6},{3,7},{4,0},{5,1},{6,4},{7,5},{8,10},{9,11},{10,... | collective-permute-start | bytes 1474568 | tf_op jit(solution)/shard_map/ppermute | solution.py:240
  17.1 2.5 %collective-permute-start.4 = (bf16[96,1280]{1,0:T(8,128)(2,1)S(1)}, bf16[96,1280]{1,0:T(8,128)(2,1)S(1)}, u32[]{:S(2)}, u32[]{:S(2)}) collective-permute-start(bf16[96,1280]{1,0:T(8,128)(2,1)S(1)} %shard_map.113), channel_id=1, source_target_pairs={{0,1},{1,0},{2,3},{3,2},{4,5},{5,4},{6,7},{7,6},{8,9},{9,8},{10,11... | collective-permute-start | bytes 737288 | tf_op jit(solution)/shard_map/ppermute | solution.py:240
  21.3 9.8 %collective-permute-start.6 = (bf16[3,96,768]{2,1,0:T(8,128)(2,1)S(1)}, bf16[3,96,768]{2,1,0:T(8,128)(2,1)S(1)}, u32[]{:S(2)}, u32[]{:S(2)}) collective-permute-start(bf16[3,96,768]{2,1,0:T(8,128)(2,1)S(1)} %shard_map.114.refs_0_), channel_id=1, source_target_pairs={{0,8},{1,17},{2,10},{3,19},{4,12},{5,21},{6,14},{7,23},{8,0},{9,25... | collective-permute-start | bytes 1327112 | tf_op jit(solution)/shard_map/ppermute | solution.py:230
  21.6 11.9 %collective-permute-start.2 = (bf16[3,96,768]{2,1,0:T(8,128)(2,1)S(1)}, bf16[3,96,768]{2,1,0:T(8,128)(2,1)S(1)}, u32[]{:S(2)}, u32[]{:S(2)}) collective-permute-start(bf16[3,96,768]{2,1,0:T(8,128)(2,1)S(1)} %add_convert_fusion.3.refs_5_.own_ref), channel_id=1, source_target_pairs={{0,16},{1,9},{2,18},{3,11},{4,20},{5,13},{6,22},{7,15},{8,24},{9,1... | collective-permute-start | bytes 1327112 | tf_op jit(solution)/shard_map/ppermute | solution.py:230
  22.8 26.2 %collective-permute-start.14 = (bf16[192,1280]{1,0:T(8,128)(2,1)S(1)}, bf16[192,1280]{1,0:T(8,128)(2,1)S(1)}, u32[]{:S(2)}, u32[]{:S(2)}) collective-permute-start(bf16[192,1280]{1,0:T(8,128)(2,1)S(1)} %get-tuple-element.51), channel_id=1, source_target_pairs={{0,6},{1,7},{2,4},{3,5},{4,2},{5,3},{6,0},{7,1},{8,14},{9,15},{10,... | collective-permute-start | bytes 1474568 | tf_op jit(solution)/shard_map/ppermute | solution.py:240
  27.8 8.0 %collective-permute-start.9 = (bf16[96,1280]{1,0:T(8,128)(2,1)S(1)}, bf16[96,1280]{1,0:T(8,128)(2,1)S(1)}, u32[]{:S(2)}, u32[]{:S(2)}) collective-permute-start(bf16[96,1280]{1,0:T(8,128)(2,1)S(1)} %shard_map.116), channel_id=1, source_target_pairs={{0,1},{1,0},{2,3},{3,2},{4,5},{5,4},{6,7},{7,6},{8,9},{9,8},{10,11... | collective-permute-start | bytes 737288 | tf_op jit(solution)/shard_map/ppermute | solution.py:240
  31.3 8.2 %collective-permute-start.7 = (bf16[3,96,768]{2,1,0:T(8,128)(2,1)S(1)}, bf16[3,96,768]{2,1,0:T(8,128)(2,1)S(1)}, u32[]{:S(2)}, u32[]{:S(2)}) collective-permute-start(bf16[3,96,768]{2,1,0:T(8,128)(2,1)S(1)} %add_convert_fusion.2.refs_5_.own_ref), channel_id=1, source_target_pairs={{0,16},{1,9},{2,18},{3,11},{4,20},{5,13},{6,22},{7,15},{8,24},{9,1... | collective-permute-start | bytes 1327112 | tf_op jit(solution)/shard_map/ppermute | solution.py:230
  37.4 12.1 %collective-permute-start.12 = (bf16[3,96,768]{2,1,0:T(8,128)(2,1)S(1)}, bf16[3,96,768]{2,1,0:T(8,128)(2,1)S(1)}, u32[]{:S(2)}, u32[]{:S(2)}) collective-permute-start(bf16[3,96,768]{2,1,0:T(8,128)(2,1)S(1)} %shard_map.117.refs_0_), channel_id=1, source_target_pairs={{0,8},{1,17},{2,10},{3,19},{4,12},{5,21},{6,14},{7,23},{8,0},{9,25... | collective-permute-start | bytes 1327112 | tf_op jit(solution)/shard_map/ppermute | solution.py:230
  49.0 2.0 %collective-permute-start.15 = (bf16[96,1280]{1,0:T(8,128)(2,1)S(1)}, bf16[96,1280]{1,0:T(8,128)(2,1)S(1)}, u32[]{:S(2)}, u32[]{:S(2)}) collective-permute-start(bf16[96,1280]{1,0:T(8,128)(2,1)S(1)} %shard_map.119), channel_id=1, source_target_pairs={{0,1},{1,0},{2,3},{3,2},{4,5},{5,4},{6,7},{7,6},{8,9},{9,8},{10,11... | collective-permute-start | bytes 737288 | tf_op jit(solution)/shard_map/ppermute | solution.py:240
  49.7 8.6 %collective-permute-start.13 = (bf16[3,96,768]{2,1,0:T(8,128)(2,1)S(1)}, bf16[3,96,768]{2,1,0:T(8,128)(2,1)S(1)}, u32[]{:S(2)}, u32[]{:S(2)}) collective-permute-start(bf16[3,96,768]{2,1,0:T(8,128)(2,1)S(1)} %add_convert_fusion.1.refs_5_.own_ref), channel_id=1, source_target_pairs={{0,16},{1,9},{2,18},{3,11},{4,20},{5,13},{6,22},{7,15},{8,24},{9,1... | collective-permute-start | bytes 1327112 | tf_op jit(solution)/shard_map/ppermute | solution.py:230
  52.7 9.5 %collective-permute-start.18 = (bf16[3,96,768]{2,1,0:T(8,128)(2,1)S(1)}, bf16[3,96,768]{2,1,0:T(8,128)(2,1)S(1)}, u32[]{:S(2)}, u32[]{:S(2)}) collective-permute-start(bf16[3,96,768]{2,1,0:T(8,128)(2,1)S(1)} %shard_map.120.refs_0_), channel_id=1, source_target_pairs={{0,8},{1,17},{2,10},{3,19},{4,12},{5,21},{6,14},{7,23},{8,0},{9,25... | collective-permute-start | bytes 1327112 | tf_op jit(solution)/shard_map/ppermute | solution.py:230
  53.0 7.6 %collective-permute-start.10 = (bf16[496,128]{1,0:T(8,128)(2,1)S(1)}, bf16[496,128]{1,0:T(8,128)(2,1)S(1)}, u32[]{:S(2)}, u32[]{:S(2)}) collective-permute-start(bf16[496,128]{1,0:T(8,128)(2,1)S(1)} %get-tuple-element.49), channel_id=1, source_target_pairs={{0,2},{1,3},{2,6},{3,7},{4,0},{5,1},{6,4},{7,5},{8,10},{9,11},{10,... | collective-permute-start | bytes 380936 | tf_op jit(solution)/shard_map/ppermute | solution.py:240
  53.0 8.1 %collective-permute-start.11 = (bf16[496,128]{1,0:T(8,128)(2,1)S(1)}, bf16[496,128]{1,0:T(8,128)(2,1)S(1)}, u32[]{:S(2)}, u32[]{:S(2)}) collective-permute-start(bf16[496,128]{1,0:T(8,128)(2,1)S(1)} %get-tuple-element.50), channel_id=1, source_target_pairs={{0,3},{1,2},{2,7},{3,6},{4,1},{5,0},{6,5},{7,4},{8,11},{9,10},{10,... | collective-permute-start | bytes 380936 | tf_op jit(solution)/shard_map/ppermute | solution.py:240
  62.2 7.5 %collective-permute-start.19 = (bf16[3,96,768]{2,1,0:T(8,128)(2,1)S(1)}, bf16[3,96,768]{2,1,0:T(8,128)(2,1)S(1)}, u32[]{:S(2)}, u32[]{:S(2)}) collective-permute-start(bf16[3,96,768]{2,1,0:T(8,128)(2,1)S(1)} %add_convert_fusion.own_ref), channel_id=1, source_target_pairs={{0,16},{1,9},{2,18},{3,11},{4,20},{5,13},{6,22},{7,15},{8,24},{9,1... | collective-permute-start | bytes 1327112 | tf_op jit(solution)/shard_map/ppermute | solution.py:230
  63.5 16.7 %collective-permute-start.5 = (bf16[496,128]{1,0:T(8,128)(2,1)S(1)}, bf16[496,128]{1,0:T(8,128)(2,1)S(1)}, u32[]{:S(2)}, u32[]{:S(2)}) collective-permute-start(bf16[496,128]{1,0:T(8,128)(2,1)S(1)} %get-tuple-element.46), channel_id=1, source_target_pairs={{0,1},{1,0},{2,3},{3,2},{4,5},{5,4},{6,7},{7,6},{8,9},{9,8},{10,11... | collective-permute-start | bytes 380936 | tf_op jit(solution)/shard_map/ppermute | solution.py:240
  63.5 16.7 %collective-permute-start.16 = (bf16[496,128]{1,0:T(8,128)(2,1)S(1)}, bf16[496,128]{1,0:T(8,128)(2,1)S(1)}, u32[]{:S(2)}, u32[]{:S(2)}) collective-permute-start(bf16[496,128]{1,0:T(8,128)(2,1)S(1)} %get-tuple-element.53), channel_id=1, source_target_pairs={{0,4},{1,5},{2,0},{3,1},{4,6},{5,7},{6,2},{7,3},{8,12},{9,13},{10,... | collective-permute-start | bytes 380936 | tf_op jit(solution)/shard_map/ppermute | solution.py:240
  63.6 16.6 %collective-permute-start.17 = (bf16[496,128]{1,0:T(8,128)(2,1)S(1)}, bf16[496,128]{1,0:T(8,128)(2,1)S(1)}, u32[]{:S(2)}, u32[]{:S(2)}) collective-permute-start(bf16[496,128]{1,0:T(8,128)(2,1)S(1)} %get-tuple-element.54), channel_id=1, source_target_pairs={{0,5},{1,4},{2,1},{3,0},{4,7},{5,6},{6,3},{7,2},{8,13},{9,12},{10,... | collective-permute-start | bytes 380936 | tf_op jit(solution)/shard_map/ppermute | solution.py:240
  72.0 10.0 %collective-permute-start.20 = (bf16[496,128]{1,0:T(8,128)(2,1)S(1)}, bf16[496,128]{1,0:T(8,128)(2,1)S(1)}, u32[]{:S(2)}, u32[]{:S(2)}) collective-permute-start(bf16[496,128]{1,0:T(8,128)(2,1)S(1)} %get-tuple-element.57), channel_id=1, source_target_pairs={{0,6},{1,7},{2,4},{3,5},{4,2},{5,3},{6,0},{7,1},{8,14},{9,15},{10,... | collective-permute-start | bytes 380936 | tf_op jit(solution)/shard_map/ppermute | solution.py:240
  73.4 12.0 %collective-permute-start.21 = (bf16[496,128]{1,0:T(8,128)(2,1)S(1)}, bf16[496,128]{1,0:T(8,128)(2,1)S(1)}, u32[]{:S(2)}, u32[]{:S(2)}) collective-permute-start(bf16[496,128]{1,0:T(8,128)(2,1)S(1)} %get-tuple-element.58), channel_id=1, source_target_pairs={{0,7},{1,6},{2,5},{3,4},{4,3},{5,2},{6,1},{7,0},{8,15},{9,14},{10,... | collective-permute-start | bytes 380936 | tf_op jit(solution)/shard_map/ppermute | solution.py:240
  74.9 10.4 %copy-start = (s32[128,2]{0,1:T(2,128)S(1)}, s32[128,2]{0,1:T(2,128)}, u32[]{:S(2)}) copy-start(s32[128,2]{0,1:T(2,128)} %param.8) | copy-start | bytes 3076
  75.0 10.4 %copy-start.1 = (bf16[128,2]{0,1:T(2,128)(2,1)S(1)}, bf16[128,2]{0,1:T(2,128)(2,1)}, u32[]{:S(2)}) copy-start(bf16[128,2]{0,1:T(2,128)(2,1)} %param.9) | copy-start | bytes 1540

commit v5 on v4

--- a/solution.py
+++ b/solution.py
@@ -88,12 +88,15 @@
     tokens = tokens_ref[...]
     cot = cot_ref[...]
     places = [(out, at) for out in out_refs for at in range(0, out.shape[0], 2 * capacity)]
+    ones = [jnp.where(hit, 1.0, 0.0) for hit in hits]
+    pick = jnp.concatenate(ones, axis=0).astype(BF16)
+    weigh = jnp.concatenate([one * scale[k : k + 1, :] for k, one in enumerate(ones)], axis=0)
+    picked = jnp.dot(pick, tokens, preferred_element_type=F32).astype(BF16)
+    weighed = jnp.dot(weigh.astype(BF16), cot, preferred_element_type=F32).astype(BF16)
     for k, (out, at) in enumerate(places):
-        pick = jnp.where(hits[k], 1.0, 0.0).astype(BF16)
-        weigh = jnp.where(hits[k], scale[k : k + 1, :], 0.0).astype(BF16)
-        mid, end = at + capacity, at + 2 * capacity
-        out[at:mid, :] = jnp.dot(pick, tokens, preferred_element_type=F32).astype(BF16)
-        out[mid:end, :] = jnp.dot(weigh, cot, preferred_element_type=F32).astype(BF16)
+        rows = slice(k * capacity, (k + 1) * capacity)
+        out[at : at + capacity, :] = picked[rows]
+        out[at + capacity : at + 2 * capacity, :] = weighed[rows]
 
 
 def hold_kernel(*refs):
@@ -129,7 +132,7 @@
             out_ref[i, :, at] = part.astype(BF16)
         return 0
 
-    lax.fori_loop(0, out_ref.shape[2] // tile, step, 0)
+    lax.fori_loop(0, out_ref.shape[2] // tile, step, 0, unroll=True)
 
 
 def backward_kernel(blocks, capacity, tile, own_ref, got_ref, gate_ref, up_ref, *refs):
@@ -177,7 +180,7 @@
             back_refs[k][pl.ds(start, per * capacity), :] = stacked
         return 0
 
-    lax.fori_loop(0, width // tile, step, 0)
+    lax.fori_loop(0, width // tile, step, 0, unroll=True)
 
 
 def weight_kernel(blocks, capacity, chunks, *refs):
@@ -200,13 +203,17 @@
     grad_ref, comb_ref = refs[-2:]
     first, second, hits = slot_masks(routes_ref[...], messages, capacity, experts)
     picks = [jnp.where(hit, 1.0, 0.0).astype(BF16) for hit in hits]
-    pick = jnp.concatenate(picks, axis=0)
+    ones = [jnp.where(hit, 1.0, 0.0) for hit in hits]
+    pick = jnp.concatenate(ones, axis=0).T.astype(BF16)
     groups = grad_ref.shape[1] // LANES
-    for c in range(groups):
-        piece = jnp.concatenate(
-            [ref[c * capacity : (c + 1) * capacity, :] for ref in back_refs], axis=0
-        )
-        grad_ref[:, c * LANES : (c + 1) * LANES] = contract_first(pick, piece).astype(BF16)
+    for c in range(0, groups, 2):
+        pieces = [
+            jnp.concatenate([ref[b * capacity : (b + 1) * capacity, :] for ref in back_refs], axis=0)
+            for b in (c, c + 1)
+        ]
+        piece = jnp.concatenate(pieces, axis=1)
+        total = jnp.dot(pick, piece, preferred_element_type=F32)
+        grad_ref[:, c * LANES : (c + 2) * LANES] = total.astype(BF16)
     total0 = jnp.zeros((1, LANES), F32)
     total1 = total0
     for k in range(len(messages)):

time: 86.9 us -> 85.8 us (0.987)
  Pallas kernels: 27 us -> 21.6 us
  waiting for transfers between devices: 32.6 us -> 37.1 us
    pallas_call x4, Pallas kernels: 8.88 us -> 5.29 us  [run_backward(): pl.pallas_call(functools.partial(backward_kernel, count, capacity, 256),...]
    ppermute x14, waiting for transfers between devices: 24.3 us -> 26.6 us  [moved(): return lax.ppermute(value, 'dp', pairs)]
    ppermute x8, waiting for transfers between devices: 8.38 us -> 10.4 us  [crossed(): return lax.ppermute(value, ('expert', 'dp'), pairs)]
    pallas_call x4, Pallas kernels: 6.72 us -> 5.17 us  [run_forward(): pl.pallas_call(functools.partial(forward_kernel, count, capacity, 256), i...]
  transfers between devices with their start and end apart: 22 -> 22, of which waited for: 12 -> 12; matrix products, arithmetic and copies ran while one was open for 0% -> 0% of each run, Pallas kernels for 27% -> 22%
where the time goes in v5:
time: 85.8 us; the launch traced here: 85.6 us
  waiting for transfers between devices  37.1 us (43%)
  starting transfers between devices  25.7 us (30%)
  Pallas kernels  21.6 us (25%)
    ppermute x14, waiting for transfers between devices, moved(): return lax.ppermute(value, 'dp', pairs)  26.6 us
    ppermute x14, starting transfers between devices, moved(): return lax.ppermute(value, 'dp', pairs)  17.8 us
    ppermute x8, waiting for transfers between devices, crossed(): return lax.ppermute(value, ('expert', 'dp'), pairs)  10.4 us
    ppermute x8, starting transfers between devices, crossed(): return lax.ppermute(value, ('expert', 'dp'), pairs)  7.9 us
    pallas_call x4, Pallas kernels, run_backward(): pl.pallas_call(functools.partial(backward_kernel, count, capacity, 256),...  5.29 us
    pallas_call x1, Pallas kernels, run_weights(): pl.pallas_call(functools.partial(weight_kernel, count, capacity, chunks),...  5.24 us
    pallas_call x4, Pallas kernels, run_forward(): pl.pallas_call(functools.partial(forward_kernel, count, capacity, 256), i...  5.17 us
    pallas_call x1, Pallas kernels, run_hold(): pl.pallas_call(hold_kernel, in_specs=in_hbm(len(weights)), out_specs=in_v...  2.76 us
  transfers between devices with their start and end apart: 22, of which 12 were waited for; matrix products, arithmetic and copies ran while one was open for 0% of the time, Pallas kernels for 22%

profile of v5, /device:TPU:13, one launch (start us, length us, event | category | flops | bytes accessed | tf_op | source)
XLA Modules:
  0.0 85.6 jit_solution(2124345943465334838)
XLA Ops:
  0.6 1.8 %shard_map.110 = (bf16[96,1280]{1,0:T(8,128)(2,1)S(1)}, bf16[96,1280]{1,0:T(8,128)(2,1)S(1)}, bf16[192,1280]{1,0:T(8,128)(2,1)S(1)}, bf16[192,1280]{1,0:T(8,128)(2,1)S(1)}, bf16[192,1280]{1,0:T(8,128)(2,1)S(1)}) custom-call(s32[2,128]{1,0:T(2,128)} %bitcast.3, bf16[2,128]{1,0:T(2,128)(2,1)} %bitcast.5, bf16[128,1280]{1,0:T(8,128)(2,1)} %tokens_hbm.1, ...), custom_call_target="tpu_custom_call" | custom-call | flops 1 | bytes 1 | tf_op jit(solution)/shard_map/pallas_call | solution.py:368
  3.4 2.8 %shard_map.111 = (bf16[1,1280,768]{2,1,0:T(8,128)(2,1)S(1)}, bf16[1,1280,768]{2,1,0:T(8,128)(2,1)S(1)}, bf16[1,768,1280]{2,1,0:T(8,128)(2,1)S(1)}) custom-call(bf16[1,1280,768]{2,1,0:T(8,128)(2,1)} %refs_0_.1, bf16[1,1280,768]{2,1,0:T(8,128)(2,1)} %refs_1_.1, bf16[1,768,1280]{2,1,0:T(8,128)(2,1)} %refs_2_.1), custom_call_target="tpu_custom_call" | custom-call | flops 1 | bytes 1 | tf_op jit(solution)/shard_map/pallas_call | solution.py:275
  7.6 2.4 %collective-permute-start.8 = (bf16[192,1280]{1,0:T(8,128)(2,1)S(1)}, bf16[192,1280]{1,0:T(8,128)(2,1)S(1)}, u32[]{:S(2)}, u32[]{:S(2)}) collective-permute-start(bf16[192,1280]{1,0:T(8,128)(2,1)S(1)} %get-tuple-element.47), channel_id=1, source_target_pairs={{0,2},{1,3},{2,6},{3,7},{4,0},{5,1},{6,4},{7,5},{8,10},{9,11},{10,... | collective-permute-start | bytes 1474568 | tf_op jit(solution)/shard_map/ppermute | solution.py:247
  9.9 7.0 %collective-permute-done.3.whole_ref.refs_0_.refs_2_ = bf16[192,1280]{1,0:T(8,128)(2,1)S(1)} collective-permute-done((bf16[192,1280]{1,0:T(8,128)(2,1)S(1)}, bf16[192,1280]{1,0:T(8,128)(2,1)S(1)}, u32[]{:S(2)}, u32[]{:S(2)}) %collective-permute-start.3) | collective-permute-done | bytes 491552 | tf_op jit(solution)/shard_map/ppermute | solution.py:247
  16.9 1.4 %collective-permute-start.4 = (bf16[96,1280]{1,0:T(8,128)(2,1)S(1)}, bf16[96,1280]{1,0:T(8,128)(2,1)S(1)}, u32[]{:S(2)}, u32[]{:S(2)}) collective-permute-start(bf16[96,1280]{1,0:T(8,128)(2,1)S(1)} %shard_map.113), channel_id=1, source_target_pairs={{0,1},{1,0},{2,3},{3,2},{4,5},{5,4},{6,7},{7,6},{8,9},{9,8},{10,11... | collective-permute-start | bytes 737288 | tf_op jit(solution)/shard_map/ppermute | solution.py:247
  23.5 4.0 %collective-permute-done.8.whole_ref.refs_0_.refs_4_ = bf16[192,1280]{1,0:T(8,128)(2,1)S(1)} collective-permute-done((bf16[192,1280]{1,0:T(8,128)(2,1)S(1)}, bf16[192,1280]{1,0:T(8,128)(2,1)S(1)}, u32[]{:S(2)}, u32[]{:S(2)}) %collective-permute-start.8) | collective-permute-done | bytes 491552 | tf_op jit(solution)/shard_map/ppermute | solution.py:247
  27.6 1.4 %collective-permute-start.9 = (bf16[96,1280]{1,0:T(8,128)(2,1)S(1)}, bf16[96,1280]{1,0:T(8,128)(2,1)S(1)}, u32[]{:S(2)}, u32[]{:S(2)}) collective-permute-start(bf16[96,1280]{1,0:T(8,128)(2,1)S(1)} %shard_map.116), channel_id=1, source_target_pairs={{0,1},{1,0},{2,3},{3,2},{4,5},{5,4},{6,7},{7,6},{8,9},{9,8},{10,11... | collective-permute-start | bytes 737288 | tf_op jit(solution)/shard_map/ppermute | solution.py:247
  29.0 1.6 %collective-permute-done.6 = bf16[3,96,768]{2,1,0:T(8,128)(2,1)S(1)} collective-permute-done((bf16[3,96,768]{2,1,0:T(8,128)(2,1)S(1)}, bf16[3,96,768]{2,1,0:T(8,128)(2,1)S(1)}, u32[]{:S(2)}, u32[]{:S(2)}) %collective-permute-start.6) | collective-permute-done | bytes 442400 | tf_op jit(solution)/shard_map/ppermute | solution.py:237
  30.7 2.3 %collective-permute-start.7 = (bf16[3,96,768]{2,1,0:T(8,128)(2,1)S(1)}, bf16[3,96,768]{2,1,0:T(8,128)(2,1)S(1)}, u32[]{:S(2)}, u32[]{:S(2)}) collective-permute-start(bf16[3,96,768]{2,1,0:T(8,128)(2,1)S(1)} %add_convert_fusion.2.refs_5_.own_ref), channel_id=1, source_target_pairs={{0,16},{1,9},{2,18},{3,11},{4,20},{5,13},{6,22},{7,15},{8,24},{9,1... | collective-permute-start | bytes 1327112 | tf_op jit(solution)/shard_map/ppermute | solution.py:237
  32.9 1.3 %shard_map.115 = (bf16[96,768]{1,0:T(8,128)(2,1)S(1)}, bf16[96,768]{1,0:T(8,128)(2,1)S(1)}, bf16[96,768]{1,0:T(8,128)(2,1)S(1)}, bf16[496,128]{1,0:T(8,128)(2,1)S(1)}, bf16[496,128]{1,0:T(8,128)(2,1)S(1)}) custom-call(bf16[3,96,768]{2,1,0:T(8,128)(2,1)S(1)} %add_convert_fusion.3.refs_5_.own_ref, bf16[3,96,768]{2,1,0:T(8,128)(2,1)S(1)} %collective-permute-done.2.got_ref, ...), custom_call_target="tpu_custom_call" | custom-call | flops 1 | bytes 1 | tf_op jit(solution)/shard_map/pallas_call | solution.py:315
  36.8 2.2 %collective-permute-done.7.got_ref = bf16[3,96,768]{2,1,0:T(8,128)(2,1)S(1)} collective-permute-done((bf16[3,96,768]{2,1,0:T(8,128)(2,1)S(1)}, bf16[3,96,768]{2,1,0:T(8,128)(2,1)S(1)}, u32[]{:S(2)}, u32[]{:S(2)}) %collective-permute-start.7) | collective-permute-done | bytes 442400 | tf_op jit(solution)/shard_map/ppermute | solution.py:237
  38.9 1.3 %shard_map.118 = (bf16[96,768]{1,0:T(8,128)(2,1)S(1)}, bf16[96,768]{1,0:T(8,128)(2,1)S(1)}, bf16[96,768]{1,0:T(8,128)(2,1)S(1)}, bf16[496,128]{1,0:T(8,128)(2,1)S(1)}, bf16[496,128]{1,0:T(8,128)(2,1)S(1)}) custom-call(bf16[3,96,768]{2,1,0:T(8,128)(2,1)S(1)} %add_convert_fusion.2.refs_5_.own_ref, bf16[3,96,768]{2,1,0:T(8,128)(2,1)S(1)} %collective-permute-done.7.got_ref, ...), custom_call_target="tpu_custom_call" | custom-call | flops 1 | bytes 1 | tf_op jit(solution)/shard_map/pallas_call | solution.py:315
  40.3 8.6 %collective-permute-done.14.whole_ref.refs_0_.refs_6_ = bf16[192,1280]{1,0:T(8,128)(2,1)S(1)} collective-permute-done((bf16[192,1280]{1,0:T(8,128)(2,1)S(1)}, bf16[192,1280]{1,0:T(8,128)(2,1)S(1)}, u32[]{:S(2)}, u32[]{:S(2)}) %collective-permute-start.14) | collective-permute-done | bytes 491552 | tf_op jit(solution)/shard_map/ppermute | solution.py:247
  52.4 4.0 %collective-permute-start.11 = (bf16[496,128]{1,0:T(8,128)(2,1)S(1)}, bf16[496,128]{1,0:T(8,128)(2,1)S(1)}, u32[]{:S(2)}, u32[]{:S(2)}) collective-permute-start(bf16[496,128]{1,0:T(8,128)(2,1)S(1)} %get-tuple-element.50), channel_id=1, source_target_pairs={{0,3},{1,2},{2,7},{3,6},{4,1},{5,0},{6,5},{7,4},{8,11},{9,10},{10,... | collective-permute-start | bytes 380936 | tf_op jit(solution)/shard_map/ppermute | solution.py:247
  56.4 2.1 %collective-permute-done.13.got_ref = bf16[3,96,768]{2,1,0:T(8,128)(2,1)S(1)} collective-permute-done((bf16[3,96,768]{2,1,0:T(8,128)(2,1)S(1)}, bf16[3,96,768]{2,1,0:T(8,128)(2,1)S(1)}, u32[]{:S(2)}, u32[]{:S(2)}) %collective-permute-start.13) | collective-permute-done | bytes 442400 | tf_op jit(solution)/shard_map/ppermute | solution.py:237
  58.6 1.3 %shard_map.121 = (bf16[96,768]{1,0:T(8,128)(2,1)S(1)}, bf16[96,768]{1,0:T(8,128)(2,1)S(1)}, bf16[96,768]{1,0:T(8,128)(2,1)S(1)}, bf16[496,128]{1,0:T(8,128)(2,1)S(1)}, bf16[496,128]{1,0:T(8,128)(2,1)S(1)}) custom-call(bf16[3,96,768]{2,1,0:T(8,128)(2,1)S(1)} %add_convert_fusion.1.refs_5_.own_ref, bf16[3,96,768]{2,1,0:T(8,128)(2,1)S(1)} %collective-permute-done.13.got_ref, ...), custom_call_target="tpu_custom_call" | custom-call | flops 1 | bytes 1 | tf_op jit(solution)/shard_map/pallas_call | solution.py:315
  60.5 1.4 %collective-permute-done.18 = bf16[3,96,768]{2,1,0:T(8,128)(2,1)S(1)} collective-permute-done((bf16[3,96,768]{2,1,0:T(8,128)(2,1)S(1)}, bf16[3,96,768]{2,1,0:T(8,128)(2,1)S(1)}, u32[]{:S(2)}, u32[]{:S(2)}) %collective-permute-start.18) | collective-permute-done | bytes 442400 | tf_op jit(solution)/shard_map/ppermute | solution.py:237
  63.4 3.1 %collective-permute-start.17 = (bf16[496,128]{1,0:T(8,128)(2,1)S(1)}, bf16[496,128]{1,0:T(8,128)(2,1)S(1)}, u32[]{:S(2)}, u32[]{:S(2)}) collective-permute-start(bf16[496,128]{1,0:T(8,128)(2,1)S(1)} %get-tuple-element.54), channel_id=1, source_target_pairs={{0,5},{1,4},{2,1},{3,0},{4,7},{5,6},{6,3},{7,2},{8,13},{9,12},{10,... | collective-permute-start | bytes 380936 | tf_op jit(solution)/shard_map/ppermute | solution.py:247
  66.5 3.1 %collective-permute-done.19.got_ref = bf16[3,96,768]{2,1,0:T(8,128)(2,1)S(1)} collective-permute-done((bf16[3,96,768]{2,1,0:T(8,128)(2,1)S(1)}, bf16[3,96,768]{2,1,0:T(8,128)(2,1)S(1)}, u32[]{:S(2)}, u32[]{:S(2)}) %collective-permute-start.19) | collective-permute-done | bytes 442400 | tf_op jit(solution)/shard_map/ppermute | solution.py:237
  70.9 1.4 %collective-permute-start.20 = (bf16[496,128]{1,0:T(8,128)(2,1)S(1)}, bf16[496,128]{1,0:T(8,128)(2,1)S(1)}, u32[]{:S(2)}, u32[]{:S(2)}) collective-permute-start(bf16[496,128]{1,0:T(8,128)(2,1)S(1)} %get-tuple-element.57), channel_id=1, source_target_pairs={{0,6},{1,7},{2,4},{3,5},{4,2},{5,3},{6,0},{7,1},{8,14},{9,15},{10,... | collective-permute-start | bytes 380936 | tf_op jit(solution)/shard_map/ppermute | solution.py:247
  72.3 1.4 %collective-permute-start.21 = (bf16[496,128]{1,0:T(8,128)(2,1)S(1)}, bf16[496,128]{1,0:T(8,128)(2,1)S(1)}, u32[]{:S(2)}, u32[]{:S(2)}) collective-permute-start(bf16[496,128]{1,0:T(8,128)(2,1)S(1)} %get-tuple-element.58), channel_id=1, source_target_pairs={{0,7},{1,6},{2,5},{3,4},{4,3},{5,2},{6,1},{7,0},{8,15},{9,14},{10,... | collective-permute-start | bytes 380936 | tf_op jit(solution)/shard_map/ppermute | solution.py:247
  73.7 5.2 %shard_map.124 = (bf16[1,1280,768]{2,1,0:T(8,128)(2,1)}, bf16[1,1280,768]{2,1,0:T(8,128)(2,1)}, bf16[1,768,1280]{2,1,0:T(8,128)(2,1)}) custom-call(bf16[96,1280]{1,0:T(8,128)(2,1)S(1)} %get-tuple-element.39.refs_0_, bf16[96,1280]{1,0:T(8,128)(2,1)S(1)} %collective-permute-done.refs_1_, ...), custom_call_target="tpu_custom_call" | custom-call | flops 1 | bytes 1 | tf_op jit(solution)/shard_map/pallas_call | solution.py:333
  78.9 2.4 %collective-permute-done.20.refs_8_ = bf16[496,128]{1,0:T(8,128)(2,1)S(1)} collective-permute-done((bf16[496,128]{1,0:T(8,128)(2,1)S(1)}, bf16[496,128]{1,0:T(8,128)(2,1)S(1)}, u32[]{:S(2)}, u32[]{:S(2)}) %collective-permute-start.20) | collective-permute-done | bytes 127008 | tf_op jit(solution)/shard_map/ppermute | solution.py:247
  81.3 3.0 %collective-permute-done.21.refs_9_ = bf16[496,128]{1,0:T(8,128)(2,1)S(1)} collective-permute-done((bf16[496,128]{1,0:T(8,128)(2,1)S(1)}, bf16[496,128]{1,0:T(8,128)(2,1)S(1)}, u32[]{:S(2)}, u32[]{:S(2)}) %collective-permute-start.21) | collective-permute-done | bytes 127008 | tf_op jit(solution)/shard_map/ppermute | solution.py:247
  (43 shorter events, 18.4 us)
Async XLA Ops:
  2.4 3.7 %collective-permute-start = (bf16[96,1280]{1,0:T(8,128)(2,1)S(1)}, bf16[96,1280]{1,0:T(8,128)(2,1)S(1)}, u32[]{:S(2)}, u32[]{:S(2)}) collective-permute-start(bf16[96,1280]{1,0:T(8,128)(2,1)S(1)} %get-tuple-element.40), channel_id=1, source_target_pairs={{0,1},{1,0},{2,3},{3,2},{4,5},{5,4},{6,7},{7,6},{8,9},{9,8},{10,11... | collective-permute-start | bytes 737288 | tf_op jit(solution)/shard_map/ppermute | solution.py:247
  3.2 13.7 %collective-permute-start.3 = (bf16[192,1280]{1,0:T(8,128)(2,1)S(1)}, bf16[192,1280]{1,0:T(8,128)(2,1)S(1)}, u32[]{:S(2)}, u32[]{:S(2)}) collective-permute-start(bf16[192,1280]{1,0:T(8,128)(2,1)S(1)} %get-tuple-element.44), channel_id=1, source_target_pairs={{0,4},{1,5},{2,0},{3,1},{4,6},{5,7},{6,2},{7,3},{8,12},{9,13},{10,... | collective-permute-start | bytes 1474568 | tf_op jit(solution)/shard_map/ppermute | solution.py:247
  7.4 10.9 %collective-permute-start.1 = (bf16[3,96,768]{2,1,0:T(8,128)(2,1)S(1)}, bf16[3,96,768]{2,1,0:T(8,128)(2,1)S(1)}, u32[]{:S(2)}, u32[]{:S(2)}) collective-permute-start(bf16[3,96,768]{2,1,0:T(8,128)(2,1)S(1)} %shard_map.112), channel_id=1, source_target_pairs={{0,8},{1,17},{2,10},{3,19},{4,12},{5,21},{6,14},{7,23},{8,0},{9,25... | collective-permute-start | bytes 1327112 | tf_op jit(solution)/shard_map/ppermute | solution.py:237
  7.6 20.0 %collective-permute-start.8 = (bf16[192,1280]{1,0:T(8,128)(2,1)S(1)}, bf16[192,1280]{1,0:T(8,128)(2,1)S(1)}, u32[]{:S(2)}, u32[]{:S(2)}) collective-permute-start(bf16[192,1280]{1,0:T(8,128)(2,1)S(1)} %get-tuple-element.47), channel_id=1, source_target_pairs={{0,2},{1,3},{2,6},{3,7},{4,0},{5,1},{6,4},{7,5},{8,10},{9,11},{10,... | collective-permute-start | bytes 1474568 | tf_op jit(solution)/shard_map/ppermute | solution.py:247
  16.9 2.5 %collective-permute-start.4 = (bf16[96,1280]{1,0:T(8,128)(2,1)S(1)}, bf16[96,1280]{1,0:T(8,128)(2,1)S(1)}, u32[]{:S(2)}, u32[]{:S(2)}) collective-permute-start(bf16[96,1280]{1,0:T(8,128)(2,1)S(1)} %shard_map.113), channel_id=1, source_target_pairs={{0,1},{1,0},{2,3},{3,2},{4,5},{5,4},{6,7},{7,6},{8,9},{9,8},{10,11... | collective-permute-start | bytes 737288 | tf_op jit(solution)/shard_map/ppermute | solution.py:247
  20.7 9.8 %collective-permute-start.6 = (bf16[3,96,768]{2,1,0:T(8,128)(2,1)S(1)}, bf16[3,96,768]{2,1,0:T(8,128)(2,1)S(1)}, u32[]{:S(2)}, u32[]{:S(2)}) collective-permute-start(bf16[3,96,768]{2,1,0:T(8,128)(2,1)S(1)} %shard_map.114.refs_0_), channel_id=1, source_target_pairs={{0,8},{1,17},{2,10},{3,19},{4,12},{5,21},{6,14},{7,23},{8,0},{9,25... | collective-permute-start | bytes 1327112 | tf_op jit(solution)/shard_map/ppermute | solution.py:237
  21.0 11.9 %collective-permute-start.2 = (bf16[3,96,768]{2,1,0:T(8,128)(2,1)S(1)}, bf16[3,96,768]{2,1,0:T(8,128)(2,1)S(1)}, u32[]{:S(2)}, u32[]{:S(2)}) collective-permute-start(bf16[3,96,768]{2,1,0:T(8,128)(2,1)S(1)} %add_convert_fusion.3.refs_5_.own_ref), channel_id=1, source_target_pairs={{0,16},{1,9},{2,18},{3,11},{4,20},{5,13},{6,22},{7,15},{8,24},{9,1... | collective-permute-start | bytes 1327112 | tf_op jit(solution)/shard_map/ppermute | solution.py:237
  22.2 26.6 %collective-permute-start.14 = (bf16[192,1280]{1,0:T(8,128)(2,1)S(1)}, bf16[192,1280]{1,0:T(8,128)(2,1)S(1)}, u32[]{:S(2)}, u32[]{:S(2)}) collective-permute-start(bf16[192,1280]{1,0:T(8,128)(2,1)S(1)} %get-tuple-element.51), channel_id=1, source_target_pairs={{0,6},{1,7},{2,4},{3,5},{4,2},{5,3},{6,0},{7,1},{8,14},{9,15},{10,... | collective-permute-start | bytes 1474568 | tf_op jit(solution)/shard_map/ppermute | solution.py:247
  27.6 6.7 %collective-permute-start.9 = (bf16[96,1280]{1,0:T(8,128)(2,1)S(1)}, bf16[96,1280]{1,0:T(8,128)(2,1)S(1)}, u32[]{:S(2)}, u32[]{:S(2)}) collective-permute-start(bf16[96,1280]{1,0:T(8,128)(2,1)S(1)} %shard_map.116), channel_id=1, source_target_pairs={{0,1},{1,0},{2,3},{3,2},{4,5},{5,4},{6,7},{7,6},{8,9},{9,8},{10,11... | collective-permute-start | bytes 737288 | tf_op jit(solution)/shard_map/ppermute | solution.py:247
  30.7 8.2 %collective-permute-start.7 = (bf16[3,96,768]{2,1,0:T(8,128)(2,1)S(1)}, bf16[3,96,768]{2,1,0:T(8,128)(2,1)S(1)}, u32[]{:S(2)}, u32[]{:S(2)}) collective-permute-start(bf16[3,96,768]{2,1,0:T(8,128)(2,1)S(1)} %add_convert_fusion.2.refs_5_.own_ref), channel_id=1, source_target_pairs={{0,16},{1,9},{2,18},{3,11},{4,20},{5,13},{6,22},{7,15},{8,24},{9,1... | collective-permute-start | bytes 1327112 | tf_op jit(solution)/shard_map/ppermute | solution.py:237
  35.6 13.8 %collective-permute-start.12 = (bf16[3,96,768]{2,1,0:T(8,128)(2,1)S(1)}, bf16[3,96,768]{2,1,0:T(8,128)(2,1)S(1)}, u32[]{:S(2)}, u32[]{:S(2)}) collective-permute-start(bf16[3,96,768]{2,1,0:T(8,128)(2,1)S(1)} %shard_map.117.refs_0_), channel_id=1, source_target_pairs={{0,8},{1,17},{2,10},{3,19},{4,12},{5,21},{6,14},{7,23},{8,0},{9,25... | collective-permute-start | bytes 1327112 | tf_op jit(solution)/shard_map/ppermute | solution.py:237
  48.9 1.9 %collective-permute-start.15 = (bf16[96,1280]{1,0:T(8,128)(2,1)S(1)}, bf16[96,1280]{1,0:T(8,128)(2,1)S(1)}, u32[]{:S(2)}, u32[]{:S(2)}) collective-permute-start(bf16[96,1280]{1,0:T(8,128)(2,1)S(1)} %shard_map.119), channel_id=1, source_target_pairs={{0,1},{1,0},{2,3},{3,2},{4,5},{5,4},{6,7},{7,6},{8,9},{9,8},{10,11... | collective-permute-start | bytes 737288 | tf_op jit(solution)/shard_map/ppermute | solution.py:247
  49.5 9.0 %collective-permute-start.13 = (bf16[3,96,768]{2,1,0:T(8,128)(2,1)S(1)}, bf16[3,96,768]{2,1,0:T(8,128)(2,1)S(1)}, u32[]{:S(2)}, u32[]{:S(2)}) collective-permute-start(bf16[3,96,768]{2,1,0:T(8,128)(2,1)S(1)} %add_convert_fusion.1.refs_5_.own_ref), channel_id=1, source_target_pairs={{0,16},{1,9},{2,18},{3,11},{4,20},{5,13},{6,22},{7,15},{8,24},{9,1... | collective-permute-start | bytes 1327112 | tf_op jit(solution)/shard_map/ppermute | solution.py:237
  52.1 9.9 %collective-permute-start.18 = (bf16[3,96,768]{2,1,0:T(8,128)(2,1)S(1)}, bf16[3,96,768]{2,1,0:T(8,128)(2,1)S(1)}, u32[]{:S(2)}, u32[]{:S(2)}) collective-permute-start(bf16[3,96,768]{2,1,0:T(8,128)(2,1)S(1)} %shard_map.120.refs_0_), channel_id=1, source_target_pairs={{0,8},{1,17},{2,10},{3,19},{4,12},{5,21},{6,14},{7,23},{8,0},{9,25... | collective-permute-start | bytes 1327112 | tf_op jit(solution)/shard_map/ppermute | solution.py:237
  52.4 7.5 %collective-permute-start.10 = (bf16[496,128]{1,0:T(8,128)(2,1)S(1)}, bf16[496,128]{1,0:T(8,128)(2,1)S(1)}, u32[]{:S(2)}, u32[]{:S(2)}) collective-permute-start(bf16[496,128]{1,0:T(8,128)(2,1)S(1)} %get-tuple-element.49), channel_id=1, source_target_pairs={{0,2},{1,3},{2,6},{3,7},{4,0},{5,1},{6,4},{7,5},{8,10},{9,11},{10,... | collective-permute-start | bytes 380936 | tf_op jit(solution)/shard_map/ppermute | solution.py:247
  52.4 8.1 %collective-permute-start.11 = (bf16[496,128]{1,0:T(8,128)(2,1)S(1)}, bf16[496,128]{1,0:T(8,128)(2,1)S(1)}, u32[]{:S(2)}, u32[]{:S(2)}) collective-permute-start(bf16[496,128]{1,0:T(8,128)(2,1)S(1)} %get-tuple-element.50), channel_id=1, source_target_pairs={{0,3},{1,2},{2,7},{3,6},{4,1},{5,0},{6,5},{7,4},{8,11},{9,10},{10,... | collective-permute-start | bytes 380936 | tf_op jit(solution)/shard_map/ppermute | solution.py:247
  62.1 7.5 %collective-permute-start.19 = (bf16[3,96,768]{2,1,0:T(8,128)(2,1)S(1)}, bf16[3,96,768]{2,1,0:T(8,128)(2,1)S(1)}, u32[]{:S(2)}, u32[]{:S(2)}) collective-permute-start(bf16[3,96,768]{2,1,0:T(8,128)(2,1)S(1)} %add_convert_fusion.own_ref), channel_id=1, source_target_pairs={{0,16},{1,9},{2,18},{3,11},{4,20},{5,13},{6,22},{7,15},{8,24},{9,1... | collective-permute-start | bytes 1327112 | tf_op jit(solution)/shard_map/ppermute | solution.py:237
  63.4 15.6 %collective-permute-start.5 = (bf16[496,128]{1,0:T(8,128)(2,1)S(1)}, bf16[496,128]{1,0:T(8,128)(2,1)S(1)}, u32[]{:S(2)}, u32[]{:S(2)}) collective-permute-start(bf16[496,128]{1,0:T(8,128)(2,1)S(1)} %get-tuple-element.46), channel_id=1, source_target_pairs={{0,1},{1,0},{2,3},{3,2},{4,5},{5,4},{6,7},{7,6},{8,9},{9,8},{10,11... | collective-permute-start | bytes 380936 | tf_op jit(solution)/shard_map/ppermute | solution.py:247
  63.4 15.6 %collective-permute-start.16 = (bf16[496,128]{1,0:T(8,128)(2,1)S(1)}, bf16[496,128]{1,0:T(8,128)(2,1)S(1)}, u32[]{:S(2)}, u32[]{:S(2)}) collective-permute-start(bf16[496,128]{1,0:T(8,128)(2,1)S(1)} %get-tuple-element.53), channel_id=1, source_target_pairs={{0,4},{1,5},{2,0},{3,1},{4,6},{5,7},{6,2},{7,3},{8,12},{9,13},{10,... | collective-permute-start | bytes 380936 | tf_op jit(solution)/shard_map/ppermute | solution.py:247
  63.4 15.6 %collective-permute-start.17 = (bf16[496,128]{1,0:T(8,128)(2,1)S(1)}, bf16[496,128]{1,0:T(8,128)(2,1)S(1)}, u32[]{:S(2)}, u32[]{:S(2)}) collective-permute-start(bf16[496,128]{1,0:T(8,128)(2,1)S(1)} %get-tuple-element.54), channel_id=1, source_target_pairs={{0,5},{1,4},{2,1},{3,0},{4,7},{5,6},{6,3},{7,2},{8,13},{9,12},{10,... | collective-permute-start | bytes 380936 | tf_op jit(solution)/shard_map/ppermute | solution.py:247
  70.9 10.4 %collective-permute-start.20 = (bf16[496,128]{1,0:T(8,128)(2,1)S(1)}, bf16[496,128]{1,0:T(8,128)(2,1)S(1)}, u32[]{:S(2)}, u32[]{:S(2)}) collective-permute-start(bf16[496,128]{1,0:T(8,128)(2,1)S(1)} %get-tuple-element.57), channel_id=1, source_target_pairs={{0,6},{1,7},{2,4},{3,5},{4,2},{5,3},{6,0},{7,1},{8,14},{9,15},{10,... | collective-permute-start | bytes 380936 | tf_op jit(solution)/shard_map/ppermute | solution.py:247
  72.3 12.0 %collective-permute-start.21 = (bf16[496,128]{1,0:T(8,128)(2,1)S(1)}, bf16[496,128]{1,0:T(8,128)(2,1)S(1)}, u32[]{:S(2)}, u32[]{:S(2)}) collective-permute-start(bf16[496,128]{1,0:T(8,128)(2,1)S(1)} %get-tuple-element.58), channel_id=1, source_target_pairs={{0,7},{1,6},{2,5},{3,4},{4,3},{5,2},{6,1},{7,0},{8,15},{9,14},{10,... | collective-permute-start | bytes 380936 | tf_op jit(solution)/shard_map/ppermute | solution.py:247
  73.7 10.6 %copy-start = (s32[128,2]{0,1:T(2,128)S(1)}, s32[128,2]{0,1:T(2,128)}, u32[]{:S(2)}) copy-start(s32[128,2]{0,1:T(2,128)} %param.8) | copy-start | bytes 3076
  73.7 10.6 %copy-start.1 = (bf16[128,2]{0,1:T(2,128)(2,1)S(1)}, bf16[128,2]{0,1:T(2,128)(2,1)}, u32[]{:S(2)}) copy-start(bf16[128,2]{0,1:T(2,128)(2,1)} %param.9) | copy-start | bytes 1540

commit v6 on v5

--- a/solution.py
+++ b/solution.py
@@ -405,12 +405,12 @@
 
     receive(0)
     receive(1)
-    receive(2)
     forward(0)
     exchange(0)
     forward(1, sums[0][0])
     exchange(1)
     backward(0, parts[1])
+    receive(2, kept[0][0])
     forward(2, sums[1][0], kept[0][0])
     exchange(2)
     backward(1, parts[2])

time: 85.8 us -> 85.8 us (level)
  waiting for transfers between devices: 37.1 us -> 38.2 us
  starting transfers between devices: 25.7 us -> 24.6 us
    ppermute x8, waiting for transfers between devices: 10.4 us -> 18.3 us  [crossed(): return lax.ppermute(value, ('expert', 'dp'), pairs)]
    ppermute x14, waiting for transfers between devices: 26.6 us -> 19.9 us  [moved(): return lax.ppermute(value, 'dp', pairs)]
    ppermute x8, starting transfers between devices: 7.9 us -> 6.1 us  [crossed(): return lax.ppermute(value, ('expert', 'dp'), pairs)]
  transfers between devices with their start and end apart: 22 -> 22, of which waited for: 12 -> 11; matrix products, arithmetic and copies ran while one was open for 0% -> 0% of each run, Pallas kernels for 22% -> 22%
where the time goes in v6:
time: 85.8 us; the launch traced here: 85.6 us
  waiting for transfers between devices  38.2 us (45%)
  starting transfers between devices  24.6 us (29%)
  Pallas kernels  21.6 us (25%)
    ppermute x14, waiting for transfers between devices, moved(): return lax.ppermute(value, 'dp', pairs)  19.9 us
    ppermute x14, starting transfers between devices, moved(): return lax.ppermute(value, 'dp', pairs)  18.5 us
    ppermute x8, waiting for transfers between devices, crossed(): return lax.ppermute(value, ('expert', 'dp'), pairs)  18.3 us
    ppermute x8, starting transfers between devices, crossed(): return lax.ppermute(value, ('expert', 'dp'), pairs)  6.1 us
    pallas_call x4, Pallas kernels, run_backward(): pl.pallas_call(functools.partial(backward_kernel, count, capacity, 256),...  5.28 us
    pallas_call x1, Pallas kernels, run_weights(): pl.pallas_call(functools.partial(weight_kernel, count, capacity, chunks),...  5.24 us
    pallas_call x4, Pallas kernels, run_forward(): pl.pallas_call(functools.partial(forward_kernel, count, capacity, 256), i...  5.18 us
    pallas_call x1, Pallas kernels, run_hold(): pl.pallas_call(hold_kernel, in_specs=in_hbm(len(weights)), out_specs=in_v...  2.76 us
  transfers between devices with their start and end apart: 22, of which 11 were waited for; matrix products, arithmetic and copies ran while one was open for 0% of the time, Pallas kernels for 22%

profile of v6, /device:TPU:13, one launch (start us, length us, event | category | flops | bytes accessed | tf_op | source)
XLA Modules:
  0.0 85.6 jit_solution(2988645335238145928)
XLA Ops:
  0.6 1.8 %shard_map.110 = (bf16[96,1280]{1,0:T(8,128)(2,1)S(1)}, bf16[96,1280]{1,0:T(8,128)(2,1)S(1)}, bf16[192,1280]{1,0:T(8,128)(2,1)S(1)}, bf16[192,1280]{1,0:T(8,128)(2,1)S(1)}, bf16[192,1280]{1,0:T(8,128)(2,1)S(1)}) custom-call(s32[2,128]{1,0:T(2,128)} %bitcast.3, bf16[2,128]{1,0:T(2,128)(2,1)} %bitcast.5, bf16[128,1280]{1,0:T(8,128)(2,1)} %tokens_hbm.1, ...), custom_call_target="tpu_custom_call" | custom-call | flops 1 | bytes 1 | tf_op jit(solution)/shard_map/pallas_call | solution.py:368
  3.4 2.8 %shard_map.111 = (bf16[1,1280,768]{2,1,0:T(8,128)(2,1)S(1)}, bf16[1,1280,768]{2,1,0:T(8,128)(2,1)S(1)}, bf16[1,768,1280]{2,1,0:T(8,128)(2,1)S(1)}) custom-call(bf16[1,1280,768]{2,1,0:T(8,128)(2,1)} %refs_0_.1, bf16[1,1280,768]{2,1,0:T(8,128)(2,1)} %refs_1_.1, bf16[1,768,1280]{2,1,0:T(8,128)(2,1)} %refs_2_.1), custom_call_target="tpu_custom_call" | custom-call | flops 1 | bytes 1 | tf_op jit(solution)/shard_map/pallas_call | solution.py:275
  7.6 2.4 %collective-permute-start.8 = (bf16[192,1280]{1,0:T(8,128)(2,1)S(1)}, bf16[192,1280]{1,0:T(8,128)(2,1)S(1)}, u32[]{:S(2)}, u32[]{:S(2)}) collective-permute-start(bf16[192,1280]{1,0:T(8,128)(2,1)S(1)} %get-tuple-element.47), channel_id=1, source_target_pairs={{0,2},{1,3},{2,6},{3,7},{4,0},{5,1},{6,4},{7,5},{8,10},{9,11},{10,... | collective-permute-start | bytes 1474568 | tf_op jit(solution)/shard_map/ppermute | solution.py:247
  9.9 7.0 %collective-permute-done.3.whole_ref.refs_0_.refs_2_ = bf16[192,1280]{1,0:T(8,128)(2,1)S(1)} collective-permute-done((bf16[192,1280]{1,0:T(8,128)(2,1)S(1)}, bf16[192,1280]{1,0:T(8,128)(2,1)S(1)}, u32[]{:S(2)}, u32[]{:S(2)}) %collective-permute-start.3) | collective-permute-done | bytes 491552 | tf_op jit(solution)/shard_map/ppermute | solution.py:247
  16.9 1.4 %collective-permute-start.4 = (bf16[96,1280]{1,0:T(8,128)(2,1)S(1)}, bf16[96,1280]{1,0:T(8,128)(2,1)S(1)}, u32[]{:S(2)}, u32[]{:S(2)}) collective-permute-start(bf16[96,1280]{1,0:T(8,128)(2,1)S(1)} %shard_map.113), channel_id=1, source_target_pairs={{0,1},{1,0},{2,3},{3,2},{4,5},{5,4},{6,7},{7,6},{8,9},{9,8},{10,11... | collective-permute-start | bytes 737288 | tf_op jit(solution)/shard_map/ppermute | solution.py:247
  21.3 1.3 %collective-permute-start.14 = (bf16[192,1280]{1,0:T(8,128)(2,1)S(1)}, bf16[192,1280]{1,0:T(8,128)(2,1)S(1)}, u32[]{:S(2)}, u32[]{:S(2)}) collective-permute-start(bf16[192,1280]{1,0:T(8,128)(2,1)S(1)} %get-tuple-element.51), channel_id=1, source_target_pairs={{0,6},{1,7},{2,4},{3,5},{4,2},{5,3},{6,0},{7,1},{8,14},{9,15},{10,... | collective-permute-start | bytes 1474568 | tf_op jit(solution)/shard_map/ppermute | solution.py:247
  22.6 4.9 %collective-permute-done.2.got_ref = bf16[3,96,768]{2,1,0:T(8,128)(2,1)S(1)} collective-permute-done((bf16[3,96,768]{2,1,0:T(8,128)(2,1)S(1)}, bf16[3,96,768]{2,1,0:T(8,128)(2,1)S(1)}, u32[]{:S(2)}, u32[]{:S(2)}) %collective-permute-start.2) | collective-permute-done | bytes 442400 | tf_op jit(solution)/shard_map/ppermute | solution.py:237
  27.4 1.3 %shard_map.115 = (bf16[96,768]{1,0:T(8,128)(2,1)S(1)}, bf16[96,768]{1,0:T(8,128)(2,1)S(1)}, bf16[96,768]{1,0:T(8,128)(2,1)S(1)}, bf16[496,128]{1,0:T(8,128)(2,1)S(1)}, bf16[496,128]{1,0:T(8,128)(2,1)S(1)}) custom-call(bf16[3,96,768]{2,1,0:T(8,128)(2,1)S(1)} %add_convert_fusion.3.refs_5_.own_ref, bf16[3,96,768]{2,1,0:T(8,128)(2,1)S(1)} %collective-permute-done.2.got_ref, ...), custom_call_target="tpu_custom_call" | custom-call | flops 1 | bytes 1 | tf_op jit(solution)/shard_map/pallas_call | solution.py:315
  28.8 2.0 %collective-permute-start.9 = (bf16[96,1280]{1,0:T(8,128)(2,1)S(1)}, bf16[96,1280]{1,0:T(8,128)(2,1)S(1)}, u32[]{:S(2)}, u32[]{:S(2)}) collective-permute-start(bf16[96,1280]{1,0:T(8,128)(2,1)S(1)} %shard_map.116), channel_id=1, source_target_pairs={{0,1},{1,0},{2,3},{3,2},{4,5},{5,4},{6,7},{7,6},{8,9},{9,8},{10,11... | collective-permute-start | bytes 737288 | tf_op jit(solution)/shard_map/ppermute | solution.py:247
  34.1 6.5 %collective-permute-done.7.got_ref = bf16[3,96,768]{2,1,0:T(8,128)(2,1)S(1)} collective-permute-done((bf16[3,96,768]{2,1,0:T(8,128)(2,1)S(1)}, bf16[3,96,768]{2,1,0:T(8,128)(2,1)S(1)}, u32[]{:S(2)}, u32[]{:S(2)}) %collective-permute-start.7) | collective-permute-done | bytes 442400 | tf_op jit(solution)/shard_map/ppermute | solution.py:237
  40.6 1.3 %shard_map.118 = (bf16[96,768]{1,0:T(8,128)(2,1)S(1)}, bf16[96,768]{1,0:T(8,128)(2,1)S(1)}, bf16[96,768]{1,0:T(8,128)(2,1)S(1)}, bf16[496,128]{1,0:T(8,128)(2,1)S(1)}, bf16[496,128]{1,0:T(8,128)(2,1)S(1)}) custom-call(bf16[3,96,768]{2,1,0:T(8,128)(2,1)S(1)} %add_convert_fusion.2.refs_5_.own_ref, bf16[3,96,768]{2,1,0:T(8,128)(2,1)S(1)} %collective-permute-done.7.got_ref, ...), custom_call_target="tpu_custom_call" | custom-call | flops 1 | bytes 1 | tf_op jit(solution)/shard_map/pallas_call | solution.py:315
  42.0 6.9 %collective-permute-done.14.whole_ref.refs_0_.refs_6_ = bf16[192,1280]{1,0:T(8,128)(2,1)S(1)} collective-permute-done((bf16[192,1280]{1,0:T(8,128)(2,1)S(1)}, bf16[192,1280]{1,0:T(8,128)(2,1)S(1)}, u32[]{:S(2)}, u32[]{:S(2)}) %collective-permute-start.14) | collective-permute-done | bytes 491552 | tf_op jit(solution)/shard_map/ppermute | solution.py:247
  52.4 4.0 %collective-permute-start.11 = (bf16[496,128]{1,0:T(8,128)(2,1)S(1)}, bf16[496,128]{1,0:T(8,128)(2,1)S(1)}, u32[]{:S(2)}, u32[]{:S(2)}) collective-permute-start(bf16[496,128]{1,0:T(8,128)(2,1)S(1)} %get-tuple-element.50), channel_id=1, source_target_pairs={{0,3},{1,2},{2,7},{3,6},{4,1},{5,0},{6,5},{7,4},{8,11},{9,10},{10,... | collective-permute-start | bytes 380936 | tf_op jit(solution)/shard_map/ppermute | solution.py:247
  56.4 2.1 %collective-permute-done.13.got_ref = bf16[3,96,768]{2,1,0:T(8,128)(2,1)S(1)} collective-permute-done((bf16[3,96,768]{2,1,0:T(8,128)(2,1)S(1)}, bf16[3,96,768]{2,1,0:T(8,128)(2,1)S(1)}, u32[]{:S(2)}, u32[]{:S(2)}) %collective-permute-start.13) | collective-permute-done | bytes 442400 | tf_op jit(solution)/shard_map/ppermute | solution.py:237
  58.6 1.3 %shard_map.121 = (bf16[96,768]{1,0:T(8,128)(2,1)S(1)}, bf16[96,768]{1,0:T(8,128)(2,1)S(1)}, bf16[96,768]{1,0:T(8,128)(2,1)S(1)}, bf16[496,128]{1,0:T(8,128)(2,1)S(1)}, bf16[496,128]{1,0:T(8,128)(2,1)S(1)}) custom-call(bf16[3,96,768]{2,1,0:T(8,128)(2,1)S(1)} %add_convert_fusion.1.refs_5_.own_ref, bf16[3,96,768]{2,1,0:T(8,128)(2,1)S(1)} %collective-permute-done.13.got_ref, ...), custom_call_target="tpu_custom_call" | custom-call | flops 1 | bytes 1 | tf_op jit(solution)/shard_map/pallas_call | solution.py:315
  60.5 1.4 %collective-permute-done.18 = bf16[3,96,768]{2,1,0:T(8,128)(2,1)S(1)} collective-permute-done((bf16[3,96,768]{2,1,0:T(8,128)(2,1)S(1)}, bf16[3,96,768]{2,1,0:T(8,128)(2,1)S(1)}, u32[]{:S(2)}, u32[]{:S(2)}) %collective-permute-start.18) | collective-permute-done | bytes 442400 | tf_op jit(solution)/shard_map/ppermute | solution.py:237
  63.4 3.1 %collective-permute-start.17 = (bf16[496,128]{1,0:T(8,128)(2,1)S(1)}, bf16[496,128]{1,0:T(8,128)(2,1)S(1)}, u32[]{:S(2)}, u32[]{:S(2)}) collective-permute-start(bf16[496,128]{1,0:T(8,128)(2,1)S(1)} %get-tuple-element.54), channel_id=1, source_target_pairs={{0,5},{1,4},{2,1},{3,0},{4,7},{5,6},{6,3},{7,2},{8,13},{9,12},{10,... | collective-permute-start | bytes 380936 | tf_op jit(solution)/shard_map/ppermute | solution.py:247
  66.5 3.1 %collective-permute-done.19.got_ref = bf16[3,96,768]{2,1,0:T(8,128)(2,1)S(1)} collective-permute-done((bf16[3,96,768]{2,1,0:T(8,128)(2,1)S(1)}, bf16[3,96,768]{2,1,0:T(8,128)(2,1)S(1)}, u32[]{:S(2)}, u32[]{:S(2)}) %collective-permute-start.19) | collective-permute-done | bytes 442400 | tf_op jit(solution)/shard_map/ppermute | solution.py:237
  69.6 1.3 %shard_map.122 = (bf16[96,768]{1,0:T(8,128)(2,1)S(1)}, bf16[96,768]{1,0:T(8,128)(2,1)S(1)}, bf16[96,768]{1,0:T(8,128)(2,1)S(1)}, bf16[496,128]{1,0:T(8,128)(2,1)S(1)}, bf16[496,128]{1,0:T(8,128)(2,1)S(1)}) custom-call(bf16[3,96,768]{2,1,0:T(8,128)(2,1)S(1)} %add_convert_fusion.own_ref, bf16[3,96,768]{2,1,0:T(8,128)(2,1)S(1)} %collective-permute-done.19.got_ref, ...), custom_call_target="tpu_custom_call" | custom-call | flops 1 | bytes 1 | tf_op jit(solution)/shard_map/pallas_call | solution.py:315
  70.9 1.4 %collective-permute-start.20 = (bf16[496,128]{1,0:T(8,128)(2,1)S(1)}, bf16[496,128]{1,0:T(8,128)(2,1)S(1)}, u32[]{:S(2)}, u32[]{:S(2)}) collective-permute-start(bf16[496,128]{1,0:T(8,128)(2,1)S(1)} %get-tuple-element.57), channel_id=1, source_target_pairs={{0,6},{1,7},{2,4},{3,5},{4,2},{5,3},{6,0},{7,1},{8,14},{9,15},{10,... | collective-permute-start | bytes 380936 | tf_op jit(solution)/shard_map/ppermute | solution.py:247
  72.3 1.4 %collective-permute-start.21 = (bf16[496,128]{1,0:T(8,128)(2,1)S(1)}, bf16[496,128]{1,0:T(8,128)(2,1)S(1)}, u32[]{:S(2)}, u32[]{:S(2)}) collective-permute-start(bf16[496,128]{1,0:T(8,128)(2,1)S(1)} %get-tuple-element.58), channel_id=1, source_target_pairs={{0,7},{1,6},{2,5},{3,4},{4,3},{5,2},{6,1},{7,0},{8,15},{9,14},{10,... | collective-permute-start | bytes 380936 | tf_op jit(solution)/shard_map/ppermute | solution.py:247
  73.7 5.2 %shard_map.124 = (bf16[1,1280,768]{2,1,0:T(8,128)(2,1)}, bf16[1,1280,768]{2,1,0:T(8,128)(2,1)}, bf16[1,768,1280]{2,1,0:T(8,128)(2,1)}) custom-call(bf16[96,1280]{1,0:T(8,128)(2,1)S(1)} %get-tuple-element.39.refs_0_, bf16[96,1280]{1,0:T(8,128)(2,1)S(1)} %collective-permute-done.refs_1_, ...), custom_call_target="tpu_custom_call" | custom-call | flops 1 | bytes 1 | tf_op jit(solution)/shard_map/pallas_call | solution.py:333
  78.9 2.4 %collective-permute-done.20.refs_8_ = bf16[496,128]{1,0:T(8,128)(2,1)S(1)} collective-permute-done((bf16[496,128]{1,0:T(8,128)(2,1)S(1)}, bf16[496,128]{1,0:T(8,128)(2,1)S(1)}, u32[]{:S(2)}, u32[]{:S(2)}) %collective-permute-start.20) | collective-permute-done | bytes 127008 | tf_op jit(solution)/shard_map/ppermute | solution.py:247
  81.3 3.0 %collective-permute-done.21.refs_9_ = bf16[496,128]{1,0:T(8,128)(2,1)S(1)} collective-permute-done((bf16[496,128]{1,0:T(8,128)(2,1)S(1)}, bf16[496,128]{1,0:T(8,128)(2,1)S(1)}, u32[]{:S(2)}, u32[]{:S(2)}) %collective-permute-start.21) | collective-permute-done | bytes 127008 | tf_op jit(solution)/shard_map/ppermute | solution.py:247
  (43 shorter events, 15.5 us)
Async XLA Ops:
  2.4 3.7 %collective-permute-start = (bf16[96,1280]{1,0:T(8,128)(2,1)S(1)}, bf16[96,1280]{1,0:T(8,128)(2,1)S(1)}, u32[]{:S(2)}, u32[]{:S(2)}) collective-permute-start(bf16[96,1280]{1,0:T(8,128)(2,1)S(1)} %get-tuple-element.40), channel_id=1, source_target_pairs={{0,1},{1,0},{2,3},{3,2},{4,5},{5,4},{6,7},{7,6},{8,9},{9,8},{10,11... | collective-permute-start | bytes 737288 | tf_op jit(solution)/shard_map/ppermute | solution.py:247
  3.2 13.7 %collective-permute-start.3 = (bf16[192,1280]{1,0:T(8,128)(2,1)S(1)}, bf16[192,1280]{1,0:T(8,128)(2,1)S(1)}, u32[]{:S(2)}, u32[]{:S(2)}) collective-permute-start(bf16[192,1280]{1,0:T(8,128)(2,1)S(1)} %get-tuple-element.44), channel_id=1, source_target_pairs={{0,4},{1,5},{2,0},{3,1},{4,6},{5,7},{6,2},{7,3},{8,12},{9,13},{10,... | collective-permute-start | bytes 1474568 | tf_op jit(solution)/shard_map/ppermute | solution.py:247
  7.4 10.9 %collective-permute-start.1 = (bf16[3,96,768]{2,1,0:T(8,128)(2,1)S(1)}, bf16[3,96,768]{2,1,0:T(8,128)(2,1)S(1)}, u32[]{:S(2)}, u32[]{:S(2)}) collective-permute-start(bf16[3,96,768]{2,1,0:T(8,128)(2,1)S(1)} %shard_map.112), channel_id=1, source_target_pairs={{0,8},{1,17},{2,10},{3,19},{4,12},{5,21},{6,14},{7,23},{8,0},{9,25... | collective-permute-start | bytes 1327112 | tf_op jit(solution)/shard_map/ppermute | solution.py:237
  7.6 21.2 %collective-permute-start.8 = (bf16[192,1280]{1,0:T(8,128)(2,1)S(1)}, bf16[192,1280]{1,0:T(8,128)(2,1)S(1)}, u32[]{:S(2)}, u32[]{:S(2)}) collective-permute-start(bf16[192,1280]{1,0:T(8,128)(2,1)S(1)} %get-tuple-element.47), channel_id=1, source_target_pairs={{0,2},{1,3},{2,6},{3,7},{4,0},{5,1},{6,4},{7,5},{8,10},{9,11},{10,... | collective-permute-start | bytes 1474568 | tf_op jit(solution)/shard_map/ppermute | solution.py:247
  16.9 2.8 %collective-permute-start.4 = (bf16[96,1280]{1,0:T(8,128)(2,1)S(1)}, bf16[96,1280]{1,0:T(8,128)(2,1)S(1)}, u32[]{:S(2)}, u32[]{:S(2)}) collective-permute-start(bf16[96,1280]{1,0:T(8,128)(2,1)S(1)} %shard_map.113), channel_id=1, source_target_pairs={{0,1},{1,0},{2,3},{3,2},{4,5},{5,4},{6,7},{7,6},{8,9},{9,8},{10,11... | collective-permute-start | bytes 737288 | tf_op jit(solution)/shard_map/ppermute | solution.py:247
  18.4 9.0 %collective-permute-start.2 = (bf16[3,96,768]{2,1,0:T(8,128)(2,1)S(1)}, bf16[3,96,768]{2,1,0:T(8,128)(2,1)S(1)}, u32[]{:S(2)}, u32[]{:S(2)}) collective-permute-start(bf16[3,96,768]{2,1,0:T(8,128)(2,1)S(1)} %add_convert_fusion.3.refs_5_.own_ref), channel_id=1, source_target_pairs={{0,16},{1,9},{2,18},{3,11},{4,20},{5,13},{6,22},{7,15},{8,24},{9,1... | collective-permute-start | bytes 1327112 | tf_op jit(solution)/shard_map/ppermute | solution.py:237
  21.0 10.2 %collective-permute-start.6 = (bf16[3,96,768]{2,1,0:T(8,128)(2,1)S(1)}, bf16[3,96,768]{2,1,0:T(8,128)(2,1)S(1)}, u32[]{:S(2)}, u32[]{:S(2)}) collective-permute-start(bf16[3,96,768]{2,1,0:T(8,128)(2,1)S(1)} %shard_map.114.refs_0_), channel_id=1, source_target_pairs={{0,8},{1,17},{2,10},{3,19},{4,12},{5,21},{6,14},{7,23},{8,0},{9,25... | collective-permute-start | bytes 1327112 | tf_op jit(solution)/shard_map/ppermute | solution.py:237
  21.3 27.5 %collective-permute-start.14 = (bf16[192,1280]{1,0:T(8,128)(2,1)S(1)}, bf16[192,1280]{1,0:T(8,128)(2,1)S(1)}, u32[]{:S(2)}, u32[]{:S(2)}) collective-permute-start(bf16[192,1280]{1,0:T(8,128)(2,1)S(1)} %get-tuple-element.51), channel_id=1, source_target_pairs={{0,6},{1,7},{2,4},{3,5},{4,2},{5,3},{6,0},{7,1},{8,14},{9,15},{10,... | collective-permute-start | bytes 1474568 | tf_op jit(solution)/shard_map/ppermute | solution.py:247
  28.8 3.7 %collective-permute-start.9 = (bf16[96,1280]{1,0:T(8,128)(2,1)S(1)}, bf16[96,1280]{1,0:T(8,128)(2,1)S(1)}, u32[]{:S(2)}, u32[]{:S(2)}) collective-permute-start(bf16[96,1280]{1,0:T(8,128)(2,1)S(1)} %shard_map.116), channel_id=1, source_target_pairs={{0,1},{1,0},{2,3},{3,2},{4,5},{5,4},{6,7},{7,6},{8,9},{9,8},{10,11... | collective-permute-start | bytes 737288 | tf_op jit(solution)/shard_map/ppermute | solution.py:247
  31.3 9.4 %collective-permute-start.7 = (bf16[3,96,768]{2,1,0:T(8,128)(2,1)S(1)}, bf16[3,96,768]{2,1,0:T(8,128)(2,1)S(1)}, u32[]{:S(2)}, u32[]{:S(2)}) collective-permute-start(bf16[3,96,768]{2,1,0:T(8,128)(2,1)S(1)} %add_convert_fusion.2.refs_5_.own_ref), channel_id=1, source_target_pairs={{0,16},{1,9},{2,18},{3,11},{4,20},{5,13},{6,22},{7,15},{8,24},{9,1... | collective-permute-start | bytes 1327112 | tf_op jit(solution)/shard_map/ppermute | solution.py:237
  33.9 15.6 %collective-permute-start.12 = (bf16[3,96,768]{2,1,0:T(8,128)(2,1)S(1)}, bf16[3,96,768]{2,1,0:T(8,128)(2,1)S(1)}, u32[]{:S(2)}, u32[]{:S(2)}) collective-permute-start(bf16[3,96,768]{2,1,0:T(8,128)(2,1)S(1)} %shard_map.117.refs_0_), channel_id=1, source_target_pairs={{0,8},{1,17},{2,10},{3,19},{4,12},{5,21},{6,14},{7,23},{8,0},{9,25... | collective-permute-start | bytes 1327112 | tf_op jit(solution)/shard_map/ppermute | solution.py:237
  48.9 1.9 %collective-permute-start.15 = (bf16[96,1280]{1,0:T(8,128)(2,1)S(1)}, bf16[96,1280]{1,0:T(8,128)(2,1)S(1)}, u32[]{:S(2)}, u32[]{:S(2)}) collective-permute-start(bf16[96,1280]{1,0:T(8,128)(2,1)S(1)} %shard_map.119), channel_id=1, source_target_pairs={{0,1},{1,0},{2,3},{3,2},{4,5},{5,4},{6,7},{7,6},{8,9},{9,8},{10,11... | collective-permute-start | bytes 737288 | tf_op jit(solution)/shard_map/ppermute | solution.py:247
  49.5 9.0 %collective-permute-start.13 = (bf16[3,96,768]{2,1,0:T(8,128)(2,1)S(1)}, bf16[3,96,768]{2,1,0:T(8,128)(2,1)S(1)}, u32[]{:S(2)}, u32[]{:S(2)}) collective-permute-start(bf16[3,96,768]{2,1,0:T(8,128)(2,1)S(1)} %add_convert_fusion.1.refs_5_.own_ref), channel_id=1, source_target_pairs={{0,16},{1,9},{2,18},{3,11},{4,20},{5,13},{6,22},{7,15},{8,24},{9,1... | collective-permute-start | bytes 1327112 | tf_op jit(solution)/shard_map/ppermute | solution.py:237
  52.1 9.9 %collective-permute-start.18 = (bf16[3,96,768]{2,1,0:T(8,128)(2,1)S(1)}, bf16[3,96,768]{2,1,0:T(8,128)(2,1)S(1)}, u32[]{:S(2)}, u32[]{:S(2)}) collective-permute-start(bf16[3,96,768]{2,1,0:T(8,128)(2,1)S(1)} %shard_map.120.refs_0_), channel_id=1, source_target_pairs={{0,8},{1,17},{2,10},{3,19},{4,12},{5,21},{6,14},{7,23},{8,0},{9,25... | collective-permute-start | bytes 1327112 | tf_op jit(solution)/shard_map/ppermute | solution.py:237
  52.4 7.5 %collective-permute-start.10 = (bf16[496,128]{1,0:T(8,128)(2,1)S(1)}, bf16[496,128]{1,0:T(8,128)(2,1)S(1)}, u32[]{:S(2)}, u32[]{:S(2)}) collective-permute-start(bf16[496,128]{1,0:T(8,128)(2,1)S(1)} %get-tuple-element.49), channel_id=1, source_target_pairs={{0,2},{1,3},{2,6},{3,7},{4,0},{5,1},{6,4},{7,5},{8,10},{9,11},{10,... | collective-permute-start | bytes 380936 | tf_op jit(solution)/shard_map/ppermute | solution.py:247
  52.4 8.1 %collective-permute-start.11 = (bf16[496,128]{1,0:T(8,128)(2,1)S(1)}, bf16[496,128]{1,0:T(8,128)(2,1)S(1)}, u32[]{:S(2)}, u32[]{:S(2)}) collective-permute-start(bf16[496,128]{1,0:T(8,128)(2,1)S(1)} %get-tuple-element.50), channel_id=1, source_target_pairs={{0,3},{1,2},{2,7},{3,6},{4,1},{5,0},{6,5},{7,4},{8,11},{9,10},{10,... | collective-permute-start | bytes 380936 | tf_op jit(solution)/shard_map/ppermute | solution.py:247
  62.1 7.5 %collective-permute-start.19 = (bf16[3,96,768]{2,1,0:T(8,128)(2,1)S(1)}, bf16[3,96,768]{2,1,0:T(8,128)(2,1)S(1)}, u32[]{:S(2)}, u32[]{:S(2)}) collective-permute-start(bf16[3,96,768]{2,1,0:T(8,128)(2,1)S(1)} %add_convert_fusion.own_ref), channel_id=1, source_target_pairs={{0,16},{1,9},{2,18},{3,11},{4,20},{5,13},{6,22},{7,15},{8,24},{9,1... | collective-permute-start | bytes 1327112 | tf_op jit(solution)/shard_map/ppermute | solution.py:237
  63.4 15.6 %collective-permute-start.5 = (bf16[496,128]{1,0:T(8,128)(2,1)S(1)}, bf16[496,128]{1,0:T(8,128)(2,1)S(1)}, u32[]{:S(2)}, u32[]{:S(2)}) collective-permute-start(bf16[496,128]{1,0:T(8,128)(2,1)S(1)} %get-tuple-element.46), channel_id=1, source_target_pairs={{0,1},{1,0},{2,3},{3,2},{4,5},{5,4},{6,7},{7,6},{8,9},{9,8},{10,11... | collective-permute-start | bytes 380936 | tf_op jit(solution)/shard_map/ppermute | solution.py:247
  63.4 15.6 %collective-permute-start.16 = (bf16[496,128]{1,0:T(8,128)(2,1)S(1)}, bf16[496,128]{1,0:T(8,128)(2,1)S(1)}, u32[]{:S(2)}, u32[]{:S(2)}) collective-permute-start(bf16[496,128]{1,0:T(8,128)(2,1)S(1)} %get-tuple-element.53), channel_id=1, source_target_pairs={{0,4},{1,5},{2,0},{3,1},{4,6},{5,7},{6,2},{7,3},{8,12},{9,13},{10,... | collective-permute-start | bytes 380936 | tf_op jit(solution)/shard_map/ppermute | solution.py:247
  63.4 15.6 %collective-permute-start.17 = (bf16[496,128]{1,0:T(8,128)(2,1)S(1)}, bf16[496,128]{1,0:T(8,128)(2,1)S(1)}, u32[]{:S(2)}, u32[]{:S(2)}) collective-permute-start(bf16[496,128]{1,0:T(8,128)(2,1)S(1)} %get-tuple-element.54), channel_id=1, source_target_pairs={{0,5},{1,4},{2,1},{3,0},{4,7},{5,6},{6,3},{7,2},{8,13},{9,12},{10,... | collective-permute-start | bytes 380936 | tf_op jit(solution)/shard_map/ppermute | solution.py:247
  70.9 10.4 %collective-permute-start.20 = (bf16[496,128]{1,0:T(8,128)(2,1)S(1)}, bf16[496,128]{1,0:T(8,128)(2,1)S(1)}, u32[]{:S(2)}, u32[]{:S(2)}) collective-permute-start(bf16[496,128]{1,0:T(8,128)(2,1)S(1)} %get-tuple-element.57), channel_id=1, source_target_pairs={{0,6},{1,7},{2,4},{3,5},{4,2},{5,3},{6,0},{7,1},{8,14},{9,15},{10,... | collective-permute-start | bytes 380936 | tf_op jit(solution)/shard_map/ppermute | solution.py:247
  72.3 12.0 %collective-permute-start.21 = (bf16[496,128]{1,0:T(8,128)(2,1)S(1)}, bf16[496,128]{1,0:T(8,128)(2,1)S(1)}, u32[]{:S(2)}, u32[]{:S(2)}) collective-permute-start(bf16[496,128]{1,0:T(8,128)(2,1)S(1)} %get-tuple-element.58), channel_id=1, source_target_pairs={{0,7},{1,6},{2,5},{3,4},{4,3},{5,2},{6,1},{7,0},{8,15},{9,14},{10,... | collective-permute-start | bytes 380936 | tf_op jit(solution)/shard_map/ppermute | solution.py:247
  73.7 10.6 %copy-start = (s32[128,2]{0,1:T(2,128)S(1)}, s32[128,2]{0,1:T(2,128)}, u32[]{:S(2)}) copy-start(s32[128,2]{0,1:T(2,128)} %param.8) | copy-start | bytes 3076
  73.7 10.6 %copy-start.1 = (bf16[128,2]{0,1:T(2,128)(2,1)S(1)}, bf16[128,2]{0,1:T(2,128)(2,1)}, u32[]{:S(2)}) copy-start(bf16[128,2]{0,1:T(2,128)(2,1)} %param.9) | copy-start | bytes 1540
